TPU v7x, 256 devices: a whole 4x4x8 slice. The times are simulated.
256 devices in a mesh: tile: 64 (over x, z, core), mode: 4 (over y).
Axes of the slice: x: 4, y: 4, z: 8, core: 2. Of those that a mesh axis runs over, the one named last changes fastest.
Arguments:
- object_tiles: bfloat16 [64, 2, 2, 256, 256], P('tile'), may hold values from -4 to 4
- probes: float32 [4, 2, 256, 256], P('mode'), may hold values from -4 to 4
- measured: bfloat16 [64, 8, 256, 256], P('tile'), may hold values from 0.25 to 4
- offsets: int32 [64, 8, 2], P('tile'), may hold values from 0 to 255, as said below
- counts: int32 [64], P('tile'), may hold values from 1 to 8, 320 in all
Outputs:
- object_grad: float32 [64, 2, 2, 256, 256], P('tile', None, None, 'mode')
- probe_grad: float32 [4, 2, 256, 256], P('mode')
Inputs may be any that keep to these rules, and one draw needn't show every extreme that they name: Slots 0 .. counts[t] - 1 of tile t hold scan positions; the others are empty. Some tile has 8 live slots. Row offsets lie in 0 .. 255 and column offsets in 128 .. 255.
All inputs are finite; a program needn't handle non-finite values. No bound on the sum of `counts` on one device may be relied on, other than what follows from the above.
Results may differ from a plain program's by a relative error of at most 0.019.
Values may be sent and summed in bfloat16 or wider, within the bound.
No kernel may reach another device: no remote copies, remote signals or barrier semaphores. Data moves between devices by JAX's collectives and lax.ppermute only.
A program may use at most 128 MiB of HBM per device.

v0:
```python
import math

import jax
import jax.numpy as jnp
import numpy as np
from jax import lax
from jax.experimental import pallas as pl
from jax.experimental.pallas import tpu as pltpu
from jax.sharding import PartitionSpec as P


PW = 256
HALF = 128
SLOTS = 8
MODES = 4
TGX = 8
TILES = 64
SHARE = PW // MODES
UNROLL = 4
f32 = jnp.float32
bf16 = jnp.bfloat16


def constants():
    indices = np.arange(PW)
    angles = ((indices[:, None] * indices[None, :]) % PW) * (2.0 * math.pi / PW)
    cosine = (np.cos(angles) / math.sqrt(PW)).astype(bf16)
    sine = (np.sin(angles) / math.sqrt(PW)).astype(bf16)
    frequency = (((indices + PW // 2) % PW) - PW // 2) / PW
    phase = np.exp(-1j * math.pi * (PW / 8.0) * frequency * frequency)
    table = cosine.astype(np.float64) - 1j * sine.astype(np.float64)
    hop = np.conj(table) @ (phase[:, None] * table)
    hop_real = hop.real.astype(bf16)
    hop_imag = hop.imag.astype(bf16)
    return cosine, sine, hop_real, hop_imag


def block_forms(cosine, sine, hop_real, hop_imag):
    return (
        jnp.block([[cosine, sine], [-sine, cosine]]),
        jnp.block([[cosine, -sine], [sine, cosine]]),
        jnp.block([[hop_real, -hop_imag], [hop_imag, hop_real]]),
        jnp.block([[hop_real, hop_imag], [-hop_imag, hop_real]]),
    )


def dot(left, right):
    return jnp.dot(left, right, preferred_element_type=f32)


def build_window(window, depth, meta, own, east, lower):
    for part in range(2):
        window[part, 0, 0:PW] = own[depth, part, :, HALF:].astype(f32)
        for lane_tile in range(2):
            lanes = slice(HALF * lane_tile, HALF * lane_tile + HALF)
            window[part, 1 + lane_tile, 0:PW] = east[depth, part, :, lanes].astype(f32)
        for step in range(MODES):
            owner = lax.rem(meta[2 * SLOTS + 1] + step, MODES)
            rows = pl.ds(pl.multiple_of(PW + SHARE * owner, SHARE), SHARE)
            for t in range(3):
                window[part, t, rows] = lower[step][depth, part, :, HALF * t : HALF * t + HALF].astype(f32)


def load_probes(probes, meta, own, near, far):
    core = meta[2 * SLOTS + 2]
    probes[0] = own[...]
    for step in range(1, MODES):
        probes[step, core] = near[step - 1]
        probes[step, 1 - core] = far[step - 1]


def corner_of(meta, turn):
    slot = meta[2 * SLOTS + 1] + MODES * turn
    return meta[2 * slot], meta[2 * slot + 1] - HALF, slot < meta[2 * SLOTS]


def cut(window, patch, row, col):
    keep = lax.broadcasted_iota(jnp.int32, (64, HALF), 1) < HALF - col
    turn = jnp.where(col == 0, 0, HALF - col)
    for part in range(2):
        for block in range(4):
            rows = pl.ds(row + 64 * block, 64)
            rolled = [pltpu.roll(window[part, t, rows], turn, 1) for t in range(3)]
            at = slice(64 * block, 64 * block + 64)
            patch[part, at, 0:HALF] = jnp.where(keep, rolled[0], rolled[1])
            patch[part, at, HALF:PW] = jnp.where(keep, rolled[1], rolled[2])


def place(total, patch, row, col):
    low = lax.broadcasted_iota(jnp.int32, (64, HALF), 1) < col
    zero = jnp.zeros((64, HALF), f32)
    for part in range(2):
        for block in range(4):
            rows = pl.ds(row + 64 * block, 64)
            at = slice(64 * block, 64 * block + 64)
            left = pltpu.roll(patch[part, at, 0:HALF], col, 1)
            right = pltpu.roll(patch[part, at, HALF:PW], col, 1)
            total[part, 0, rows] = total[part, 0, rows] + jnp.where(low, zero, left)
            total[part, 1, rows] = total[part, 1, rows] + jnp.where(low, left, right)
            total[part, 2, rows] = total[part, 2, rows] + jnp.where(low, right, zero)


def share_rows(total, shares, mode):
    for step in range(MODES):
        owner = lax.rem(mode + step, MODES)
        for half in range(2):
            rows = pl.ds(pl.multiple_of(PW * half + SHARE * owner, SHARE), SHARE)
            for part in range(2):
                for t in range(3):
                    shares[step][part, half, t] = total[part, t, rows].astype(bf16)


def set_rows(both, top, bottom):
    both[0:PW] = top.astype(bf16)
    both[PW:] = bottom.astype(bf16)


def set_lanes(both, stacked):
    both[:, 0:PW] = stacked[0:PW].astype(bf16)
    both[:, PW:] = stacked[PW:].astype(bf16)


def each_mode(step):
    def trip(index, _):
        for lane_set in range(UNROLL):
            step(index * UNROLL + lane_set, lane_set)
        return 0

    return lax.fori_loop(0, MODES // UNROLL, trip, 0)


def propagate_kernel(meta, own, east, l0, l1, l2, l3, probe, near, far, left, right, arrived, window, patch, probes, rows, lanes):
    load_probes(probes, meta, probe, near, far)
    build_window(window, 0, meta, own, east, (l0, l1, l2, l3))

    def one_slot(turn, _):
        row, col, _ = corner_of(meta, turn)
        cut(window, patch, row, col)

        def one_mode(mode, lane_set):
            probe_real, probe_imag = probes[mode, 0].astype(f32), probes[mode, 1].astype(f32)
            real, imag = patch[0], patch[1]
            set_rows(rows.at[lane_set], probe_real * real - probe_imag * imag, probe_real * imag + probe_imag * real)
            set_lanes(lanes.at[lane_set], dot(left[...], rows[lane_set]))
            arrived[turn, mode] = dot(lanes[lane_set], right[...])

        return each_mode(one_mode)

    lax.fori_loop(0, 2, one_slot, 0)


def detector_kernel(meta, own, east, l0, l1, l2, l3, arrived, measured, plus, minus, arrived_grad, g0, g1, g2, g3, window, patch, rows, lanes, far, weight, second, total):
    build_window(window, 1, meta, own, east, (l0, l1, l2, l3))
    total[...] = jnp.zeros_like(total)

    def one_slot(turn, _):
        row, col, live = corner_of(meta, turn)
        cut(window, patch, row, col)

        def forth(mode, lane_set):
            wave_real, wave_imag = arrived[turn, mode, :, 0:PW], arrived[turn, mode, :, PW:]
            real, imag = patch[0], patch[1]
            set_rows(rows.at[lane_set], wave_real * real - wave_imag * imag, wave_real * imag + wave_imag * real)
            set_lanes(lanes.at[lane_set], dot(plus[...], rows[lane_set]))
            field = dot(lanes[lane_set], minus[...])
            far[mode] = field
            power = field[:, 0:PW] * field[:, 0:PW] + field[:, PW:] * field[:, PW:]

            @pl.when(mode == 0)
            def _():
                weight[...] = power - measured[turn].astype(f32)

            @pl.when(mode > 0)
            def _():
                weight[...] = weight[...] + power

        each_mode(forth)
        weight[...] = jnp.where(live, weight[...], 0.0)
        second[...] = jnp.zeros_like(second)

        def back(mode, lane_set):
            scale = weight[...]
            set_rows(rows.at[lane_set], scale * far[mode, :, 0:PW], scale * far[mode, :, PW:])
            set_lanes(lanes.at[lane_set], dot(minus[...], rows[lane_set]))
            leaving = dot(lanes[lane_set], plus[...])
            grad_real, grad_imag = leaving[:, 0:PW], leaving[:, PW:]
            wave_real, wave_imag = arrived[turn, mode, :, 0:PW], arrived[turn, mode, :, PW:]
            second[0] = second[0] + (wave_real * grad_real + wave_imag * grad_imag)
            second[1] = second[1] + (wave_real * grad_imag - wave_imag * grad_real)
            real, imag = patch[0], patch[1]
            arrived_grad[turn, mode, 0:PW] = (real * grad_real + imag * grad_imag).astype(bf16)
            arrived_grad[turn, mode, PW:] = (real * grad_imag - imag * grad_real).astype(bf16)

        each_mode(back)
        place(total, second, row, col)
        return 0

    lax.fori_loop(0, 2, one_slot, 0)
    share_rows(total, (g0, g1, g2, g3), meta[2 * SLOTS + 1])


def return_kernel(meta, own, east, l0, l1, l2, l3, arrived_grad, probe, near, far, left, right, g0, g1, g2, g3, kept, sent, window, patch, probes, lanes, first, total, probe_total):
    load_probes(probes, meta, probe, near, far)
    build_window(window, 0, meta, own, east, (l0, l1, l2, l3))
    total[...] = jnp.zeros_like(total)
    probe_total[...] = jnp.zeros_like(probe_total)

    def one_slot(turn, _):
        row, col, _ = corner_of(meta, turn)
        cut(window, patch, row, col)
        first[...] = jnp.zeros_like(first)

        def one_mode(mode, lane_set):
            set_lanes(lanes.at[lane_set], dot(left[...], arrived_grad[turn, mode]))
            grad = dot(lanes[lane_set], right[...])
            grad_real, grad_imag = grad[:, 0:PW], grad[:, PW:]
            probe_real, probe_imag = probes[mode, 0].astype(f32), probes[mode, 1].astype(f32)
            real, imag = patch[0], patch[1]
            first[0] = first[0] + (probe_real * grad_real + probe_imag * grad_imag)
            first[1] = first[1] + (probe_real * grad_imag - probe_imag * grad_real)
            probe_total[0, mode] = probe_total[0, mode] + (real * grad_real + imag * grad_imag)
            probe_total[1, mode] = probe_total[1, mode] + (real * grad_imag - imag * grad_real)

        each_mode(one_mode)
        place(total, first, row, col)
        return 0

    lax.fori_loop(0, 2, one_slot, 0)
    share_rows(total, (g0, g1, g2, g3), meta[2 * SLOTS + 1])
    core = meta[2 * SLOTS + 2]
    kept[...] = probe_total[core]
    sent[...] = probe_total[1 - core].astype(bf16)


def kernel_call(body, out_shape, scratch, operands, flops, limit):
    vmem = pl.BlockSpec(memory_space=pltpu.VMEM)
    smem = pl.BlockSpec(memory_space=pltpu.SMEM)
    return pl.pallas_call(
        body,
        out_shape=tuple(jax.ShapeDtypeStruct(*shape) for shape in out_shape),
        in_specs=[smem] + [vmem] * (len(operands) - 1),
        out_specs=tuple(vmem for _ in out_shape),
        scratch_shapes=[pltpu.VMEM(*shape) for shape in scratch],
        compiler_params=pltpu.CompilerParams(vmem_limit_bytes=limit << 20),
        cost_estimate=pl.CostEstimate(flops=flops, bytes_accessed=12 << 20, transcendentals=0),
    )(*operands)


WINDOW = ((2, 3, 2 * PW, HALF), f32)
PATCH = ((2, PW, PW), f32)
ROWS = ((UNROLL, 2 * PW, PW), bf16)
LANES = ((UNROLL, PW, 2 * PW), bf16)
PROBES = ((MODES, 2, PW, PW), bf16)
SHARES = [((2, 2, 3, SHARE, HALF), bf16)] * MODES
TRANSFORM = 8 * 16 * PW * PW * PW


def kernels(meta, pieces, all_probes, turns, matrices):
    plus, minus, left, right = matrices
    (arrived,) = kernel_call(
        propagate_kernel,
        [((2, MODES, PW, 2 * PW), f32)],
        [WINDOW, PATCH, PROBES, ROWS, LANES],
        (meta, *pieces, *all_probes, left, right),
        TRANSFORM,
        16,
    )
    arrived_grad, *second_shares = kernel_call(
        detector_kernel,
        [((2, MODES, 2 * PW, PW), bf16)] + SHARES,
        [WINDOW, PATCH, ROWS, LANES, ((MODES, PW, 2 * PW), f32), ((PW, PW), f32), PATCH, WINDOW],
        (meta, *pieces, arrived, turns, plus, minus),
        2 * TRANSFORM,
        26,
    )
    *first_shares, kept, sent = kernel_call(
        return_kernel,
        SHARES + [((MODES, PW, PW), f32), ((MODES, PW, PW), bf16)],
        [WINDOW, PATCH, PROBES, LANES, PATCH, WINDOW, ((2, MODES, PW, PW), f32)],
        (meta, *pieces, arrived_grad, *all_probes, right, left),
        TRANSFORM,
        20,
    )
    return second_shares, first_shares, kept, sent


def toward(value, steps):
    pairs = [(t, t + steps) for t in range(TILES) if 0 <= t + steps < TILES]
    return lax.ppermute(value, "tile", pairs)


def to_mode(value, steps):
    return lax.ppermute(value, "mode", [(m, (m + steps) % MODES) for m in range(MODES)])


def tile_of(x, z, core):
    return (x * 8 + z) * 2 + core


def to_core(value):
    return lax.ppermute(value, "tile", [(t, t ^ 1) for t in range(TILES)])


def send_rows(shares):
    received = [shares[0]]
    for step in range(1, MODES):
        received.append(to_mode(shares[step], step))
    return received


def fetch(value):
    received = []
    for step in range(1, MODES):
        received.append(to_mode(value, MODES - step))
    return received


def add_up(values):
    total = values[0].astype(f32)
    for value in values[1:]:
        total = total + value.astype(f32)
    return total


def exchange(value):
    groups = [[tile_of(x, z, c) for x in range(4) for z in range(8)] for c in range(2)]
    return lax.all_to_all(value, "tile", 0, 0, axis_index_groups=groups)


def one_step(object_tiles, probes, measured, offsets, counts):
    tile = lax.axis_index("tile")
    mode = lax.axis_index("mode")
    core = lax.rem(tile, 2)
    own = object_tiles[0]
    quarter = lax.dynamic_slice_in_dim(own, SHARE * mode, SHARE, 2)
    corner = toward(quarter, -TGX - 1)
    south = toward(quarter[..., HALF:], -TGX)
    probe = probes[0].astype(bf16)
    near = jnp.stack(fetch(lax.dynamic_index_in_dim(probe, core, 0, keepdims=False)))
    far = to_core(near)
    east = toward(own, -1)
    lower = jnp.concatenate([south, corner], axis=-1)
    quarters = [lower] + fetch(lower)
    pieces = (own, east, *quarters)
    all_probes = (probe, near, far)
    matrices = block_forms(*lax.optimization_barrier(tuple(jnp.asarray(table) for table in constants())))
    meta = jnp.concatenate([offsets.reshape(-1), counts, jnp.stack([mode, core])]).astype(jnp.int32)
    turns = lax.dynamic_index_in_dim(measured[0].reshape(2, MODES, PW, PW), mode, 1, keepdims=False)
    second_shares, first_shares, kept, sent = kernels(meta, pieces, all_probes, turns, matrices)
    second = add_up(send_rows(second_shares))
    halves = kept + to_core(sent).astype(f32)
    mine = add_up(send_rows([halves[0]] + [halves[step].astype(bf16) for step in range(1, MODES)]))
    parts = exchange(mine.astype(bf16).reshape(32, 8, PW))
    part = jnp.sum(parts.astype(f32), axis=0).astype(bf16)
    first = add_up(send_rows(first_shares))
    rows = jnp.stack([first, second])
    eastward = toward(rows[:, :, :, 1:].astype(bf16), 1).astype(f32)
    joined = jnp.concatenate([eastward[:, :, :, 0], eastward[:, :, :, 1] + rows[:, :, :, 0]], axis=-1)
    object_grad = joined[:, :, 0] + toward(joined[:, :, 1].astype(bf16), TGX).astype(f32)
    plane = exchange(jnp.broadcast_to(part[None], (32, 8, PW))).reshape(PW, PW)
    other = to_core(plane)
    real = jnp.where(core == 0, plane, other)
    imag = jnp.where(core == 0, other, plane)
    return (object_grad[None], jnp.stack([real, imag]).astype(f32)[None])


def solution(mesh):
    placed = (
        P("tile", None, None, None, None),
        P("mode", None, None, None),
        P("tile", None, None, None),
        P("tile", None, None),
        P("tile"),
    )
    return jax.shard_map(
        one_step,
        mesh=mesh,
        in_specs=placed,
        out_specs=(P("tile", None, None, "mode", None), P("mode", None, None, None)),
        check_vma=False,
    )
```

profile of v0, /device:TPU:1, one launch (start us, length us, event | category | flops | bytes accessed | tf_op | source)
XLA Modules:
  0.0 130.1 jit_solution(4876944274244917806)
XLA Ops:
  2.0 2.2 %collective-permute-start.8 = (bf16[256,256]{1,0:T(8,128)(2,1)S(1)}, bf16[256,256]{1,0:T(8,128)(2,1)S(1)}, u32[]{:S(2)}, u32[]{:S(2)}) collective-permute-start(bf16[256,256]{1,0:T(8,128)(2,1)S(1)} %dynamic-slice_bitcast_fusion.1), channel_id=1, source_target_pairs={{0,1},{1,2},{2,3},{3,0},{4,5},{5,6},{6,7},{7,4},{8,9},{9,10},{10,1... | collective-permute-start | bytes 393224 | tf_op jit(solution)/shard_map/ppermute | solution.py:293
  4.1 2.6 %collective-permute-start.7 = (bf16[256,256]{1,0:T(8,128)(2,1)S(1)}, bf16[256,256]{1,0:T(8,128)(2,1)S(1)}, u32[]{:S(2)}, u32[]{:S(2)}) collective-permute-start(bf16[256,256]{1,0:T(8,128)(2,1)S(1)} %dynamic-slice_bitcast_fusion.1), channel_id=1, source_target_pairs={{0,2},{1,3},{2,0},{3,1},{4,6},{5,7},{6,4},{7,5},{8,10},{9,11},{10,... | collective-permute-start | bytes 393224 | tf_op jit(solution)/shard_map/ppermute | solution.py:293
  14.0 7.5 %collective-permute-done.1 = bf16[2,2,64,128]{3,2,1,0:T(8,128)(2,1)S(1)} collective-permute-done((bf16[2,2,64,128]{3,2,1,0:T(8,128)(2,1)S(1)}, bf16[2,2,64,128]{3,2,1,0:T(8,128)(2,1)S(1)}, u32[]{:S(2)}, u32[]{:S(2)}) %collective-permute-start.1) | collective-permute-done | bytes 65568 | tf_op jit(solution)/shard_map/ppermute | solution.py:289
  21.5 3.5 %collective-permute-start = (bf16[2,2,256,256]{3,2,1,0:T(8,128)(2,1)}, bf16[2,2,256,256]{3,2,1,0:T(8,128)(2,1)S(1)}, u32[]{:S(2)}, u32[]{:S(2)}) collective-permute-start(bf16[2,2,256,256]{3,2,1,0:T(8,128)(2,1)} %bitcast.69), channel_id=1, source_target_pairs={{4,0},{8,4},{12,8},{16,12},{20,16},{24,20},{28,24},{32,28},{36,32}... | collective-permute-start | bytes 1572872 | tf_op jit(solution)/shard_map/ppermute | solution.py:289
  26.5 2.0 %collective-permute-start.3 = (bf16[2,2,64,384]{3,2,1,0:T(8,128)(2,1)S(1)}, bf16[2,2,64,384]{3,2,1,0:T(8,128)(2,1)S(1)}, u32[]{:S(2)}, u32[]{:S(2)}) collective-permute-start(bf16[2,2,64,384]{3,2,1,0:T(8,128)(2,1)S(1)} %constant_dynamic-update-slice_fusion.l0), channel_id=1, source_target_pairs={{0,3},{1,0},{2,1},{3,2},{4,7},{5,4},{6,5},{7,6},{8,11},{9,8},{10,9... | collective-permute-start | bytes 589832 | tf_op jit(solution)/shard_map/ppermute | solution.py:293
  29.7 6.9 %collective-permute-done.5.l3 = bf16[2,2,64,384]{3,2,1,0:T(8,128)(2,1)S(1)} collective-permute-done((bf16[2,2,64,384]{3,2,1,0:T(8,128)(2,1)S(1)}, bf16[2,2,64,384]{3,2,1,0:T(8,128)(2,1)S(1)}, u32[]{:S(2)}, u32[]{:S(2)}) %collective-permute-start.5) | collective-permute-done | bytes 196640 | tf_op jit(solution)/shard_map/ppermute | solution.py:293
  37.1 4.4 %shard_map.104.arrived = f32[2,4,256,512]{3,2,1,0:T(8,128)S(1)} custom-call(s32[19]{0:T(128)S(1)} %pad_add_fusion.meta, bf16[2,2,256,256]{3,2,1,0:T(8,128)(2,1)S(1)} %bitcast.70, bf16[2,2,256,256]{3,2,1,0:T(8,128)(2,1)S(1)} %collective-permute-done.east, bf16[2,2,64,384]{3,2,1,0:T(8,128)(2,1)S(1)} %constant_dynamic-update-slice_fusion.l0, ...), custom_call_target="tpu_custom_call" | custom-call | flops 2147483648 | bytes 12582912 | tf_op jit(solution)/shard_map/pallas_call | solution.py:238
  41.5 8.8 %shard_map.105 = (bf16[2,4,512,256]{3,2,1,0:T(8,128)(2,1)S(1)}, bf16[2,2,3,64,128]{4,3,2,1,0:T(8,128)(2,1)S(1)}, bf16[2,2,3,64,128]{4,3,2,1,0:T(8,128)(2,1)S(1)}...) custom-call(s32[19]{0:T(128)S(1)} %pad_add_fusion.meta, bf16[2,2,256,256]{3,2,1,0:T(8,128)(2,1)S(1)} %bitcast.71, ...), custom_call_target="tpu_custom_call" | custom-call | flops 4294967296 | bytes 12582912 | tf_op jit(solution)/shard_map/pallas_call | solution.py:238
  50.3 5.7 %shard_map.106 = (bf16[2,2,3,64,128]{4,3,2,1,0:T(8,128)(2,1)S(1)}, bf16[2,2,3,64,128]{4,3,2,1,0:T(8,128)(2,1)S(1)}, bf16[2,2,3,64,128]{4,3,2,1,0:T(8,128)(2,1)S(...) custom-call(s32[19]{0:T(128)S(1)} %pad_add_fusion.meta, ...), custom_call_target="tpu_custom_call" | custom-call | flops 2147483648 | bytes 12582912 | tf_op jit(solution)/shard_map/pallas_call | solution.py:238
  56.0 1.6 %collective-permute-start.18 = (bf16[4,256,256]{2,1,0:T(8,128)(2,1)S(1)}, bf16[4,256,256]{2,1,0:T(8,128)(2,1)S(1)}, u32[]{:S(2)}, u32[]{:S(2)}) collective-permute-start(bf16[4,256,256]{2,1,0:T(8,128)(2,1)S(1)} %get-tuple-element.31), channel_id=1, source_target_pairs={{0,4},{4,0},{8,12},{12,8},{16,20},{20,16},{24,28},{28,24},{32,36},... | collective-permute-start | bytes 1572872 | tf_op jit(solution)/shard_map/ppermute | solution.py:301
  58.1 3.1 %collective-permute-start.11 = (bf16[2,2,3,64,128]{4,3,2,1,0:T(8,128)(2,1)S(1)}, bf16[2,2,3,64,128]{4,3,2,1,0:T(8,128)(2,1)S(1)}, u32[]{:S(2)}, u32[]{:S(2)}) collective-permute-start(bf16[2,2,3,64,128]{4,3,2,1,0:T(8,128)(2,1)S(1)} %get-tuple-element.24), channel_id=1, source_target_pairs={{0,2},{1,3},{2,0},{3,1},{4,6},{5,7},{6,4},{7,5},{8,10},{9,11},{10,... | collective-permute-start | bytes 589832 | tf_op jit(solution)/shard_map/ppermute | solution.py:293
  61.2 1.5 %collective-permute-start.13 = (bf16[2,2,3,64,128]{4,3,2,1,0:T(8,128)(2,1)S(1)}, bf16[2,2,3,64,128]{4,3,2,1,0:T(8,128)(2,1)S(1)}, u32[]{:S(2)}, u32[]{:S(2)}) collective-permute-start(bf16[2,2,3,64,128]{4,3,2,1,0:T(8,128)(2,1)S(1)} %get-tuple-element.27), channel_id=1, source_target_pairs={{0,1},{1,2},{2,3},{3,0},{4,5},{5,6},{6,7},{7,4},{8,9},{9,10},{10,1... | collective-permute-start | bytes 589832 | tf_op jit(solution)/shard_map/ppermute | solution.py:293
  62.7 2.5 %collective-permute-done.10 = bf16[2,2,3,64,128]{4,3,2,1,0:T(8,128)(2,1)S(1)} collective-permute-done((bf16[2,2,3,64,128]{4,3,2,1,0:T(8,128)(2,1)S(1)}, bf16[2,2,3,64,128]{4,3,2,1,0:T(8,128)(2,1)S(1)}, u32[]{:S(2)}, u32[]{:S(2)}) %collective-permute-start.10) | collective-permute-done | bytes 196640 | tf_op jit(solution)/shard_map/ppermute | solution.py:293
  65.4 5.0 %collective-permute-done.11 = bf16[2,2,3,64,128]{4,3,2,1,0:T(8,128)(2,1)S(1)} collective-permute-done((bf16[2,2,3,64,128]{4,3,2,1,0:T(8,128)(2,1)S(1)}, bf16[2,2,3,64,128]{4,3,2,1,0:T(8,128)(2,1)S(1)}, u32[]{:S(2)}, u32[]{:S(2)}) %collective-permute-start.11) | collective-permute-done | bytes 196640 | tf_op jit(solution)/shard_map/ppermute | solution.py:293
  70.7 1.5 %collective-permute-start.19 = (bf16[256,256]{1,0:T(8,128)(2,1)S(1)}, bf16[256,256]{1,0:T(8,128)(2,1)S(1)}, u32[]{:S(2)}, u32[]{:S(2)}) collective-permute-start(bf16[256,256]{1,0:T(8,128)(2,1)S(1)} %get-tuple-element.34), channel_id=1, source_target_pairs={{0,1},{1,2},{2,3},{3,0},{4,5},{5,6},{6,7},{7,4},{8,9},{9,10},{10,1... | collective-permute-start | bytes 393224 | tf_op jit(solution)/shard_map/ppermute | solution.py:293
  72.2 1.8 %collective-permute-start.21 = (bf16[256,256]{1,0:T(8,128)(2,1)S(1)}, bf16[256,256]{1,0:T(8,128)(2,1)S(1)}, u32[]{:S(2)}, u32[]{:S(2)}) collective-permute-start(bf16[256,256]{1,0:T(8,128)(2,1)S(1)} %get-tuple-element.35), channel_id=1, source_target_pairs={{0,3},{1,0},{2,1},{3,2},{4,7},{5,4},{6,5},{7,6},{8,11},{9,8},{10,9... | collective-permute-start | bytes 393224 | tf_op jit(solution)/shard_map/ppermute | solution.py:293
  75.2 3.7 %collective-permute-done.14 = bf16[2,2,3,64,128]{4,3,2,1,0:T(8,128)(2,1)S(1)} collective-permute-done((bf16[2,2,3,64,128]{4,3,2,1,0:T(8,128)(2,1)S(1)}, bf16[2,2,3,64,128]{4,3,2,1,0:T(8,128)(2,1)S(1)}, u32[]{:S(2)}, u32[]{:S(2)}) %collective-permute-start.14) | collective-permute-done | bytes 196640 | tf_op jit(solution)/shard_map/ppermute | solution.py:293
  79.1 7.1 %collective-permute-start.16 = (bf16[2,2,2,2,64,128]{5,4,2,1,0,3:T(8,128)(2,1)S(1)}, bf16[2,2,2,2,64,128]{5,4,2,1,0,3:T(8,128)(2,1)S(1)}, u32[]{:S(2)}, u32[]{:S(2)}) collective-permute-start(bf16[2,2,2,2,64,128]{5,4,2,1,0,3:T(8,128)(2,1)S(1)} %copy.25), channel_id=1, source_target_pairs={{0,4},{4,8},{8,12},{12,16},{16,20},{20,24},{24,28},{28,32},{32,36}... | collective-permute-start | bytes 786440 | tf_op jit(solution)/shard_map/ppermute | solution.py:289
  87.0 14.1 %all-to-all-start = ((bf16[32,8,256]{2,1,0:T(8,128)(2,1)}), bf16[32,8,256]{2,1,0:T(8,128)(2,1)S(1)}, u32[]{:S(2)}, u32[]{:S(2)}) async-start(bf16[32,8,256]{2,1,0:T(8,128)(2,1)} %fusion.17), calls=%async_computation | async-start | bytes 262144 | tf_op jit(solution)/shard_map/all_to_all | solution.py:327
  101.2 9.1 %all-to-all-done = bf16[32,8,256]{2,1,0:T(8,128)(2,1)S(1)} async-done(((bf16[32,8,256]{2,1,0:T(8,128)(2,1)}), bf16[32,8,256]{2,1,0:T(8,128)(2,1)S(1)}, u32[]{:S(2)}, u32[]{:S(2)}) %all-to-all-start) | async-done | bytes 131104 | tf_op jit(solution)/shard_map/all_to_all | solution.py:327
  111.0 3.9 %all-to-all-start.1 = ((bf16[32,8,256]{2,1,0:T(8,128)(2,1)}), bf16[32,8,256]{2,1,0:T(8,128)(2,1)S(1)}, u32[]{:S(2)}, u32[]{:S(2)}) async-start(bf16[32,8,256]{2,1,0:T(8,128)(2,1)} %broadcast_in_dim.5), calls=%async_computation.1 | async-start | bytes 262144 | tf_op jit(solution)/shard_map/all_to_all | solution.py:327
  114.9 7.0 %collective-permute-start.17 = (bf16[2,2,64,256]{3,2,1,0:T(8,128)(2,1)S(1)}, bf16[2,2,64,256]{3,2,1,0:T(8,128)(2,1)S(1)}, u32[]{:S(2)}, u32[]{:S(2)}) collective-permute-start(bf16[2,2,64,256]{3,2,1,0:T(8,128)(2,1)S(1)} %fusion.16), channel_id=1, source_target_pairs={{0,32},{4,36},{8,40},{12,44},{16,48},{20,52},{24,56},{28,60},{32,6... | collective-permute-start | bytes 393224 | tf_op jit(solution)/shard_map/ppermute | solution.py:289
  121.9 2.1 %all-to-all-done.1 = bf16[32,8,256]{2,1,0:T(8,128)(2,1)S(1)} async-done(((bf16[32,8,256]{2,1,0:T(8,128)(2,1)}), bf16[32,8,256]{2,1,0:T(8,128)(2,1)S(1)}, u32[]{:S(2)}, u32[]{:S(2)}) %all-to-all-start.1) | async-done | bytes 131104 | tf_op jit(solution)/shard_map/all_to_all | solution.py:327
  124.0 4.3 %collective-permute-start.22 = (bf16[256,256]{1,0:T(8,128)(2,1)S(1)}, bf16[256,256]{1,0:T(8,128)(2,1)S(1)}, u32[]{:S(2)}, u32[]{:S(2)}) collective-permute-start(bf16[256,256]{1,0:T(8,128)(2,1)S(1)} %bitcast.73), channel_id=1, source_target_pairs={{0,4},{4,0},{8,12},{12,8},{16,20},{20,16},{24,28},{28,24},{32,36},... | collective-permute-start | bytes 393224 | tf_op jit(solution)/shard_map/ppermute | solution.py:301
  (73 shorter events, 16.5 us)
Async XLA Ops:
  2.0 23.0 %collective-permute-start.8 = (bf16[256,256]{1,0:T(8,128)(2,1)S(1)}, bf16[256,256]{1,0:T(8,128)(2,1)S(1)}, u32[]{:S(2)}, u32[]{:S(2)}) collective-permute-start(bf16[256,256]{1,0:T(8,128)(2,1)S(1)} %dynamic-slice_bitcast_fusion.1), channel_id=1, source_target_pairs={{0,1},{1,2},{2,3},{3,0},{4,5},{5,6},{6,7},{7,4},{8,9},{9,10},{10,1... | collective-permute-start | bytes 393224 | tf_op jit(solution)/shard_map/ppermute | solution.py:293
  4.1 20.9 %collective-permute-start.7 = (bf16[256,256]{1,0:T(8,128)(2,1)S(1)}, bf16[256,256]{1,0:T(8,128)(2,1)S(1)}, u32[]{:S(2)}, u32[]{:S(2)}) collective-permute-start(bf16[256,256]{1,0:T(8,128)(2,1)S(1)} %dynamic-slice_bitcast_fusion.1), channel_id=1, source_target_pairs={{0,2},{1,3},{2,0},{3,1},{4,6},{5,7},{6,4},{7,5},{8,10},{9,11},{10,... | collective-permute-start | bytes 393224 | tf_op jit(solution)/shard_map/ppermute | solution.py:293
  6.8 18.2 %collective-permute-start.6 = (bf16[256,256]{1,0:T(8,128)(2,1)S(1)}, bf16[256,256]{1,0:T(8,128)(2,1)S(1)}, u32[]{:S(2)}, u32[]{:S(2)}) collective-permute-start(bf16[256,256]{1,0:T(8,128)(2,1)S(1)} %dynamic-slice_bitcast_fusion.1), channel_id=1, source_target_pairs={{0,3},{1,0},{2,1},{3,2},{4,7},{5,4},{6,5},{7,6},{8,11},{9,8},{10,9... | collective-permute-start | bytes 393224 | tf_op jit(solution)/shard_map/ppermute | solution.py:293
  8.8 16.4 %collective-permute-start.2 = (bf16[2,2,64,256]{3,2,1,0:T(8,128)(2,1)S(1)}, bf16[2,2,64,256]{3,2,1,0:T(8,128)(2,1)S(1)}, u32[]{:S(2)}, u32[]{:S(2)}) collective-permute-start(bf16[2,2,64,256]{3,2,1,0:T(8,128)(2,1)S(1)} %dynamic-slice_bitcast_fusion.2), channel_id=1, source_target_pairs={{36,0},{40,4},{44,8},{48,12},{52,16},{56,20},{60,24},{64,28},{68,3... | collective-permute-start | bytes 393224 | tf_op jit(solution)/shard_map/ppermute | solution.py:289
  10.1 11.4 %collective-permute-start.1 = (bf16[2,2,64,128]{3,2,1,0:T(8,128)(2,1)S(1)}, bf16[2,2,64,128]{3,2,1,0:T(8,128)(2,1)S(1)}, u32[]{:S(2)}, u32[]{:S(2)}) collective-permute-start(bf16[2,2,64,128]{3,2,1,0:T(8,128)(2,1)S(1)} %slice.49), channel_id=1, source_target_pairs={{32,0},{36,4},{40,8},{44,12},{48,16},{52,20},{56,24},{60,28},{64,3... | collective-permute-start | bytes 196616 | tf_op jit(solution)/shard_map/ppermute | solution.py:289
  21.5 15.6 %collective-permute-start = (bf16[2,2,256,256]{3,2,1,0:T(8,128)(2,1)}, bf16[2,2,256,256]{3,2,1,0:T(8,128)(2,1)S(1)}, u32[]{:S(2)}, u32[]{:S(2)}) collective-permute-start(bf16[2,2,256,256]{3,2,1,0:T(8,128)(2,1)} %bitcast.69), channel_id=1, source_target_pairs={{4,0},{8,4},{12,8},{16,12},{20,16},{24,20},{28,24},{32,28},{36,32}... | collective-permute-start | bytes 1572872 | tf_op jit(solution)/shard_map/ppermute | solution.py:289
  25.1 12.0 %collective-permute-start.9 = (bf16[3,256,256]{2,1,0:T(8,128)(2,1)S(1)}, bf16[3,256,256]{2,1,0:T(8,128)(2,1)S(1)}, u32[]{:S(2)}, u32[]{:S(2)}) collective-permute-start(bf16[3,256,256]{2,1,0:T(8,128)(2,1)S(1)} %pad_maximum_fusion.9.near), channel_id=1, source_target_pairs={{0,4},{4,0},{8,12},{12,8},{16,20},{20,16},{24,28},{28,24},{32,36},... | collective-permute-start | bytes 1179656 | tf_op jit(solution)/shard_map/ppermute | solution.py:301
  25.2 11.5 %collective-permute-start.5 = (bf16[2,2,64,384]{3,2,1,0:T(8,128)(2,1)S(1)}, bf16[2,2,64,384]{3,2,1,0:T(8,128)(2,1)S(1)}, u32[]{:S(2)}, u32[]{:S(2)}) collective-permute-start(bf16[2,2,64,384]{3,2,1,0:T(8,128)(2,1)S(1)} %constant_dynamic-update-slice_fusion.l0), channel_id=1, source_target_pairs={{0,1},{1,2},{2,3},{3,0},{4,5},{5,6},{6,7},{7,4},{8,9},{9,10},{10,1... | collective-permute-start | bytes 589832 | tf_op jit(solution)/shard_map/ppermute | solution.py:293
  25.7 11.0 %collective-permute-start.4 = (bf16[2,2,64,384]{3,2,1,0:T(8,128)(2,1)S(1)}, bf16[2,2,64,384]{3,2,1,0:T(8,128)(2,1)S(1)}, u32[]{:S(2)}, u32[]{:S(2)}) collective-permute-start(bf16[2,2,64,384]{3,2,1,0:T(8,128)(2,1)S(1)} %constant_dynamic-update-slice_fusion.l0), channel_id=1, source_target_pairs={{0,2},{1,3},{2,0},{3,1},{4,6},{5,7},{6,4},{7,5},{8,10},{9,11},{10,... | collective-permute-start | bytes 589832 | tf_op jit(solution)/shard_map/ppermute | solution.py:293
  26.5 10.6 %collective-permute-start.3 = (bf16[2,2,64,384]{3,2,1,0:T(8,128)(2,1)S(1)}, bf16[2,2,64,384]{3,2,1,0:T(8,128)(2,1)S(1)}, u32[]{:S(2)}, u32[]{:S(2)}) collective-permute-start(bf16[2,2,64,384]{3,2,1,0:T(8,128)(2,1)S(1)} %constant_dynamic-update-slice_fusion.l0), channel_id=1, source_target_pairs={{0,3},{1,0},{2,1},{3,2},{4,7},{5,4},{6,5},{7,6},{8,11},{9,8},{10,9... | collective-permute-start | bytes 589832 | tf_op jit(solution)/shard_map/ppermute | solution.py:293
  56.0 14.5 %collective-permute-start.18 = (bf16[4,256,256]{2,1,0:T(8,128)(2,1)S(1)}, bf16[4,256,256]{2,1,0:T(8,128)(2,1)S(1)}, u32[]{:S(2)}, u32[]{:S(2)}) collective-permute-start(bf16[4,256,256]{2,1,0:T(8,128)(2,1)S(1)} %get-tuple-element.31), channel_id=1, source_target_pairs={{0,4},{4,0},{8,12},{12,8},{16,20},{20,16},{24,28},{28,24},{32,36},... | collective-permute-start | bytes 1572872 | tf_op jit(solution)/shard_map/ppermute | solution.py:301
  57.6 7.6 %collective-permute-start.10 = (bf16[2,2,3,64,128]{4,3,2,1,0:T(8,128)(2,1)S(1)}, bf16[2,2,3,64,128]{4,3,2,1,0:T(8,128)(2,1)S(1)}, u32[]{:S(2)}, u32[]{:S(2)}) collective-permute-start(bf16[2,2,3,64,128]{4,3,2,1,0:T(8,128)(2,1)S(1)} %get-tuple-element.23), channel_id=1, source_target_pairs={{0,1},{1,2},{2,3},{3,0},{4,5},{5,6},{6,7},{7,4},{8,9},{9,10},{10,1... | collective-permute-start | bytes 589832 | tf_op jit(solution)/shard_map/ppermute | solution.py:293
  58.1 12.3 %collective-permute-start.11 = (bf16[2,2,3,64,128]{4,3,2,1,0:T(8,128)(2,1)S(1)}, bf16[2,2,3,64,128]{4,3,2,1,0:T(8,128)(2,1)S(1)}, u32[]{:S(2)}, u32[]{:S(2)}) collective-permute-start(bf16[2,2,3,64,128]{4,3,2,1,0:T(8,128)(2,1)S(1)} %get-tuple-element.24), channel_id=1, source_target_pairs={{0,2},{1,3},{2,0},{3,1},{4,6},{5,7},{6,4},{7,5},{8,10},{9,11},{10,... | collective-permute-start | bytes 589832 | tf_op jit(solution)/shard_map/ppermute | solution.py:293
  61.2 9.2 %collective-permute-start.12 = (bf16[2,2,3,64,128]{4,3,2,1,0:T(8,128)(2,1)S(1)}, bf16[2,2,3,64,128]{4,3,2,1,0:T(8,128)(2,1)S(1)}, u32[]{:S(2)}, u32[]{:S(2)}) collective-permute-start(bf16[2,2,3,64,128]{4,3,2,1,0:T(8,128)(2,1)S(1)} %get-tuple-element.25), channel_id=1, source_target_pairs={{0,3},{1,0},{2,1},{3,2},{4,7},{5,4},{6,5},{7,6},{8,11},{9,8},{10,9... | collective-permute-start | bytes 589832 | tf_op jit(solution)/shard_map/ppermute | solution.py:293
  61.2 12.8 %collective-permute-start.13 = (bf16[2,2,3,64,128]{4,3,2,1,0:T(8,128)(2,1)S(1)}, bf16[2,2,3,64,128]{4,3,2,1,0:T(8,128)(2,1)S(1)}, u32[]{:S(2)}, u32[]{:S(2)}) collective-permute-start(bf16[2,2,3,64,128]{4,3,2,1,0:T(8,128)(2,1)S(1)} %get-tuple-element.27), channel_id=1, source_target_pairs={{0,1},{1,2},{2,3},{3,0},{4,5},{5,6},{6,7},{7,4},{8,9},{9,10},{10,1... | collective-permute-start | bytes 589832 | tf_op jit(solution)/shard_map/ppermute | solution.py:293
  65.2 13.6 %collective-permute-start.14 = (bf16[2,2,3,64,128]{4,3,2,1,0:T(8,128)(2,1)S(1)}, bf16[2,2,3,64,128]{4,3,2,1,0:T(8,128)(2,1)S(1)}, u32[]{:S(2)}, u32[]{:S(2)}) collective-permute-start(bf16[2,2,3,64,128]{4,3,2,1,0:T(8,128)(2,1)S(1)} %get-tuple-element.28), channel_id=1, source_target_pairs={{0,2},{1,3},{2,0},{3,1},{4,6},{5,7},{6,4},{7,5},{8,10},{9,11},{10,... | collective-permute-start | bytes 589832 | tf_op jit(solution)/shard_map/ppermute | solution.py:293
  70.4 8.5 %collective-permute-start.15 = (bf16[2,2,3,64,128]{4,3,2,1,0:T(8,128)(2,1)S(1)}, bf16[2,2,3,64,128]{4,3,2,1,0:T(8,128)(2,1)S(1)}, u32[]{:S(2)}, u32[]{:S(2)}) collective-permute-start(bf16[2,2,3,64,128]{4,3,2,1,0:T(8,128)(2,1)S(1)} %get-tuple-element.29), channel_id=1, source_target_pairs={{0,3},{1,0},{2,1},{3,2},{4,7},{5,4},{6,5},{7,6},{8,11},{9,8},{10,9... | collective-permute-start | bytes 589832 | tf_op jit(solution)/shard_map/ppermute | solution.py:293
  70.7 15.5 %collective-permute-start.19 = (bf16[256,256]{1,0:T(8,128)(2,1)S(1)}, bf16[256,256]{1,0:T(8,128)(2,1)S(1)}, u32[]{:S(2)}, u32[]{:S(2)}) collective-permute-start(bf16[256,256]{1,0:T(8,128)(2,1)S(1)} %get-tuple-element.34), channel_id=1, source_target_pairs={{0,1},{1,2},{2,3},{3,0},{4,5},{5,6},{6,7},{7,4},{8,9},{9,10},{10,1... | collective-permute-start | bytes 393224 | tf_op jit(solution)/shard_map/ppermute | solution.py:293
  72.2 14.0 %collective-permute-start.21 = (bf16[256,256]{1,0:T(8,128)(2,1)S(1)}, bf16[256,256]{1,0:T(8,128)(2,1)S(1)}, u32[]{:S(2)}, u32[]{:S(2)}) collective-permute-start(bf16[256,256]{1,0:T(8,128)(2,1)S(1)} %get-tuple-element.35), channel_id=1, source_target_pairs={{0,3},{1,0},{2,1},{3,2},{4,7},{5,4},{6,5},{7,6},{8,11},{9,8},{10,9... | collective-permute-start | bytes 393224 | tf_op jit(solution)/shard_map/ppermute | solution.py:293
  74.1 12.2 %collective-permute-start.20 = (bf16[256,256]{1,0:T(8,128)(2,1)S(1)}, bf16[256,256]{1,0:T(8,128)(2,1)S(1)}, u32[]{:S(2)}, u32[]{:S(2)}) collective-permute-start(bf16[256,256]{1,0:T(8,128)(2,1)S(1)} %get-tuple-element.36), channel_id=1, source_target_pairs={{0,2},{1,3},{2,0},{3,1},{4,6},{5,7},{6,4},{7,5},{8,10},{9,11},{10,... | collective-permute-start | bytes 393224 | tf_op jit(solution)/shard_map/ppermute | solution.py:293
  79.1 22.0 %collective-permute-start.16 = (bf16[2,2,2,2,64,128]{5,4,2,1,0,3:T(8,128)(2,1)S(1)}, bf16[2,2,2,2,64,128]{5,4,2,1,0,3:T(8,128)(2,1)S(1)}, u32[]{:S(2)}, u32[]{:S(2)}) collective-permute-start(bf16[2,2,2,2,64,128]{5,4,2,1,0,3:T(8,128)(2,1)S(1)} %copy.25), channel_id=1, source_target_pairs={{0,4},{4,8},{8,12},{12,16},{16,20},{20,24},{24,28},{28,32},{32,36}... | collective-permute-start | bytes 786440 | tf_op jit(solution)/shard_map/ppermute | solution.py:289
  87.0 23.3 %all-to-all-start = ((bf16[32,8,256]{2,1,0:T(8,128)(2,1)}), bf16[32,8,256]{2,1,0:T(8,128)(2,1)S(1)}, u32[]{:S(2)}, u32[]{:S(2)}) async-start(bf16[32,8,256]{2,1,0:T(8,128)(2,1)} %fusion.17), calls=%async_computation | async-start | bytes 262144 | tf_op jit(solution)/shard_map/all_to_all | solution.py:327
  111.0 13.0 %all-to-all-start.1 = ((bf16[32,8,256]{2,1,0:T(8,128)(2,1)}), bf16[32,8,256]{2,1,0:T(8,128)(2,1)S(1)}, u32[]{:S(2)}, u32[]{:S(2)}) async-start(bf16[32,8,256]{2,1,0:T(8,128)(2,1)} %broadcast_in_dim.5), calls=%async_computation.1 | async-start | bytes 262144 | tf_op jit(solution)/shard_map/all_to_all | solution.py:327
  114.9 13.4 %collective-permute-start.17 = (bf16[2,2,64,256]{3,2,1,0:T(8,128)(2,1)S(1)}, bf16[2,2,64,256]{3,2,1,0:T(8,128)(2,1)S(1)}, u32[]{:S(2)}, u32[]{:S(2)}) collective-permute-start(bf16[2,2,64,256]{3,2,1,0:T(8,128)(2,1)S(1)} %fusion.16), channel_id=1, source_target_pairs={{0,32},{4,36},{8,40},{12,44},{16,48},{20,52},{24,56},{28,60},{32,6... | collective-permute-start | bytes 393224 | tf_op jit(solution)/shard_map/ppermute | solution.py:289
  (7 other events, 168.9 us)
where the time goes:
time: 131 us; the launch traced here: 130 us
  starting transfers between devices  62.9 us (48%)
  waiting for transfers between devices  37.6 us (29%)
  Pallas kernels  18.9 us (14%)
  other arithmetic  6.36 us (5%)
  local copies, waits for them, and re-layouts  2.62 us (2%)
  between operations  1.73 us (1%)
    ppermute x5, starting transfers between devices, toward(): return lax.ppermute(value, 'tile', pairs)  20.1 us
    pallas_call x3, Pallas kernels, kernel_call(): pl.pallas_call(body, out_shape=tuple((jax.ShapeDtypeStruct(*shape) for sh...  18.9 us
    ppermute x15, starting transfers between devices, to_mode(): lax.ppermute(value, 'mode', [(m, (m + steps) % MODES) for m in range(MODE...  18.8 us
    ppermute x15, waiting for transfers between devices, to_mode(): lax.ppermute(value, 'mode', [(m, (m + steps) % MODES) for m in range(MODE...  18.6 us
    all_to_all x2, starting transfers between devices, exchange(): return lax.all_to_all(value, 'tile', 0, 0, axis_index_groups=groups)  18 us
    all_to_all x2, waiting for transfers between devices, exchange(): return lax.all_to_all(value, 'tile', 0, 0, axis_index_groups=groups)  11.2 us
    ppermute x5, waiting for transfers between devices, toward(): return lax.ppermute(value, 'tile', pairs)  7.5 us
    ppermute x3, starting transfers between devices, to_core(): return lax.ppermute(value, 'tile', [(t, t ^ 1) for t in range(TILES)])  5.98 us
  transfers between devices with their start and end apart: 25, of which 9 were waited for; matrix products, arithmetic and copies ran while one was open for 5% of the time, Pallas kernels for 0%

commit v1 on v0

--- a/solution.py
+++ b/solution.py
@@ -100,14 +100,15 @@
             total[part, 2, rows] = total[part, 2, rows] + jnp.where(low, right, zero)
 
 
-def share_rows(total, shares, mode):
+def share_rows(totals, shares, mode):
     for step in range(MODES):
         owner = lax.rem(mode + step, MODES)
         for half in range(2):
             rows = pl.ds(pl.multiple_of(PW * half + SHARE * owner, SHARE), SHARE)
             for part in range(2):
                 for t in range(3):
-                    shares[step][part, half, t] = total[part, t, rows].astype(bf16)
+                    for depth in range(2):
+                        shares[step][depth, part, half, t] = totals[depth][part, t, rows].astype(bf16)
 
 
 def set_rows(both, top, bottom):
@@ -129,12 +130,13 @@
     return lax.fori_loop(0, MODES // UNROLL, trip, 0)
 
 
-def propagate_kernel(meta, own, east, l0, l1, l2, l3, probe, near, far, left, right, arrived, window, patch, probes, rows, lanes):
+def propagate_kernel(meta, own, east, l0, l1, l2, l3, probe, near, far, left, right, arrived, patches, window, probes, rows, lanes):
     load_probes(probes, meta, probe, near, far)
     build_window(window, 0, meta, own, east, (l0, l1, l2, l3))
 
     def one_slot(turn, _):
         row, col, _ = corner_of(meta, turn)
+        patch = patches.at[turn]
         cut(window, patch, row, col)
 
         def one_mode(mode, lane_set):
@@ -149,7 +151,7 @@
     lax.fori_loop(0, 2, one_slot, 0)
 
 
-def detector_kernel(meta, own, east, l0, l1, l2, l3, arrived, measured, plus, minus, arrived_grad, g0, g1, g2, g3, window, patch, rows, lanes, far, weight, second, total):
+def detector_kernel(meta, own, east, l0, l1, l2, l3, arrived, measured, plus, minus, arrived_grad, total, window, patch, rows, lanes, far, weight, second):
     build_window(window, 1, meta, own, east, (l0, l1, l2, l3))
     total[...] = jnp.zeros_like(total)
 
@@ -196,18 +198,16 @@
         return 0
 
     lax.fori_loop(0, 2, one_slot, 0)
-    share_rows(total, (g0, g1, g2, g3), meta[2 * SLOTS + 1])
-
-
-def return_kernel(meta, own, east, l0, l1, l2, l3, arrived_grad, probe, near, far, left, right, g0, g1, g2, g3, kept, sent, window, patch, probes, lanes, first, total, probe_total):
+
+
+def return_kernel(meta, patches, arrived_grad, second_total, probe, near, far, left, right, g0, g1, g2, g3, kept, sent, probes, lanes, first, total, probe_total):
     load_probes(probes, meta, probe, near, far)
-    build_window(window, 0, meta, own, east, (l0, l1, l2, l3))
     total[...] = jnp.zeros_like(total)
     probe_total[...] = jnp.zeros_like(probe_total)
 
     def one_slot(turn, _):
         row, col, _ = corner_of(meta, turn)
-        cut(window, patch, row, col)
+        patch = patches.at[turn]
         first[...] = jnp.zeros_like(first)
 
         def one_mode(mode, lane_set):
@@ -226,7 +226,7 @@
         return 0
 
     lax.fori_loop(0, 2, one_slot, 0)
-    share_rows(total, (g0, g1, g2, g3), meta[2 * SLOTS + 1])
+    share_rows((total, second_total), (g0, g1, g2, g3), meta[2 * SLOTS + 1])
     core = meta[2 * SLOTS + 2]
     kept[...] = probe_total[core]
     sent[...] = probe_total[1 - core].astype(bf16)
@@ -251,37 +251,37 @@
 ROWS = ((UNROLL, 2 * PW, PW), bf16)
 LANES = ((UNROLL, PW, 2 * PW), bf16)
 PROBES = ((MODES, 2, PW, PW), bf16)
-SHARES = [((2, 2, 3, SHARE, HALF), bf16)] * MODES
+SHARES = [((2, 2, 2, 3, SHARE, HALF), bf16)] * MODES
 TRANSFORM = 8 * 16 * PW * PW * PW
 
 
 def kernels(meta, pieces, all_probes, turns, matrices):
     plus, minus, left, right = matrices
-    (arrived,) = kernel_call(
+    arrived, patches = kernel_call(
         propagate_kernel,
-        [((2, MODES, PW, 2 * PW), f32)],
-        [WINDOW, PATCH, PROBES, ROWS, LANES],
+        [((2, MODES, PW, 2 * PW), f32), ((2, 2, PW, PW), f32)],
+        [WINDOW, PROBES, ROWS, LANES],
         (meta, *pieces, *all_probes, left, right),
         TRANSFORM,
         16,
     )
-    arrived_grad, *second_shares = kernel_call(
+    arrived_grad, second_total = kernel_call(
         detector_kernel,
-        [((2, MODES, 2 * PW, PW), bf16)] + SHARES,
-        [WINDOW, PATCH, ROWS, LANES, ((MODES, PW, 2 * PW), f32), ((PW, PW), f32), PATCH, WINDOW],
+        [((2, MODES, 2 * PW, PW), bf16), WINDOW],
+        [WINDOW, PATCH, ROWS, LANES, ((MODES, PW, 2 * PW), f32), ((PW, PW), f32), PATCH],
         (meta, *pieces, arrived, turns, plus, minus),
         2 * TRANSFORM,
         26,
     )
-    *first_shares, kept, sent = kernel_call(
+    *shares, kept, sent = kernel_call(
         return_kernel,
         SHARES + [((MODES, PW, PW), f32), ((MODES, PW, PW), bf16)],
-        [WINDOW, PATCH, PROBES, LANES, PATCH, WINDOW, ((2, MODES, PW, PW), f32)],
-        (meta, *pieces, arrived_grad, *all_probes, right, left),
+        [PROBES, LANES, PATCH, WINDOW, ((2, MODES, PW, PW), f32)],
+        (meta, patches, arrived_grad, second_total, *all_probes, right, left),
         TRANSFORM,
         20,
     )
-    return second_shares, first_shares, kept, sent
+    return shares, kept, sent
 
 
 def toward(value, steps):
@@ -335,33 +335,32 @@
     quarter = lax.dynamic_slice_in_dim(own, SHARE * mode, SHARE, 2)
     corner = toward(quarter, -TGX - 1)
     south = toward(quarter[..., HALF:], -TGX)
-    probe = probes[0].astype(bf16)
-    near = jnp.stack(fetch(lax.dynamic_index_in_dim(probe, core, 0, keepdims=False)))
+    near = fetch(lax.dynamic_index_in_dim(probes[0], core, 0, keepdims=False).astype(bf16))
+    near = jnp.stack(near)
     far = to_core(near)
     east = toward(own, -1)
     lower = jnp.concatenate([south, corner], axis=-1)
     quarters = [lower] + fetch(lower)
     pieces = (own, east, *quarters)
+    probe = probes[0].astype(bf16)
     all_probes = (probe, near, far)
     matrices = block_forms(*lax.optimization_barrier(tuple(jnp.asarray(table) for table in constants())))
     meta = jnp.concatenate([offsets.reshape(-1), counts, jnp.stack([mode, core])]).astype(jnp.int32)
     turns = lax.dynamic_index_in_dim(measured[0].reshape(2, MODES, PW, PW), mode, 1, keepdims=False)
-    second_shares, first_shares, kept, sent = kernels(meta, pieces, all_probes, turns, matrices)
-    second = add_up(send_rows(second_shares))
+    shares, kept, sent = kernels(meta, pieces, all_probes, turns, matrices)
     halves = kept + to_core(sent).astype(f32)
     mine = add_up(send_rows([halves[0]] + [halves[step].astype(bf16) for step in range(1, MODES)]))
     parts = exchange(mine.astype(bf16).reshape(32, 8, PW))
     part = jnp.sum(parts.astype(f32), axis=0).astype(bf16)
-    first = add_up(send_rows(first_shares))
-    rows = jnp.stack([first, second])
+    rows = add_up(send_rows(shares))
     eastward = toward(rows[:, :, :, 1:].astype(bf16), 1).astype(f32)
     joined = jnp.concatenate([eastward[:, :, :, 0], eastward[:, :, :, 1] + rows[:, :, :, 0]], axis=-1)
     object_grad = joined[:, :, 0] + toward(joined[:, :, 1].astype(bf16), TGX).astype(f32)
     plane = exchange(jnp.broadcast_to(part[None], (32, 8, PW))).reshape(PW, PW)
     other = to_core(plane)
-    real = jnp.where(core == 0, plane, other)
-    imag = jnp.where(core == 0, other, plane)
-    return (object_grad[None], jnp.stack([real, imag]).astype(f32)[None])
+    mine_first = (jnp.arange(2, dtype=jnp.int32) == core)[:, None, None]
+    probe_grad = jnp.where(mine_first, plane[None].astype(f32), other[None].astype(f32))
+    return (object_grad[None], probe_grad[None])
 
 
 def solution(mesh):

time: 131 us -> 128 us (0.977)
  starting transfers between devices: 62.9 us -> 58.6 us
    ppermute x15 -> x12, waiting for transfers between devices: 18.6 us -> 23.1 us  [to_mode(): lax.ppermute(value, 'mode', [(m, (m + steps) % MODES) for m in range(MODE...]
    ppermute x5, waiting for transfers between devices: 7.5 us -> 3.11 us  [toward(): return lax.ppermute(value, 'tile', pairs)]
    ppermute x15 -> x12, starting transfers between devices: 18.8 us -> 15.8 us  [to_mode(): lax.ppermute(value, 'mode', [(m, (m + steps) % MODES) for m in range(MODE...]
    convert_element_type x2 -> x1, other arithmetic: 2.28 us -> 0.03 us  [one_step(): probe = probes[0].astype(bf16)]
  transfers between devices with their start and end apart: 25 -> 22, of which waited for: 9 -> 9; matrix products, arithmetic and copies ran while one was open for 5% -> 6% of each run, Pallas kernels for 0% -> 0%
where the time goes in v1:
time: 128 us; the launch traced here: 127 us
  starting transfers between devices  58.6 us (46%)
  waiting for transfers between devices  37.6 us (29%)
  Pallas kernels  19.3 us (15%)
  other arithmetic  6.27 us (5%)
  local copies, waits for them, and re-layouts  3.68 us (3%)
  between operations  1.65 us (1%)
    ppermute x12, waiting for transfers between devices, to_mode(): lax.ppermute(value, 'mode', [(m, (m + steps) % MODES) for m in range(MODE...  23.1 us
    ppermute x5, starting transfers between devices, toward(): return lax.ppermute(value, 'tile', pairs)  20.4 us
    pallas_call x3, Pallas kernels, kernel_call(): pl.pallas_call(body, out_shape=tuple((jax.ShapeDtypeStruct(*shape) for sh...  19.3 us
    all_to_all x2, starting transfers between devices, exchange(): return lax.all_to_all(value, 'tile', 0, 0, axis_index_groups=groups)  17.4 us
    ppermute x12, starting transfers between devices, to_mode(): lax.ppermute(value, 'mode', [(m, (m + steps) % MODES) for m in range(MODE...  15.8 us
    all_to_all x2, waiting for transfers between devices, exchange(): return lax.all_to_all(value, 'tile', 0, 0, axis_index_groups=groups)  10.4 us
    ppermute x3, starting transfers between devices, to_core(): return lax.ppermute(value, 'tile', [(t, t ^ 1) for t in range(TILES)])  5.05 us
    ppermute x5, waiting for transfers between devices, toward(): return lax.ppermute(value, 'tile', pairs)  3.11 us
  transfers between devices with their start and end apart: 22, of which 9 were waited for; matrix products, arithmetic and copies ran while one was open for 6% of the time, Pallas kernels for 0%

profile of v1, /device:TPU:1, one launch (start us, length us, event | category | flops | bytes accessed | tf_op | source)
XLA Modules:
  0.0 127.1 jit_solution(4619273562280420972)
XLA Ops:
  1.7 2.2 %collective-permute-start.8 = (bf16[256,256]{1,0:T(8,128)(2,1)S(1)}, bf16[256,256]{1,0:T(8,128)(2,1)S(1)}, u32[]{:S(2)}, u32[]{:S(2)}) collective-permute-start(bf16[256,256]{1,0:T(8,128)(2,1)S(1)} %fusion.14), channel_id=1, source_target_pairs={{0,1},{1,2},{2,3},{3,0},{4,5},{5,6},{6,7},{7,4},{8,9},{9,10},{10,1... | collective-permute-start | bytes 393224 | tf_op jit(solution)/shard_map/ppermute | solution.py:293
  3.9 2.6 %collective-permute-start.7 = (bf16[256,256]{1,0:T(8,128)(2,1)S(1)}, bf16[256,256]{1,0:T(8,128)(2,1)S(1)}, u32[]{:S(2)}, u32[]{:S(2)}) collective-permute-start(bf16[256,256]{1,0:T(8,128)(2,1)S(1)} %fusion.14), channel_id=1, source_target_pairs={{0,2},{1,3},{2,0},{3,1},{4,6},{5,7},{6,4},{7,5},{8,10},{9,11},{10,... | collective-permute-start | bytes 393224 | tf_op jit(solution)/shard_map/ppermute | solution.py:293
  8.6 1.4 %collective-permute-start.2 = (bf16[2,2,64,256]{3,2,1,0:T(8,128)(2,1)S(1)}, bf16[2,2,64,256]{3,2,1,0:T(8,128)(2,1)S(1)}, u32[]{:S(2)}, u32[]{:S(2)}) collective-permute-start(bf16[2,2,64,256]{3,2,1,0:T(8,128)(2,1)S(1)} %dynamic-slice_bitcast_fusion.1), channel_id=1, source_target_pairs={{36,0},{40,4},{44,8},{48,12},{52,16},{56,20},{60,24},{64,28},{68,3... | collective-permute-start | bytes 393224 | tf_op jit(solution)/shard_map/ppermute | solution.py:289
  10.0 1.3 %collective-permute-start.1 = (bf16[2,2,64,128]{3,2,1,0:T(8,128)(2,1)S(1)}, bf16[2,2,64,128]{3,2,1,0:T(8,128)(2,1)S(1)}, u32[]{:S(2)}, u32[]{:S(2)}) collective-permute-start(bf16[2,2,64,128]{3,2,1,0:T(8,128)(2,1)S(1)} %slice.49), channel_id=1, source_target_pairs={{32,0},{36,4},{40,8},{44,12},{48,16},{52,20},{56,24},{60,28},{64,3... | collective-permute-start | bytes 196616 | tf_op jit(solution)/shard_map/ppermute | solution.py:289
  16.1 3.4 %collective-permute-start = (bf16[2,2,256,256]{3,2,1,0:T(8,128)(2,1)S(1)}, bf16[2,2,256,256]{3,2,1,0:T(8,128)(2,1)S(1)}, u32[]{:S(2)}, u32[]{:S(2)}) collective-permute-start(bf16[2,2,256,256]{3,2,1,0:T(8,128)(2,1)S(1)} %bitcast.60), channel_id=1, source_target_pairs={{4,0},{8,4},{12,8},{16,12},{20,16},{24,20},{28,24},{32,28},{36,32}... | collective-permute-start | bytes 1572872 | tf_op jit(solution)/shard_map/ppermute | solution.py:289
  19.7 1.7 %collective-permute-done.1 = bf16[2,2,64,128]{3,2,1,0:T(8,128)(2,1)S(1)} collective-permute-done((bf16[2,2,64,128]{3,2,1,0:T(8,128)(2,1)S(1)}, bf16[2,2,64,128]{3,2,1,0:T(8,128)(2,1)S(1)}, u32[]{:S(2)}, u32[]{:S(2)}) %collective-permute-start.1) | collective-permute-done | bytes 65568 | tf_op jit(solution)/shard_map/ppermute | solution.py:289
  21.4 1.4 %collective-permute-done.2 = bf16[2,2,64,256]{3,2,1,0:T(8,128)(2,1)S(1)} collective-permute-done((bf16[2,2,64,256]{3,2,1,0:T(8,128)(2,1)S(1)}, bf16[2,2,64,256]{3,2,1,0:T(8,128)(2,1)S(1)}, u32[]{:S(2)}, u32[]{:S(2)}) %collective-permute-start.2) | collective-permute-done | bytes 131104 | tf_op jit(solution)/shard_map/ppermute | solution.py:289
  24.4 2.0 %collective-permute-start.3 = (bf16[2,2,64,384]{3,2,1,0:T(8,128)(2,1)S(1)}, bf16[2,2,64,384]{3,2,1,0:T(8,128)(2,1)S(1)}, u32[]{:S(2)}, u32[]{:S(2)}) collective-permute-start(bf16[2,2,64,384]{3,2,1,0:T(8,128)(2,1)S(1)} %constant_dynamic-update-slice_fusion.l0), channel_id=1, source_target_pairs={{0,3},{1,0},{2,1},{3,2},{4,7},{5,4},{6,5},{7,6},{8,11},{9,8},{10,9... | collective-permute-start | bytes 589832 | tf_op jit(solution)/shard_map/ppermute | solution.py:293
  26.4 8.3 %collective-permute-done.5.l3 = bf16[2,2,64,384]{3,2,1,0:T(8,128)(2,1)S(1)} collective-permute-done((bf16[2,2,64,384]{3,2,1,0:T(8,128)(2,1)S(1)}, bf16[2,2,64,384]{3,2,1,0:T(8,128)(2,1)S(1)}, u32[]{:S(2)}, u32[]{:S(2)}) %collective-permute-start.5) | collective-permute-done | bytes 196640 | tf_op jit(solution)/shard_map/ppermute | solution.py:293
  35.0 4.7 %shard_map.104 = (f32[2,4,256,512]{3,2,1,0:T(8,128)S(1)}, f32[2,2,256,256]{3,2,1,0:T(8,128)S(1)}) custom-call(s32[19]{0:T(128)S(1)} %pad_add_fusion.meta, bf16[2,2,256,256]{3,2,1,0:T(8,128)(2,1)S(1)} %bitcast.61, bf16[2,2,256,256]{3,2,1,0:T(8,128)(2,1)S(1)} %collective-permute-done.east, bf16[2,2,64,384]{3,2,1,0:T(8,128)(2,1)S(1)} %constant_dynamic-update-slice_fusion.l0, ...), custom_call_target="tpu_custom_call" | custom-call | flops 2147483648 | bytes 12582912 | tf_op jit(solution)/shard_map/pallas_call | solution.py:238
  39.7 8.8 %shard_map.105 = (bf16[2,4,512,256]{3,2,1,0:T(8,128)(2,1)S(1)}, f32[2,3,512,128]{3,2,1,0:T(8,128)S(1)}) custom-call(s32[19]{0:T(128)S(1)} %pad_add_fusion.meta, bf16[2,2,256,256]{3,2,1,0:T(8,128)(2,1)S(1)} %bitcast.62, bf16[2,2,256,256]{3,2,1,0:T(8,128)(2,1)S(1)} %collective-permute-done.east, ...), custom_call_target="tpu_custom_call" | custom-call | flops 4294967296 | bytes 12582912 | tf_op jit(solution)/shard_map/pallas_call | solution.py:238
  48.5 5.9 %shard_map.106 = (bf16[2,2,2,3,64,128]{5,4,3,2,1,0:T(8,128)(2,1)S(1)}, bf16[2,2,2,3,64,128]{5,4,3,2,1,0:T(8,128)(2,1)S(1)}, bf16[2,2,2,3,64,128]{5,4,3,2,1,0:T(8...) custom-call(s32[19]{0:T(128)S(1)} %pad_add_fusion.meta, ...), custom_call_target="tpu_custom_call" | custom-call | flops 2147483648 | bytes 12582912 | tf_op jit(solution)/shard_map/pallas_call | solution.py:238
  54.4 1.4 %collective-permute-start.15 = (bf16[4,256,256]{2,1,0:T(8,128)(2,1)S(1)}, bf16[4,256,256]{2,1,0:T(8,128)(2,1)S(1)}, u32[]{:S(2)}, u32[]{:S(2)}) collective-permute-start(bf16[4,256,256]{2,1,0:T(8,128)(2,1)S(1)} %get-tuple-element.29), channel_id=1, source_target_pairs={{0,4},{4,0},{8,12},{12,8},{16,20},{20,16},{24,28},{28,24},{32,36},... | collective-permute-start | bytes 1572872 | tf_op jit(solution)/shard_map/ppermute | solution.py:301
  56.4 2.9 %collective-permute-start.11 = (bf16[2,2,2,3,64,128]{5,4,3,2,1,0:T(8,128)(2,1)S(1)}, bf16[2,2,2,3,64,128]{5,4,3,2,1,0:T(8,128)(2,1)S(1)}, u32[]{:S(2)}, u32[]{:S(2)}) collective-permute-start(bf16[2,2,2,3,64,128]{5,4,3,2,1,0:T(8,128)(2,1)S(1)} %get-tuple-element.26), channel_id=1, source_target_pairs={{0,2},{1,3},{2,0},{3,1},{4,6},{5,7},{6,4},{7,5},{8,10},{9,11},{10,... | collective-permute-start | bytes 1179656 | tf_op jit(solution)/shard_map/ppermute | solution.py:293
  59.5 1.5 %collective-permute-start.16 = (bf16[256,256]{1,0:T(8,128)(2,1)S(1)}, bf16[256,256]{1,0:T(8,128)(2,1)S(1)}, u32[]{:S(2)}, u32[]{:S(2)}) collective-permute-start(bf16[256,256]{1,0:T(8,128)(2,1)S(1)} %get-tuple-element.32), channel_id=1, source_target_pairs={{0,1},{1,2},{2,3},{3,0},{4,5},{5,6},{6,7},{7,4},{8,9},{9,10},{10,1... | collective-permute-start | bytes 393224 | tf_op jit(solution)/shard_map/ppermute | solution.py:293
  62.3 5.3 %collective-permute-done.10 = bf16[2,2,2,3,64,128]{5,4,3,2,1,0:T(8,128)(2,1)S(1)} collective-permute-done((bf16[2,2,2,3,64,128]{5,4,3,2,1,0:T(8,128)(2,1)S(1)}, bf16[2,2,2,3,64,128]{5,4,3,2,1,0:T(8,128)(2,1)S(1)}, u32[]{:S(2)}, u32[]{:S(2)}) %collective-permute-start.10) | collective-permute-done | bytes 393248 | tf_op jit(solution)/shard_map/ppermute | solution.py:293
  67.7 9.2 %collective-permute-done.11 = bf16[2,2,2,3,64,128]{5,4,3,2,1,0:T(8,128)(2,1)S(1)} collective-permute-done((bf16[2,2,2,3,64,128]{5,4,3,2,1,0:T(8,128)(2,1)S(1)}, bf16[2,2,2,3,64,128]{5,4,3,2,1,0:T(8,128)(2,1)S(1)}, u32[]{:S(2)}, u32[]{:S(2)}) %collective-permute-start.11) | collective-permute-done | bytes 393248 | tf_op jit(solution)/shard_map/ppermute | solution.py:293
  77.2 7.2 %collective-permute-start.13 = (bf16[2,2,2,2,64,128]{5,4,2,1,0,3:T(8,128)(2,1)S(1)}, bf16[2,2,2,2,64,128]{5,4,2,1,0,3:T(8,128)(2,1)S(1)}, u32[]{:S(2)}, u32[]{:S(2)}) collective-permute-start(bf16[2,2,2,2,64,128]{5,4,2,1,0,3:T(8,128)(2,1)S(1)} %copy.25), channel_id=1, source_target_pairs={{0,4},{4,8},{8,12},{12,16},{16,20},{20,24},{24,28},{28,32},{32,36}... | collective-permute-start | bytes 786440 | tf_op jit(solution)/shard_map/ppermute | solution.py:289
  85.1 13.5 %all-to-all-start = ((bf16[32,8,256]{2,1,0:T(8,128)(2,1)}), bf16[32,8,256]{2,1,0:T(8,128)(2,1)S(1)}, u32[]{:S(2)}, u32[]{:S(2)}) async-start(bf16[32,8,256]{2,1,0:T(8,128)(2,1)} %fusion.16), calls=%async_computation | async-start | bytes 262144 | tf_op jit(solution)/shard_map/all_to_all | solution.py:327
  98.8 7.0 %collective-permute-start.14 = (bf16[2,2,64,256]{3,2,1,0:T(8,128)(2,1)S(1)}, bf16[2,2,64,256]{3,2,1,0:T(8,128)(2,1)S(1)}, u32[]{:S(2)}, u32[]{:S(2)}) collective-permute-start(bf16[2,2,64,256]{3,2,1,0:T(8,128)(2,1)S(1)} %fusion.15), channel_id=1, source_target_pairs={{0,32},{4,36},{8,40},{12,44},{16,48},{20,52},{24,56},{28,60},{32,6... | collective-permute-start | bytes 393224 | tf_op jit(solution)/shard_map/ppermute | solution.py:289
  105.9 2.0 %all-to-all-done = bf16[32,8,256]{2,1,0:T(8,128)(2,1)S(1)} async-done(((bf16[32,8,256]{2,1,0:T(8,128)(2,1)}), bf16[32,8,256]{2,1,0:T(8,128)(2,1)S(1)}, u32[]{:S(2)}, u32[]{:S(2)}) %all-to-all-start) | async-done | bytes 131104 | tf_op jit(solution)/shard_map/all_to_all | solution.py:327
  108.5 3.9 %all-to-all-start.1 = ((bf16[32,8,256]{2,1,0:T(8,128)(2,1)}), bf16[32,8,256]{2,1,0:T(8,128)(2,1)S(1)}, u32[]{:S(2)}, u32[]{:S(2)}) async-start(bf16[32,8,256]{2,1,0:T(8,128)(2,1)} %broadcast_in_dim.38), calls=%async_computation.1 | async-start | bytes 262144 | tf_op jit(solution)/shard_map/all_to_all | solution.py:327
  113.2 8.4 %all-to-all-done.1 = bf16[32,8,256]{2,1,0:T(8,128)(2,1)S(1)} async-done(((bf16[32,8,256]{2,1,0:T(8,128)(2,1)}), bf16[32,8,256]{2,1,0:T(8,128)(2,1)S(1)}, u32[]{:S(2)}, u32[]{:S(2)}) %all-to-all-start.1) | async-done | bytes 131104 | tf_op jit(solution)/shard_map/all_to_all | solution.py:327
  121.6 3.6 %collective-permute-start.19 = (bf16[256,256]{1,0:T(8,128)(2,1)S(1)}, bf16[256,256]{1,0:T(8,128)(2,1)S(1)}, u32[]{:S(2)}, u32[]{:S(2)}) collective-permute-start(bf16[256,256]{1,0:T(8,128)(2,1)S(1)} %bitcast.63), channel_id=1, source_target_pairs={{0,4},{4,0},{8,12},{12,8},{16,20},{20,16},{24,28},{28,24},{32,36},... | collective-permute-start | bytes 393224 | tf_op jit(solution)/shard_map/ppermute | solution.py:301
  (65 shorter events, 16.0 us)
Async XLA Ops:
  0.6 15.4 %copy-start.3 = (bf16[256,256]{1,0:T(8,128)(2,1)S(1)}, bf16[256,256]{1,0:T(8,128)(2,1)}, u32[]{:S(2)}) copy-start(bf16[256,256]{1,0:T(8,128)(2,1)} %constant.45.clone) | copy-start | bytes 393220
  0.7 15.4 %copy-start.4 = (bf16[256,256]{1,0:T(8,128)(2,1)S(1)}, bf16[256,256]{1,0:T(8,128)(2,1)}, u32[]{:S(2)}) copy-start(bf16[256,256]{1,0:T(8,128)(2,1)} %constant.44.clone) | copy-start | bytes 393220
  1.7 14.4 %collective-permute-start.8 = (bf16[256,256]{1,0:T(8,128)(2,1)S(1)}, bf16[256,256]{1,0:T(8,128)(2,1)S(1)}, u32[]{:S(2)}, u32[]{:S(2)}) collective-permute-start(bf16[256,256]{1,0:T(8,128)(2,1)S(1)} %fusion.14), channel_id=1, source_target_pairs={{0,1},{1,2},{2,3},{3,0},{4,5},{5,6},{6,7},{7,4},{8,9},{9,10},{10,1... | collective-permute-start | bytes 393224 | tf_op jit(solution)/shard_map/ppermute | solution.py:293
  3.9 15.6 %collective-permute-start.7 = (bf16[256,256]{1,0:T(8,128)(2,1)S(1)}, bf16[256,256]{1,0:T(8,128)(2,1)S(1)}, u32[]{:S(2)}, u32[]{:S(2)}) collective-permute-start(bf16[256,256]{1,0:T(8,128)(2,1)S(1)} %fusion.14), channel_id=1, source_target_pairs={{0,2},{1,3},{2,0},{3,1},{4,6},{5,7},{6,4},{7,5},{8,10},{9,11},{10,... | collective-permute-start | bytes 393224 | tf_op jit(solution)/shard_map/ppermute | solution.py:293
  6.6 13.0 %collective-permute-start.6 = (bf16[256,256]{1,0:T(8,128)(2,1)S(1)}, bf16[256,256]{1,0:T(8,128)(2,1)S(1)}, u32[]{:S(2)}, u32[]{:S(2)}) collective-permute-start(bf16[256,256]{1,0:T(8,128)(2,1)S(1)} %fusion.14), channel_id=1, source_target_pairs={{0,3},{1,0},{2,1},{3,2},{4,7},{5,4},{6,5},{7,6},{8,11},{9,8},{10,9... | collective-permute-start | bytes 393224 | tf_op jit(solution)/shard_map/ppermute | solution.py:293
  8.6 14.3 %collective-permute-start.2 = (bf16[2,2,64,256]{3,2,1,0:T(8,128)(2,1)S(1)}, bf16[2,2,64,256]{3,2,1,0:T(8,128)(2,1)S(1)}, u32[]{:S(2)}, u32[]{:S(2)}) collective-permute-start(bf16[2,2,64,256]{3,2,1,0:T(8,128)(2,1)S(1)} %dynamic-slice_bitcast_fusion.1), channel_id=1, source_target_pairs={{36,0},{40,4},{44,8},{48,12},{52,16},{56,20},{60,24},{64,28},{68,3... | collective-permute-start | bytes 393224 | tf_op jit(solution)/shard_map/ppermute | solution.py:289
  10.0 11.4 %collective-permute-start.1 = (bf16[2,2,64,128]{3,2,1,0:T(8,128)(2,1)S(1)}, bf16[2,2,64,128]{3,2,1,0:T(8,128)(2,1)S(1)}, u32[]{:S(2)}, u32[]{:S(2)}) collective-permute-start(bf16[2,2,64,128]{3,2,1,0:T(8,128)(2,1)S(1)} %slice.49), channel_id=1, source_target_pairs={{32,0},{36,4},{40,8},{44,12},{48,16},{52,20},{56,24},{60,28},{64,3... | collective-permute-start | bytes 196616 | tf_op jit(solution)/shard_map/ppermute | solution.py:289
  16.1 18.9 %collective-permute-start = (bf16[2,2,256,256]{3,2,1,0:T(8,128)(2,1)S(1)}, bf16[2,2,256,256]{3,2,1,0:T(8,128)(2,1)S(1)}, u32[]{:S(2)}, u32[]{:S(2)}) collective-permute-start(bf16[2,2,256,256]{3,2,1,0:T(8,128)(2,1)S(1)} %bitcast.60), channel_id=1, source_target_pairs={{4,0},{8,4},{12,8},{16,12},{20,16},{24,20},{28,24},{32,28},{36,32}... | collective-permute-start | bytes 1572872 | tf_op jit(solution)/shard_map/ppermute | solution.py:289
  19.6 15.4 %collective-permute-start.9 = (bf16[3,256,256]{2,1,0:T(8,128)(2,1)S(1)}, bf16[3,256,256]{2,1,0:T(8,128)(2,1)S(1)}, u32[]{:S(2)}, u32[]{:S(2)}) collective-permute-start(bf16[3,256,256]{2,1,0:T(8,128)(2,1)S(1)} %pad_maximum_fusion.8.near), channel_id=1, source_target_pairs={{0,4},{4,0},{8,12},{12,8},{16,20},{20,16},{24,28},{28,24},{32,36},... | collective-permute-start | bytes 1179656 | tf_op jit(solution)/shard_map/ppermute | solution.py:301
  22.9 11.8 %collective-permute-start.5 = (bf16[2,2,64,384]{3,2,1,0:T(8,128)(2,1)S(1)}, bf16[2,2,64,384]{3,2,1,0:T(8,128)(2,1)S(1)}, u32[]{:S(2)}, u32[]{:S(2)}) collective-permute-start(bf16[2,2,64,384]{3,2,1,0:T(8,128)(2,1)S(1)} %constant_dynamic-update-slice_fusion.l0), channel_id=1, source_target_pairs={{0,1},{1,2},{2,3},{3,0},{4,5},{5,6},{6,7},{7,4},{8,9},{9,10},{10,1... | collective-permute-start | bytes 589832 | tf_op jit(solution)/shard_map/ppermute | solution.py:293
  23.4 11.3 %collective-permute-start.4 = (bf16[2,2,64,384]{3,2,1,0:T(8,128)(2,1)S(1)}, bf16[2,2,64,384]{3,2,1,0:T(8,128)(2,1)S(1)}, u32[]{:S(2)}, u32[]{:S(2)}) collective-permute-start(bf16[2,2,64,384]{3,2,1,0:T(8,128)(2,1)S(1)} %constant_dynamic-update-slice_fusion.l0), channel_id=1, source_target_pairs={{0,2},{1,3},{2,0},{3,1},{4,6},{5,7},{6,4},{7,5},{8,10},{9,11},{10,... | collective-permute-start | bytes 589832 | tf_op jit(solution)/shard_map/ppermute | solution.py:293
  24.4 10.6 %collective-permute-start.3 = (bf16[2,2,64,384]{3,2,1,0:T(8,128)(2,1)S(1)}, bf16[2,2,64,384]{3,2,1,0:T(8,128)(2,1)S(1)}, u32[]{:S(2)}, u32[]{:S(2)}) collective-permute-start(bf16[2,2,64,384]{3,2,1,0:T(8,128)(2,1)S(1)} %constant_dynamic-update-slice_fusion.l0), channel_id=1, source_target_pairs={{0,3},{1,0},{2,1},{3,2},{4,7},{5,4},{6,5},{7,6},{8,11},{9,8},{10,9... | collective-permute-start | bytes 589832 | tf_op jit(solution)/shard_map/ppermute | solution.py:293
  54.4 4.9 %collective-permute-start.15 = (bf16[4,256,256]{2,1,0:T(8,128)(2,1)S(1)}, bf16[4,256,256]{2,1,0:T(8,128)(2,1)S(1)}, u32[]{:S(2)}, u32[]{:S(2)}) collective-permute-start(bf16[4,256,256]{2,1,0:T(8,128)(2,1)S(1)} %get-tuple-element.29), channel_id=1, source_target_pairs={{0,4},{4,0},{8,12},{12,8},{16,20},{20,16},{24,28},{28,24},{32,36},... | collective-permute-start | bytes 1572872 | tf_op jit(solution)/shard_map/ppermute | solution.py:301
  55.7 11.8 %collective-permute-start.10 = (bf16[2,2,2,3,64,128]{5,4,3,2,1,0:T(8,128)(2,1)S(1)}, bf16[2,2,2,3,64,128]{5,4,3,2,1,0:T(8,128)(2,1)S(1)}, u32[]{:S(2)}, u32[]{:S(2)}) collective-permute-start(bf16[2,2,2,3,64,128]{5,4,3,2,1,0:T(8,128)(2,1)S(1)} %get-tuple-element.25), channel_id=1, source_target_pairs={{0,1},{1,2},{2,3},{3,0},{4,5},{5,6},{6,7},{7,4},{8,9},{9,10},{10,1... | collective-permute-start | bytes 1179656 | tf_op jit(solution)/shard_map/ppermute | solution.py:293
  56.4 20.5 %collective-permute-start.11 = (bf16[2,2,2,3,64,128]{5,4,3,2,1,0:T(8,128)(2,1)S(1)}, bf16[2,2,2,3,64,128]{5,4,3,2,1,0:T(8,128)(2,1)S(1)}, u32[]{:S(2)}, u32[]{:S(2)}) collective-permute-start(bf16[2,2,2,3,64,128]{5,4,3,2,1,0:T(8,128)(2,1)S(1)} %get-tuple-element.26), channel_id=1, source_target_pairs={{0,2},{1,3},{2,0},{3,1},{4,6},{5,7},{6,4},{7,5},{8,10},{9,11},{10,... | collective-permute-start | bytes 1179656 | tf_op jit(solution)/shard_map/ppermute | solution.py:293
  59.3 17.6 %collective-permute-start.12 = (bf16[2,2,2,3,64,128]{5,4,3,2,1,0:T(8,128)(2,1)S(1)}, bf16[2,2,2,3,64,128]{5,4,3,2,1,0:T(8,128)(2,1)S(1)}, u32[]{:S(2)}, u32[]{:S(2)}) collective-permute-start(bf16[2,2,2,3,64,128]{5,4,3,2,1,0:T(8,128)(2,1)S(1)} %get-tuple-element.27), channel_id=1, source_target_pairs={{0,3},{1,0},{2,1},{3,2},{4,7},{5,4},{6,5},{7,6},{8,11},{9,8},{10,9... | collective-permute-start | bytes 1179656 | tf_op jit(solution)/shard_map/ppermute | solution.py:293
  59.5 24.9 %collective-permute-start.16 = (bf16[256,256]{1,0:T(8,128)(2,1)S(1)}, bf16[256,256]{1,0:T(8,128)(2,1)S(1)}, u32[]{:S(2)}, u32[]{:S(2)}) collective-permute-start(bf16[256,256]{1,0:T(8,128)(2,1)S(1)} %get-tuple-element.32), channel_id=1, source_target_pairs={{0,1},{1,2},{2,3},{3,0},{4,5},{5,6},{6,7},{7,4},{8,9},{9,10},{10,1... | collective-permute-start | bytes 393224 | tf_op jit(solution)/shard_map/ppermute | solution.py:293
  61.1 23.3 %collective-permute-start.18 = (bf16[256,256]{1,0:T(8,128)(2,1)S(1)}, bf16[256,256]{1,0:T(8,128)(2,1)S(1)}, u32[]{:S(2)}, u32[]{:S(2)}) collective-permute-start(bf16[256,256]{1,0:T(8,128)(2,1)S(1)} %get-tuple-element.33), channel_id=1, source_target_pairs={{0,3},{1,0},{2,1},{3,2},{4,7},{5,4},{6,5},{7,6},{8,11},{9,8},{10,9... | collective-permute-start | bytes 393224 | tf_op jit(solution)/shard_map/ppermute | solution.py:293
  67.5 16.9 %collective-permute-start.17 = (bf16[256,256]{1,0:T(8,128)(2,1)S(1)}, bf16[256,256]{1,0:T(8,128)(2,1)S(1)}, u32[]{:S(2)}, u32[]{:S(2)}) collective-permute-start(bf16[256,256]{1,0:T(8,128)(2,1)S(1)} %get-tuple-element.34), channel_id=1, source_target_pairs={{0,2},{1,3},{2,0},{3,1},{4,6},{5,7},{6,4},{7,5},{8,10},{9,11},{10,... | collective-permute-start | bytes 393224 | tf_op jit(solution)/shard_map/ppermute | solution.py:293
  77.2 21.5 %collective-permute-start.13 = (bf16[2,2,2,2,64,128]{5,4,2,1,0,3:T(8,128)(2,1)S(1)}, bf16[2,2,2,2,64,128]{5,4,2,1,0,3:T(8,128)(2,1)S(1)}, u32[]{:S(2)}, u32[]{:S(2)}) collective-permute-start(bf16[2,2,2,2,64,128]{5,4,2,1,0,3:T(8,128)(2,1)S(1)} %copy.25), channel_id=1, source_target_pairs={{0,4},{4,8},{8,12},{12,16},{16,20},{20,24},{24,28},{28,32},{32,36}... | collective-permute-start | bytes 786440 | tf_op jit(solution)/shard_map/ppermute | solution.py:289
  85.1 22.7 %all-to-all-start = ((bf16[32,8,256]{2,1,0:T(8,128)(2,1)}), bf16[32,8,256]{2,1,0:T(8,128)(2,1)S(1)}, u32[]{:S(2)}, u32[]{:S(2)}) async-start(bf16[32,8,256]{2,1,0:T(8,128)(2,1)} %fusion.16), calls=%async_computation | async-start | bytes 262144 | tf_op jit(solution)/shard_map/all_to_all | solution.py:327
  98.8 13.6 %collective-permute-start.14 = (bf16[2,2,64,256]{3,2,1,0:T(8,128)(2,1)S(1)}, bf16[2,2,64,256]{3,2,1,0:T(8,128)(2,1)S(1)}, u32[]{:S(2)}, u32[]{:S(2)}) collective-permute-start(bf16[2,2,64,256]{3,2,1,0:T(8,128)(2,1)S(1)} %fusion.15), channel_id=1, source_target_pairs={{0,32},{4,36},{8,40},{12,44},{16,48},{20,52},{24,56},{28,60},{32,6... | collective-permute-start | bytes 393224 | tf_op jit(solution)/shard_map/ppermute | solution.py:289
  108.5 13.0 %all-to-all-start.1 = ((bf16[32,8,256]{2,1,0:T(8,128)(2,1)}), bf16[32,8,256]{2,1,0:T(8,128)(2,1)S(1)}, u32[]{:S(2)}, u32[]{:S(2)}) async-start(bf16[32,8,256]{2,1,0:T(8,128)(2,1)} %broadcast_in_dim.38), calls=%async_computation.1 | async-start | bytes 262144 | tf_op jit(solution)/shard_map/all_to_all | solution.py:327
  121.6 4.6 %collective-permute-start.19 = (bf16[256,256]{1,0:T(8,128)(2,1)S(1)}, bf16[256,256]{1,0:T(8,128)(2,1)S(1)}, u32[]{:S(2)}, u32[]{:S(2)}) collective-permute-start(bf16[256,256]{1,0:T(8,128)(2,1)S(1)} %bitcast.63), channel_id=1, source_target_pairs={{0,4},{4,0},{8,12},{12,8},{16,20},{20,16},{24,28},{28,24},{32,36},... | collective-permute-start | bytes 393224 | tf_op jit(solution)/shard_map/ppermute | solution.py:301
  (3 other events, 33.3 us)

commit v2 on v0

--- a/solution.py
+++ b/solution.py
@@ -32,15 +32,15 @@
     hop = np.conj(table) @ (phase[:, None] * table)
     hop_real = hop.real.astype(bf16)
     hop_imag = hop.imag.astype(bf16)
-    return cosine, sine, hop_real, hop_imag
-
-
-def block_forms(cosine, sine, hop_real, hop_imag):
+    return cosine, sine, -sine, hop_real, hop_imag, -hop_imag
+
+
+def block_forms(cosine, sine, minus_sine, hop_real, hop_imag, minus_imag):
     return (
-        jnp.block([[cosine, sine], [-sine, cosine]]),
-        jnp.block([[cosine, -sine], [sine, cosine]]),
-        jnp.block([[hop_real, -hop_imag], [hop_imag, hop_real]]),
-        jnp.block([[hop_real, hop_imag], [-hop_imag, hop_real]]),
+        jnp.block([[cosine, sine], [minus_sine, cosine]]),
+        jnp.block([[cosine, minus_sine], [sine, cosine]]),
+        jnp.block([[hop_real, minus_imag], [hop_imag, hop_real]]),
+        jnp.block([[hop_real, hop_imag], [minus_imag, hop_real]]),
     )
 
 
@@ -129,12 +129,13 @@
     return lax.fori_loop(0, MODES // UNROLL, trip, 0)
 
 
-def propagate_kernel(meta, own, east, l0, l1, l2, l3, probe, near, far, left, right, arrived, window, patch, probes, rows, lanes):
+def propagate_kernel(meta, own, east, l0, l1, l2, l3, probe, near, far, left, right, arrived, patches, window, probes, rows, lanes):
     load_probes(probes, meta, probe, near, far)
     build_window(window, 0, meta, own, east, (l0, l1, l2, l3))
 
     def one_slot(turn, _):
         row, col, _ = corner_of(meta, turn)
+        patch = patches.at[turn]
         cut(window, patch, row, col)
 
         def one_mode(mode, lane_set):
@@ -199,15 +200,14 @@
     share_rows(total, (g0, g1, g2, g3), meta[2 * SLOTS + 1])
 
 
-def return_kernel(meta, own, east, l0, l1, l2, l3, arrived_grad, probe, near, far, left, right, g0, g1, g2, g3, kept, sent, window, patch, probes, lanes, first, total, probe_total):
+def return_kernel(meta, patches, arrived_grad, probe, near, far, left, right, g0, g1, g2, g3, kept, sent, probes, lanes, first, total, probe_total):
     load_probes(probes, meta, probe, near, far)
-    build_window(window, 0, meta, own, east, (l0, l1, l2, l3))
     total[...] = jnp.zeros_like(total)
     probe_total[...] = jnp.zeros_like(probe_total)
 
     def one_slot(turn, _):
         row, col, _ = corner_of(meta, turn)
-        cut(window, patch, row, col)
+        patch = patches.at[turn]
         first[...] = jnp.zeros_like(first)
 
         def one_mode(mode, lane_set):
@@ -257,10 +257,10 @@
 
 def kernels(meta, pieces, all_probes, turns, matrices):
     plus, minus, left, right = matrices
-    (arrived,) = kernel_call(
+    arrived, patches = kernel_call(
         propagate_kernel,
-        [((2, MODES, PW, 2 * PW), f32)],
-        [WINDOW, PATCH, PROBES, ROWS, LANES],
+        [((2, MODES, PW, 2 * PW), f32), ((2, 2, PW, PW), f32)],
+        [WINDOW, PROBES, ROWS, LANES],
         (meta, *pieces, *all_probes, left, right),
         TRANSFORM,
         16,
@@ -276,8 +276,8 @@
     *first_shares, kept, sent = kernel_call(
         return_kernel,
         SHARES + [((MODES, PW, PW), f32), ((MODES, PW, PW), bf16)],
-        [WINDOW, PATCH, PROBES, LANES, PATCH, WINDOW, ((2, MODES, PW, PW), f32)],
-        (meta, *pieces, arrived_grad, *all_probes, right, left),
+        [PROBES, LANES, PATCH, WINDOW, ((2, MODES, PW, PW), f32)],
+        (meta, patches, arrived_grad, *all_probes, right, left),
         TRANSFORM,
         20,
     )
@@ -335,17 +335,18 @@
     quarter = lax.dynamic_slice_in_dim(own, SHARE * mode, SHARE, 2)
     corner = toward(quarter, -TGX - 1)
     south = toward(quarter[..., HALF:], -TGX)
-    probe = probes[0].astype(bf16)
-    near = jnp.stack(fetch(lax.dynamic_index_in_dim(probe, core, 0, keepdims=False)))
+    near = fetch(lax.dynamic_index_in_dim(probes[0], core, 0, keepdims=False).astype(bf16))
+    near = jnp.stack(near)
     far = to_core(near)
     east = toward(own, -1)
     lower = jnp.concatenate([south, corner], axis=-1)
     quarters = [lower] + fetch(lower)
     pieces = (own, east, *quarters)
-    all_probes = (probe, near, far)
+    probe = probes[0].astype(bf16)
     matrices = block_forms(*lax.optimization_barrier(tuple(jnp.asarray(table) for table in constants())))
     meta = jnp.concatenate([offsets.reshape(-1), counts, jnp.stack([mode, core])]).astype(jnp.int32)
     turns = lax.dynamic_index_in_dim(measured[0].reshape(2, MODES, PW, PW), mode, 1, keepdims=False)
+    all_probes = (probe, near, far)
     second_shares, first_shares, kept, sent = kernels(meta, pieces, all_probes, turns, matrices)
     second = add_up(send_rows(second_shares))
     halves = kept + to_core(sent).astype(f32)
@@ -354,14 +355,14 @@
     part = jnp.sum(parts.astype(f32), axis=0).astype(bf16)
     first = add_up(send_rows(first_shares))
     rows = jnp.stack([first, second])
-    eastward = toward(rows[:, :, :, 1:].astype(bf16), 1).astype(f32)
-    joined = jnp.concatenate([eastward[:, :, :, 0], eastward[:, :, :, 1] + rows[:, :, :, 0]], axis=-1)
-    object_grad = joined[:, :, 0] + toward(joined[:, :, 1].astype(bf16), TGX).astype(f32)
+    upper = rows[:, :, 0] + toward(rows[:, :, 1].astype(bf16), TGX).astype(f32)
+    eastward = toward(upper[:, :, 1:].astype(bf16), 1).astype(f32)
+    object_grad = jnp.concatenate([eastward[:, :, 0], eastward[:, :, 1] + upper[:, :, 0]], axis=-1)
     plane = exchange(jnp.broadcast_to(part[None], (32, 8, PW))).reshape(PW, PW)
     other = to_core(plane)
-    real = jnp.where(core == 0, plane, other)
-    imag = jnp.where(core == 0, other, plane)
-    return (object_grad[None], jnp.stack([real, imag]).astype(f32)[None])
+    mine_first = (jnp.arange(2, dtype=jnp.int32) == core)[:, None, None]
+    probe_grad = jnp.where(mine_first, plane[None].astype(f32), other[None].astype(f32))
+    return (object_grad[None], probe_grad[None])
 
 
 def solution(mesh):

time: 131 us -> 140 us (1.069)
  waiting for transfers between devices: 37.6 us -> 44.4 us
  starting transfers between devices: 62.9 us -> 64.5 us
    all_to_all x2, waiting for transfers between devices: 11.2 us -> 18.5 us  [exchange(): return lax.all_to_all(value, 'tile', 0, 0, axis_index_groups=groups)]
    ppermute x5, waiting for transfers between devices: 7.5 us -> 3.75 us  [toward(): return lax.ppermute(value, 'tile', pairs)]
    ppermute x3, starting transfers between devices: 5.98 us -> 2.41 us  [to_core(): return lax.ppermute(value, 'tile', [(t, t ^ 1) for t in range(TILES)])]
    ppermute x5, starting transfers between devices: 20.1 us -> 23.5 us  [toward(): return lax.ppermute(value, 'tile', pairs)]
    concatenate x1 -> x2, other arithmetic: 0.18 us -> 2.56 us  [the longest x1 1.28 us: block_forms(): jnp.block([[hop_real, hop_imag], [minus_imag, hop_real]])]
    ppermute x15, waiting for transfers between devices: 18.6 us -> 20.9 us  [to_mode(): lax.ppermute(value, 'mode', [(m, (m + steps) % MODES) for m in range(MODE...]
    ppermute x15, starting transfers between devices: 18.8 us -> 21.1 us  [to_mode(): lax.ppermute(value, 'mode', [(m, (m + steps) % MODES) for m in range(MODE...]
    convert_element_type x2 -> x1, other arithmetic: 2.28 us -> 0.03 us  [one_step(): probe = probes[0].astype(bf16)]
  transfers between devices with their start and end apart: 25 -> 25, of which waited for: 9 -> 12; matrix products, arithmetic and copies ran while one was open for 5% -> 5% of each run, Pallas kernels for 0% -> 0%
where the time goes in v2:
time: 140 us; the launch traced here: 139 us
  starting transfers between devices  64.5 us (46%)
  waiting for transfers between devices  44.4 us (32%)
  Pallas kernels  19.3 us (14%)
  other arithmetic  5.62 us (4%)
  local copies, waits for them, and re-layouts  3.67 us (3%)
  between operations  1.64 us (1%)
    ppermute x5, starting transfers between devices, toward(): return lax.ppermute(value, 'tile', pairs)  23.5 us
    ppermute x15, starting transfers between devices, to_mode(): lax.ppermute(value, 'mode', [(m, (m + steps) % MODES) for m in range(MODE...  21.1 us
    ppermute x15, waiting for transfers between devices, to_mode(): lax.ppermute(value, 'mode', [(m, (m + steps) % MODES) for m in range(MODE...  20.9 us
    pallas_call x3, Pallas kernels, kernel_call(): pl.pallas_call(body, out_shape=tuple((jax.ShapeDtypeStruct(*shape) for sh...  19.3 us
    all_to_all x2, waiting for transfers between devices, exchange(): return lax.all_to_all(value, 'tile', 0, 0, axis_index_groups=groups)  18.5 us
    all_to_all x2, starting transfers between devices, exchange(): return lax.all_to_all(value, 'tile', 0, 0, axis_index_groups=groups)  17.5 us
    ppermute x5, waiting for transfers between devices, toward(): return lax.ppermute(value, 'tile', pairs)  3.75 us
  transfers between devices with their start and end apart: 25, of which 12 were waited for; matrix products, arithmetic and copies ran while one was open for 5% of the time, Pallas kernels for 0%

profile of v2, /device:TPU:1, one launch (start us, length us, event | category | flops | bytes accessed | tf_op | source)
XLA Modules:
  0.0 139.2 jit_solution(3106071904810869854)
XLA Ops:
  1.8 2.2 %collective-permute-start.8 = (bf16[256,256]{1,0:T(8,128)(2,1)S(1)}, bf16[256,256]{1,0:T(8,128)(2,1)S(1)}, u32[]{:S(2)}, u32[]{:S(2)}) collective-permute-start(bf16[256,256]{1,0:T(8,128)(2,1)S(1)} %fusion.13), channel_id=1, source_target_pairs={{0,1},{1,2},{2,3},{3,0},{4,5},{5,6},{6,7},{7,4},{8,9},{9,10},{10,1... | collective-permute-start | bytes 393224 | tf_op jit(solution)/shard_map/ppermute | solution.py:293
  4.0 2.6 %collective-permute-start.7 = (bf16[256,256]{1,0:T(8,128)(2,1)S(1)}, bf16[256,256]{1,0:T(8,128)(2,1)S(1)}, u32[]{:S(2)}, u32[]{:S(2)}) collective-permute-start(bf16[256,256]{1,0:T(8,128)(2,1)S(1)} %fusion.13), channel_id=1, source_target_pairs={{0,2},{1,3},{2,0},{3,1},{4,6},{5,7},{6,4},{7,5},{8,10},{9,11},{10,... | collective-permute-start | bytes 393224 | tf_op jit(solution)/shard_map/ppermute | solution.py:293
  15.4 3.4 %collective-permute-start = (bf16[2,2,256,256]{3,2,1,0:T(8,128)(2,1)}, bf16[2,2,256,256]{3,2,1,0:T(8,128)(2,1)S(1)}, u32[]{:S(2)}, u32[]{:S(2)}) collective-permute-start(bf16[2,2,256,256]{3,2,1,0:T(8,128)(2,1)} %bitcast.62), channel_id=1, source_target_pairs={{4,0},{8,4},{12,8},{16,12},{20,16},{24,20},{28,24},{32,28},{36,32}... | collective-permute-start | bytes 1572872 | tf_op jit(solution)/shard_map/ppermute | solution.py:289
  19.0 2.3 %collective-permute-done.1 = bf16[2,2,64,128]{3,2,1,0:T(8,128)(2,1)S(1)} collective-permute-done((bf16[2,2,64,128]{3,2,1,0:T(8,128)(2,1)S(1)}, bf16[2,2,64,128]{3,2,1,0:T(8,128)(2,1)S(1)}, u32[]{:S(2)}, u32[]{:S(2)}) %collective-permute-start.1) | collective-permute-done | bytes 65568 | tf_op jit(solution)/shard_map/ppermute | solution.py:289
  24.3 2.0 %collective-permute-start.3 = (bf16[2,2,64,384]{3,2,1,0:T(8,128)(2,1)S(1)}, bf16[2,2,64,384]{3,2,1,0:T(8,128)(2,1)S(1)}, u32[]{:S(2)}, u32[]{:S(2)}) collective-permute-start(bf16[2,2,64,384]{3,2,1,0:T(8,128)(2,1)S(1)} %constant_dynamic-update-slice_fusion.l0), channel_id=1, source_target_pairs={{0,3},{1,0},{2,1},{3,2},{4,7},{5,4},{6,5},{7,6},{8,11},{9,8},{10,9... | collective-permute-start | bytes 589832 | tf_op jit(solution)/shard_map/ppermute | solution.py:293
  26.3 8.3 %collective-permute-done.5.l3 = bf16[2,2,64,384]{3,2,1,0:T(8,128)(2,1)S(1)} collective-permute-done((bf16[2,2,64,384]{3,2,1,0:T(8,128)(2,1)S(1)}, bf16[2,2,64,384]{3,2,1,0:T(8,128)(2,1)S(1)}, u32[]{:S(2)}, u32[]{:S(2)}) %collective-permute-start.5) | collective-permute-done | bytes 196640 | tf_op jit(solution)/shard_map/ppermute | solution.py:293
  34.9 4.7 %shard_map.122 = (f32[2,4,256,512]{3,2,1,0:T(8,128)S(1)}, f32[2,2,256,256]{3,2,1,0:T(8,128)S(1)}) custom-call(s32[19]{0:T(128)S(1)} %pad_add_fusion.meta, bf16[2,2,256,256]{3,2,1,0:T(8,128)(2,1)S(1)} %bitcast.63, bf16[2,2,256,256]{3,2,1,0:T(8,128)(2,1)S(1)} %collective-permute-done.east, bf16[2,2,64,384]{3,2,1,0:T(8,128)(2,1)S(1)} %constant_dynamic-update-slice_fusion.l0, ...), custom_call_target="tpu_custom_call" | custom-call | flops 2147483648 | bytes 12582912 | tf_op jit(solution)/shard_map/pallas_call | solution.py:238
  39.6 8.8 %shard_map.123 = (bf16[2,4,512,256]{3,2,1,0:T(8,128)(2,1)S(1)}, bf16[2,2,3,64,128]{4,3,2,1,0:T(8,128)(2,1)S(1)}, bf16[2,2,3,64,128]{4,3,2,1,0:T(8,128)(2,1)S(1)}...) custom-call(s32[19]{0:T(128)S(1)} %pad_add_fusion.meta, bf16[2,2,256,256]{3,2,1,0:T(8,128)(2,1)S(1)} %bitcast.64, ...), custom_call_target="tpu_custom_call" | custom-call | flops 4294967296 | bytes 12582912 | tf_op jit(solution)/shard_map/pallas_call | solution.py:238
  48.5 5.8 %shard_map.124 = (bf16[2,2,3,64,128]{4,3,2,1,0:T(8,128)(2,1)S(1)}, bf16[2,2,3,64,128]{4,3,2,1,0:T(8,128)(2,1)S(1)}, bf16[2,2,3,64,128]{4,3,2,1,0:T(8,128)(2,1)S(...) custom-call(s32[19]{0:T(128)S(1)} %pad_add_fusion.meta, ...), custom_call_target="tpu_custom_call" | custom-call | flops 2147483648 | bytes 12582912 | tf_op jit(solution)/shard_map/pallas_call | solution.py:238
  54.3 1.5 %collective-permute-start.10 = (bf16[2,2,3,64,128]{4,3,2,1,0:T(8,128)(2,1)S(1)}, bf16[2,2,3,64,128]{4,3,2,1,0:T(8,128)(2,1)S(1)}, u32[]{:S(2)}, u32[]{:S(2)}) collective-permute-start(bf16[2,2,3,64,128]{4,3,2,1,0:T(8,128)(2,1)S(1)} %get-tuple-element.31), channel_id=1, source_target_pairs={{0,1},{1,2},{2,3},{3,0},{4,5},{5,6},{6,7},{7,4},{8,9},{9,10},{10,1... | collective-permute-start | bytes 589832 | tf_op jit(solution)/shard_map/ppermute | solution.py:293
  55.8 2.9 %collective-permute-start.11 = (bf16[2,2,3,64,128]{4,3,2,1,0:T(8,128)(2,1)S(1)}, bf16[2,2,3,64,128]{4,3,2,1,0:T(8,128)(2,1)S(1)}, u32[]{:S(2)}, u32[]{:S(2)}) collective-permute-start(bf16[2,2,3,64,128]{4,3,2,1,0:T(8,128)(2,1)S(1)} %get-tuple-element.32), channel_id=1, source_target_pairs={{0,2},{1,3},{2,0},{3,1},{4,6},{5,7},{6,4},{7,5},{8,10},{9,11},{10,... | collective-permute-start | bytes 589832 | tf_op jit(solution)/shard_map/ppermute | solution.py:293
  58.7 1.5 %collective-permute-start.13 = (bf16[2,2,3,64,128]{4,3,2,1,0:T(8,128)(2,1)S(1)}, bf16[2,2,3,64,128]{4,3,2,1,0:T(8,128)(2,1)S(1)}, u32[]{:S(2)}, u32[]{:S(2)}) collective-permute-start(bf16[2,2,3,64,128]{4,3,2,1,0:T(8,128)(2,1)S(1)} %get-tuple-element.35), channel_id=1, source_target_pairs={{0,1},{1,2},{2,3},{3,0},{4,5},{5,6},{6,7},{7,4},{8,9},{9,10},{10,1... | collective-permute-start | bytes 589832 | tf_op jit(solution)/shard_map/ppermute | solution.py:293
  60.2 1.5 %collective-permute-done.10 = bf16[2,2,3,64,128]{4,3,2,1,0:T(8,128)(2,1)S(1)} collective-permute-done((bf16[2,2,3,64,128]{4,3,2,1,0:T(8,128)(2,1)S(1)}, bf16[2,2,3,64,128]{4,3,2,1,0:T(8,128)(2,1)S(1)}, u32[]{:S(2)}, u32[]{:S(2)}) %collective-permute-start.10) | collective-permute-done | bytes 196640 | tf_op jit(solution)/shard_map/ppermute | solution.py:293
  61.7 1.7 %collective-permute-start.15 = (bf16[2,2,3,64,128]{4,3,2,1,0:T(8,128)(2,1)S(1)}, bf16[2,2,3,64,128]{4,3,2,1,0:T(8,128)(2,1)S(1)}, u32[]{:S(2)}, u32[]{:S(2)}) collective-permute-start(bf16[2,2,3,64,128]{4,3,2,1,0:T(8,128)(2,1)S(1)} %get-tuple-element.37), channel_id=1, source_target_pairs={{0,3},{1,0},{2,1},{3,2},{4,7},{5,4},{6,5},{7,6},{8,11},{9,8},{10,9... | collective-permute-start | bytes 589832 | tf_op jit(solution)/shard_map/ppermute | solution.py:293
  63.5 4.0 %collective-permute-done.11 = bf16[2,2,3,64,128]{4,3,2,1,0:T(8,128)(2,1)S(1)} collective-permute-done((bf16[2,2,3,64,128]{4,3,2,1,0:T(8,128)(2,1)S(1)}, bf16[2,2,3,64,128]{4,3,2,1,0:T(8,128)(2,1)S(1)}, u32[]{:S(2)}, u32[]{:S(2)}) %collective-permute-start.11) | collective-permute-done | bytes 196640 | tf_op jit(solution)/shard_map/ppermute | solution.py:293
  67.4 2.3 %collective-permute-start.18 = (bf16[4,256,256]{2,1,0:T(8,128)(2,1)S(1)}, bf16[4,256,256]{2,1,0:T(8,128)(2,1)S(1)}, u32[]{:S(2)}, u32[]{:S(2)}) collective-permute-start(bf16[4,256,256]{2,1,0:T(8,128)(2,1)S(1)} %get-tuple-element.39), channel_id=1, source_target_pairs={{0,4},{4,0},{8,12},{12,8},{16,20},{20,16},{24,28},{28,24},{32,36},... | collective-permute-start | bytes 1572872 | tf_op jit(solution)/shard_map/ppermute | solution.py:301
  70.6 5.2 %collective-permute-done.14 = bf16[2,2,3,64,128]{4,3,2,1,0:T(8,128)(2,1)S(1)} collective-permute-done((bf16[2,2,3,64,128]{4,3,2,1,0:T(8,128)(2,1)S(1)}, bf16[2,2,3,64,128]{4,3,2,1,0:T(8,128)(2,1)S(1)}, u32[]{:S(2)}, u32[]{:S(2)}) %collective-permute-start.14) | collective-permute-done | bytes 196640 | tf_op jit(solution)/shard_map/ppermute | solution.py:293
  76.0 13.2 %collective-permute-start.16 = (bf16[2,2,3,64,128]{4,3,2,1,0:T(8,128)(2,1)S(1)}, bf16[2,2,3,64,128]{4,3,2,1,0:T(8,128)(2,1)S(1)}, u32[]{:S(2)}, u32[]{:S(2)}) collective-permute-start(bf16[2,2,3,64,128]{4,3,2,1,0:T(8,128)(2,1)S(1)} %fusion.12), channel_id=1, source_target_pairs={{0,32},{4,36},{8,40},{12,44},{16,48},{20,52},{24,56},{28,60},{32,6... | collective-permute-start | bytes 589832 | tf_op jit(solution)/shard_map/ppermute | solution.py:289
  90.3 2.1 %collective-permute-start.21 = (bf16[256,256]{1,0:T(8,128)(2,1)S(1)}, bf16[256,256]{1,0:T(8,128)(2,1)S(1)}, u32[]{:S(2)}, u32[]{:S(2)}) collective-permute-start(bf16[256,256]{1,0:T(8,128)(2,1)S(1)} %get-tuple-element.43), channel_id=1, source_target_pairs={{0,3},{1,0},{2,1},{3,2},{4,7},{5,4},{6,5},{7,6},{8,11},{9,8},{10,9... | collective-permute-start | bytes 393224 | tf_op jit(solution)/shard_map/ppermute | solution.py:293
  93.6 4.3 %collective-permute-start.17 = (bf16[2,2,2,64,128]{4,3,1,0,2:T(8,128)(2,1)S(1)}, bf16[2,2,2,64,128]{4,3,1,0,2:T(8,128)(2,1)S(1)}, u32[]{:S(2)}, u32[]{:S(2)}) collective-permute-start(bf16[2,2,2,64,128]{4,3,1,0,2:T(8,128)(2,1)S(1)} %copy.27), channel_id=1, source_target_pairs={{0,4},{4,8},{8,12},{12,16},{16,20},{20,24},{24,28},{28,32},{32,36}... | collective-permute-start | bytes 393224 | tf_op jit(solution)/shard_map/ppermute | solution.py:289
  99.4 13.6 %all-to-all-start = ((bf16[32,8,256]{2,1,0:T(8,128)(2,1)}), bf16[32,8,256]{2,1,0:T(8,128)(2,1)S(1)}, u32[]{:S(2)}, u32[]{:S(2)}) async-start(bf16[32,8,256]{2,1,0:T(8,128)(2,1)} %fusion.14), calls=%async_computation | async-start | bytes 262144 | tf_op jit(solution)/shard_map/all_to_all | solution.py:327
  113.1 9.1 %all-to-all-done = bf16[32,8,256]{2,1,0:T(8,128)(2,1)S(1)} async-done(((bf16[32,8,256]{2,1,0:T(8,128)(2,1)}), bf16[32,8,256]{2,1,0:T(8,128)(2,1)S(1)}, u32[]{:S(2)}, u32[]{:S(2)}) %all-to-all-start) | async-done | bytes 131104 | tf_op jit(solution)/shard_map/all_to_all | solution.py:327
  122.9 3.9 %all-to-all-start.1 = ((bf16[32,8,256]{2,1,0:T(8,128)(2,1)}), bf16[32,8,256]{2,1,0:T(8,128)(2,1)S(1)}, u32[]{:S(2)}, u32[]{:S(2)}) async-start(bf16[32,8,256]{2,1,0:T(8,128)(2,1)} %broadcast_in_dim.38), calls=%async_computation.1 | async-start | bytes 262144 | tf_op jit(solution)/shard_map/all_to_all | solution.py:327
  127.5 9.3 %all-to-all-done.1 = bf16[32,8,256]{2,1,0:T(8,128)(2,1)S(1)} async-done(((bf16[32,8,256]{2,1,0:T(8,128)(2,1)}), bf16[32,8,256]{2,1,0:T(8,128)(2,1)S(1)}, u32[]{:S(2)}, u32[]{:S(2)}) %all-to-all-start.1) | async-done | bytes 131104 | tf_op jit(solution)/shard_map/all_to_all | solution.py:327
  (67 shorter events, 21.2 us)
Async XLA Ops:
  1.8 13.6 %collective-permute-start.8 = (bf16[256,256]{1,0:T(8,128)(2,1)S(1)}, bf16[256,256]{1,0:T(8,128)(2,1)S(1)}, u32[]{:S(2)}, u32[]{:S(2)}) collective-permute-start(bf16[256,256]{1,0:T(8,128)(2,1)S(1)} %fusion.13), channel_id=1, source_target_pairs={{0,1},{1,2},{2,3},{3,0},{4,5},{5,6},{6,7},{7,4},{8,9},{9,10},{10,1... | collective-permute-start | bytes 393224 | tf_op jit(solution)/shard_map/ppermute | solution.py:293
  4.0 14.8 %collective-permute-start.7 = (bf16[256,256]{1,0:T(8,128)(2,1)S(1)}, bf16[256,256]{1,0:T(8,128)(2,1)S(1)}, u32[]{:S(2)}, u32[]{:S(2)}) collective-permute-start(bf16[256,256]{1,0:T(8,128)(2,1)S(1)} %fusion.13), channel_id=1, source_target_pairs={{0,2},{1,3},{2,0},{3,1},{4,6},{5,7},{6,4},{7,5},{8,10},{9,11},{10,... | collective-permute-start | bytes 393224 | tf_op jit(solution)/shard_map/ppermute | solution.py:293
  6.6 12.2 %collective-permute-start.6 = (bf16[256,256]{1,0:T(8,128)(2,1)S(1)}, bf16[256,256]{1,0:T(8,128)(2,1)S(1)}, u32[]{:S(2)}, u32[]{:S(2)}) collective-permute-start(bf16[256,256]{1,0:T(8,128)(2,1)S(1)} %fusion.13), channel_id=1, source_target_pairs={{0,3},{1,0},{2,1},{3,2},{4,7},{5,4},{6,5},{7,6},{8,11},{9,8},{10,9... | collective-permute-start | bytes 393224 | tf_op jit(solution)/shard_map/ppermute | solution.py:293
  8.6 14.2 %collective-permute-start.2 = (bf16[2,2,64,256]{3,2,1,0:T(8,128)(2,1)S(1)}, bf16[2,2,64,256]{3,2,1,0:T(8,128)(2,1)S(1)}, u32[]{:S(2)}, u32[]{:S(2)}) collective-permute-start(bf16[2,2,64,256]{3,2,1,0:T(8,128)(2,1)S(1)} %dynamic-slice_bitcast_fusion.1), channel_id=1, source_target_pairs={{36,0},{40,4},{44,8},{48,12},{52,16},{56,20},{60,24},{64,28},{68,3... | collective-permute-start | bytes 393224 | tf_op jit(solution)/shard_map/ppermute | solution.py:289
  9.9 11.4 %collective-permute-start.1 = (bf16[2,2,64,128]{3,2,1,0:T(8,128)(2,1)S(1)}, bf16[2,2,64,128]{3,2,1,0:T(8,128)(2,1)S(1)}, u32[]{:S(2)}, u32[]{:S(2)}) collective-permute-start(bf16[2,2,64,128]{3,2,1,0:T(8,128)(2,1)S(1)} %slice.49), channel_id=1, source_target_pairs={{32,0},{36,4},{40,8},{44,12},{48,16},{52,20},{56,24},{60,28},{64,3... | collective-permute-start | bytes 196616 | tf_op jit(solution)/shard_map/ppermute | solution.py:289
  15.4 19.5 %collective-permute-start = (bf16[2,2,256,256]{3,2,1,0:T(8,128)(2,1)}, bf16[2,2,256,256]{3,2,1,0:T(8,128)(2,1)S(1)}, u32[]{:S(2)}, u32[]{:S(2)}) collective-permute-start(bf16[2,2,256,256]{3,2,1,0:T(8,128)(2,1)} %bitcast.62), channel_id=1, source_target_pairs={{4,0},{8,4},{12,8},{16,12},{20,16},{24,20},{28,24},{32,28},{36,32}... | collective-permute-start | bytes 1572872 | tf_op jit(solution)/shard_map/ppermute | solution.py:289
  18.9 16.0 %collective-permute-start.9 = (bf16[3,256,256]{2,1,0:T(8,128)(2,1)S(1)}, bf16[3,256,256]{2,1,0:T(8,128)(2,1)S(1)}, u32[]{:S(2)}, u32[]{:S(2)}) collective-permute-start(bf16[3,256,256]{2,1,0:T(8,128)(2,1)S(1)} %pad_maximum_fusion.9.near), channel_id=1, source_target_pairs={{0,4},{4,0},{8,12},{12,8},{16,20},{20,16},{24,28},{28,24},{32,36},... | collective-permute-start | bytes 1179656 | tf_op jit(solution)/shard_map/ppermute | solution.py:301
  22.8 11.8 %collective-permute-start.5 = (bf16[2,2,64,384]{3,2,1,0:T(8,128)(2,1)S(1)}, bf16[2,2,64,384]{3,2,1,0:T(8,128)(2,1)S(1)}, u32[]{:S(2)}, u32[]{:S(2)}) collective-permute-start(bf16[2,2,64,384]{3,2,1,0:T(8,128)(2,1)S(1)} %constant_dynamic-update-slice_fusion.l0), channel_id=1, source_target_pairs={{0,1},{1,2},{2,3},{3,0},{4,5},{5,6},{6,7},{7,4},{8,9},{9,10},{10,1... | collective-permute-start | bytes 589832 | tf_op jit(solution)/shard_map/ppermute | solution.py:293
  23.3 11.3 %collective-permute-start.4 = (bf16[2,2,64,384]{3,2,1,0:T(8,128)(2,1)S(1)}, bf16[2,2,64,384]{3,2,1,0:T(8,128)(2,1)S(1)}, u32[]{:S(2)}, u32[]{:S(2)}) collective-permute-start(bf16[2,2,64,384]{3,2,1,0:T(8,128)(2,1)S(1)} %constant_dynamic-update-slice_fusion.l0), channel_id=1, source_target_pairs={{0,2},{1,3},{2,0},{3,1},{4,6},{5,7},{6,4},{7,5},{8,10},{9,11},{10,... | collective-permute-start | bytes 589832 | tf_op jit(solution)/shard_map/ppermute | solution.py:293
  24.3 10.6 %collective-permute-start.3 = (bf16[2,2,64,384]{3,2,1,0:T(8,128)(2,1)S(1)}, bf16[2,2,64,384]{3,2,1,0:T(8,128)(2,1)S(1)}, u32[]{:S(2)}, u32[]{:S(2)}) collective-permute-start(bf16[2,2,64,384]{3,2,1,0:T(8,128)(2,1)S(1)} %constant_dynamic-update-slice_fusion.l0), channel_id=1, source_target_pairs={{0,3},{1,0},{2,1},{3,2},{4,7},{5,4},{6,5},{7,6},{8,11},{9,8},{10,9... | collective-permute-start | bytes 589832 | tf_op jit(solution)/shard_map/ppermute | solution.py:293
  54.3 7.5 %collective-permute-start.10 = (bf16[2,2,3,64,128]{4,3,2,1,0:T(8,128)(2,1)S(1)}, bf16[2,2,3,64,128]{4,3,2,1,0:T(8,128)(2,1)S(1)}, u32[]{:S(2)}, u32[]{:S(2)}) collective-permute-start(bf16[2,2,3,64,128]{4,3,2,1,0:T(8,128)(2,1)S(1)} %get-tuple-element.31), channel_id=1, source_target_pairs={{0,1},{1,2},{2,3},{3,0},{4,5},{5,6},{6,7},{7,4},{8,9},{9,10},{10,1... | collective-permute-start | bytes 589832 | tf_op jit(solution)/shard_map/ppermute | solution.py:293
  55.8 11.6 %collective-permute-start.11 = (bf16[2,2,3,64,128]{4,3,2,1,0:T(8,128)(2,1)S(1)}, bf16[2,2,3,64,128]{4,3,2,1,0:T(8,128)(2,1)S(1)}, u32[]{:S(2)}, u32[]{:S(2)}) collective-permute-start(bf16[2,2,3,64,128]{4,3,2,1,0:T(8,128)(2,1)S(1)} %get-tuple-element.32), channel_id=1, source_target_pairs={{0,2},{1,3},{2,0},{3,1},{4,6},{5,7},{6,4},{7,5},{8,10},{9,11},{10,... | collective-permute-start | bytes 589832 | tf_op jit(solution)/shard_map/ppermute | solution.py:293
  58.7 11.1 %collective-permute-start.12 = (bf16[2,2,3,64,128]{4,3,2,1,0:T(8,128)(2,1)S(1)}, bf16[2,2,3,64,128]{4,3,2,1,0:T(8,128)(2,1)S(1)}, u32[]{:S(2)}, u32[]{:S(2)}) collective-permute-start(bf16[2,2,3,64,128]{4,3,2,1,0:T(8,128)(2,1)S(1)} %get-tuple-element.33), channel_id=1, source_target_pairs={{0,3},{1,0},{2,1},{3,2},{4,7},{5,4},{6,5},{7,6},{8,11},{9,8},{10,9... | collective-permute-start | bytes 589832 | tf_op jit(solution)/shard_map/ppermute | solution.py:293
  58.7 11.9 %collective-permute-start.13 = (bf16[2,2,3,64,128]{4,3,2,1,0:T(8,128)(2,1)S(1)}, bf16[2,2,3,64,128]{4,3,2,1,0:T(8,128)(2,1)S(1)}, u32[]{:S(2)}, u32[]{:S(2)}) collective-permute-start(bf16[2,2,3,64,128]{4,3,2,1,0:T(8,128)(2,1)S(1)} %get-tuple-element.35), channel_id=1, source_target_pairs={{0,1},{1,2},{2,3},{3,0},{4,5},{5,6},{6,7},{7,4},{8,9},{9,10},{10,1... | collective-permute-start | bytes 589832 | tf_op jit(solution)/shard_map/ppermute | solution.py:293
  60.2 15.7 %collective-permute-start.14 = (bf16[2,2,3,64,128]{4,3,2,1,0:T(8,128)(2,1)S(1)}, bf16[2,2,3,64,128]{4,3,2,1,0:T(8,128)(2,1)S(1)}, u32[]{:S(2)}, u32[]{:S(2)}) collective-permute-start(bf16[2,2,3,64,128]{4,3,2,1,0:T(8,128)(2,1)S(1)} %get-tuple-element.36), channel_id=1, source_target_pairs={{0,2},{1,3},{2,0},{3,1},{4,6},{5,7},{6,4},{7,5},{8,10},{9,11},{10,... | collective-permute-start | bytes 589832 | tf_op jit(solution)/shard_map/ppermute | solution.py:293
  61.7 14.2 %collective-permute-start.15 = (bf16[2,2,3,64,128]{4,3,2,1,0:T(8,128)(2,1)S(1)}, bf16[2,2,3,64,128]{4,3,2,1,0:T(8,128)(2,1)S(1)}, u32[]{:S(2)}, u32[]{:S(2)}) collective-permute-start(bf16[2,2,3,64,128]{4,3,2,1,0:T(8,128)(2,1)S(1)} %get-tuple-element.37), channel_id=1, source_target_pairs={{0,3},{1,0},{2,1},{3,2},{4,7},{5,4},{6,5},{7,6},{8,11},{9,8},{10,9... | collective-permute-start | bytes 589832 | tf_op jit(solution)/shard_map/ppermute | solution.py:293
  67.4 21.8 %collective-permute-start.18 = (bf16[4,256,256]{2,1,0:T(8,128)(2,1)S(1)}, bf16[4,256,256]{2,1,0:T(8,128)(2,1)S(1)}, u32[]{:S(2)}, u32[]{:S(2)}) collective-permute-start(bf16[4,256,256]{2,1,0:T(8,128)(2,1)S(1)} %get-tuple-element.39), channel_id=1, source_target_pairs={{0,4},{4,0},{8,12},{12,8},{16,20},{20,16},{24,28},{28,24},{32,36},... | collective-permute-start | bytes 1572872 | tf_op jit(solution)/shard_map/ppermute | solution.py:301
  76.0 17.5 %collective-permute-start.16 = (bf16[2,2,3,64,128]{4,3,2,1,0:T(8,128)(2,1)S(1)}, bf16[2,2,3,64,128]{4,3,2,1,0:T(8,128)(2,1)S(1)}, u32[]{:S(2)}, u32[]{:S(2)}) collective-permute-start(bf16[2,2,3,64,128]{4,3,2,1,0:T(8,128)(2,1)S(1)} %fusion.12), channel_id=1, source_target_pairs={{0,32},{4,36},{8,40},{12,44},{16,48},{20,52},{24,56},{28,60},{32,6... | collective-permute-start | bytes 589832 | tf_op jit(solution)/shard_map/ppermute | solution.py:289
  89.5 8.4 %collective-permute-start.19 = (bf16[256,256]{1,0:T(8,128)(2,1)S(1)}, bf16[256,256]{1,0:T(8,128)(2,1)S(1)}, u32[]{:S(2)}, u32[]{:S(2)}) collective-permute-start(bf16[256,256]{1,0:T(8,128)(2,1)S(1)} %get-tuple-element.42), channel_id=1, source_target_pairs={{0,1},{1,2},{2,3},{3,0},{4,5},{5,6},{6,7},{7,4},{8,9},{9,10},{10,1... | collective-permute-start | bytes 393224 | tf_op jit(solution)/shard_map/ppermute | solution.py:293
  90.3 7.6 %collective-permute-start.21 = (bf16[256,256]{1,0:T(8,128)(2,1)S(1)}, bf16[256,256]{1,0:T(8,128)(2,1)S(1)}, u32[]{:S(2)}, u32[]{:S(2)}) collective-permute-start(bf16[256,256]{1,0:T(8,128)(2,1)S(1)} %get-tuple-element.43), channel_id=1, source_target_pairs={{0,3},{1,0},{2,1},{3,2},{4,7},{5,4},{6,5},{7,6},{8,11},{9,8},{10,9... | collective-permute-start | bytes 393224 | tf_op jit(solution)/shard_map/ppermute | solution.py:293
  92.4 6.3 %collective-permute-start.20 = (bf16[256,256]{1,0:T(8,128)(2,1)S(1)}, bf16[256,256]{1,0:T(8,128)(2,1)S(1)}, u32[]{:S(2)}, u32[]{:S(2)}) collective-permute-start(bf16[256,256]{1,0:T(8,128)(2,1)S(1)} %get-tuple-element.44), channel_id=1, source_target_pairs={{0,2},{1,3},{2,0},{3,1},{4,6},{5,7},{6,4},{7,5},{8,10},{9,11},{10,... | collective-permute-start | bytes 393224 | tf_op jit(solution)/shard_map/ppermute | solution.py:293
  93.6 19.4 %collective-permute-start.17 = (bf16[2,2,2,64,128]{4,3,1,0,2:T(8,128)(2,1)S(1)}, bf16[2,2,2,64,128]{4,3,1,0,2:T(8,128)(2,1)S(1)}, u32[]{:S(2)}, u32[]{:S(2)}) collective-permute-start(bf16[2,2,2,64,128]{4,3,1,0,2:T(8,128)(2,1)S(1)} %copy.27), channel_id=1, source_target_pairs={{0,4},{4,8},{8,12},{12,16},{16,20},{20,24},{24,28},{28,32},{32,36}... | collective-permute-start | bytes 393224 | tf_op jit(solution)/shard_map/ppermute | solution.py:289
  99.4 22.9 %all-to-all-start = ((bf16[32,8,256]{2,1,0:T(8,128)(2,1)}), bf16[32,8,256]{2,1,0:T(8,128)(2,1)S(1)}, u32[]{:S(2)}, u32[]{:S(2)}) async-start(bf16[32,8,256]{2,1,0:T(8,128)(2,1)} %fusion.14), calls=%async_computation | async-start | bytes 262144 | tf_op jit(solution)/shard_map/all_to_all | solution.py:327
  122.9 13.9 %all-to-all-start.1 = ((bf16[32,8,256]{2,1,0:T(8,128)(2,1)}), bf16[32,8,256]{2,1,0:T(8,128)(2,1)S(1)}, u32[]{:S(2)}, u32[]{:S(2)}) async-start(bf16[32,8,256]{2,1,0:T(8,128)(2,1)} %broadcast_in_dim.38), calls=%async_computation.1 | async-start | bytes 262144 | tf_op jit(solution)/shard_map/all_to_all | solution.py:327
  (4 other events, 73.3 us)

commit v3 on v2

--- a/solution.py
+++ b/solution.py
@@ -53,7 +53,7 @@
         window[part, 0, 0:PW] = own[depth, part, :, HALF:].astype(f32)
         for lane_tile in range(2):
             lanes = slice(HALF * lane_tile, HALF * lane_tile + HALF)
-            window[part, 1 + lane_tile, 0:PW] = east[depth, part, :, lanes].astype(f32)
+            window[part, 1 + lane_tile, 0:PW] = east[part, :, lanes].astype(f32)
         for step in range(MODES):
             owner = lax.rem(meta[2 * SLOTS + 1] + step, MODES)
             rows = pl.ds(pl.multiple_of(PW + SHARE * owner, SHARE), SHARE)
@@ -147,7 +147,7 @@
 
         return each_mode(one_mode)
 
-    lax.fori_loop(0, 2, one_slot, 0)
+    lax.fori_loop(0, 2, one_slot, 0, unroll=True)
 
 
 def detector_kernel(meta, own, east, l0, l1, l2, l3, arrived, measured, plus, minus, arrived_grad, g0, g1, g2, g3, window, patch, rows, lanes, far, weight, second, total):
@@ -225,7 +225,7 @@
         place(total, first, row, col)
         return 0
 
-    lax.fori_loop(0, 2, one_slot, 0)
+    lax.fori_loop(0, 2, one_slot, 0, unroll=True)
     share_rows(total, (g0, g1, g2, g3), meta[2 * SLOTS + 1])
     core = meta[2 * SLOTS + 2]
     kept[...] = probe_total[core]
@@ -257,11 +257,12 @@
 
 def kernels(meta, pieces, all_probes, turns, matrices):
     plus, minus, left, right = matrices
+    own, east_one, east_two, *quarters = pieces
     arrived, patches = kernel_call(
         propagate_kernel,
         [((2, MODES, PW, 2 * PW), f32), ((2, 2, PW, PW), f32)],
         [WINDOW, PROBES, ROWS, LANES],
-        (meta, *pieces, *all_probes, left, right),
+        (meta, own, east_one, *quarters, *all_probes, left, right),
         TRANSFORM,
         16,
     )
@@ -269,7 +270,7 @@
         detector_kernel,
         [((2, MODES, 2 * PW, PW), bf16)] + SHARES,
         [WINDOW, PATCH, ROWS, LANES, ((MODES, PW, 2 * PW), f32), ((PW, PW), f32), PATCH, WINDOW],
-        (meta, *pieces, arrived, turns, plus, minus),
+        (meta, own, east_two, *quarters, arrived, turns, plus, minus),
         2 * TRANSFORM,
         26,
     )
@@ -338,10 +339,11 @@
     near = fetch(lax.dynamic_index_in_dim(probes[0], core, 0, keepdims=False).astype(bf16))
     near = jnp.stack(near)
     far = to_core(near)
-    east = toward(own, -1)
+    east_one = toward(own[0], -1)
+    east_two = toward(own[1], -1)
     lower = jnp.concatenate([south, corner], axis=-1)
     quarters = [lower] + fetch(lower)
-    pieces = (own, east, *quarters)
+    pieces = (own, east_one, east_two, *quarters)
     probe = probes[0].astype(bf16)
     matrices = block_forms(*lax.optimization_barrier(tuple(jnp.asarray(table) for table in constants())))
     meta = jnp.concatenate([offsets.reshape(-1), counts, jnp.stack([mode, core])]).astype(jnp.int32)

time: 140 us -> 140 us (level)
  waiting for transfers between devices: 44.4 us -> 38.6 us
  starting transfers between devices: 64.5 us -> 69.9 us
  Pallas kernels: 19.3 us -> 17.8 us
    ppermute x15, waiting for transfers between devices: 20.9 us -> 17.2 us  [to_mode(): lax.ppermute(value, 'mode', [(m, (m + steps) % MODES) for m in range(MODE...]
    ppermute x5 -> x6, starting transfers between devices: 23.5 us -> 27 us  [toward(): return lax.ppermute(value, 'tile', pairs)]
    all_to_all x2, starting transfers between devices: 17.5 us -> 19.5 us  [exchange(): return lax.all_to_all(value, 'tile', 0, 0, axis_index_groups=groups)]
    ppermute x5 -> x6, waiting for transfers between devices: 3.75 us -> 1.88 us  [toward(): return lax.ppermute(value, 'tile', pairs)]
    pallas_call x3, Pallas kernels: 19.3 us -> 17.8 us  [kernel_call(): pl.pallas_call(body, out_shape=tuple((jax.ShapeDtypeStruct(*shape) for sh...]
  transfers between devices with their start and end apart: 25 -> 26, of which waited for: 12 -> 13; matrix products, arithmetic and copies ran while one was open for 5% -> 6% of each run, Pallas kernels for 0% -> 3%
where the time goes in v3:
time: 140 us; the launch traced here: 139 us
  starting transfers between devices  69.9 us (50%)
  waiting for transfers between devices  38.6 us (28%)
  Pallas kernels  17.8 us (13%)
  other arithmetic  6.66 us (5%)
  local copies, waits for them, and re-layouts  4.7 us (3%)
  between operations  1.64 us (1%)
    ppermute x6, starting transfers between devices, toward(): return lax.ppermute(value, 'tile', pairs)  27 us
    ppermute x15, starting transfers between devices, to_mode(): lax.ppermute(value, 'mode', [(m, (m + steps) % MODES) for m in range(MODE...  21 us
    all_to_all x2, starting transfers between devices, exchange(): return lax.all_to_all(value, 'tile', 0, 0, axis_index_groups=groups)  19.5 us
    all_to_all x2, waiting for transfers between devices, exchange(): return lax.all_to_all(value, 'tile', 0, 0, axis_index_groups=groups)  18.2 us
    pallas_call x3, Pallas kernels, kernel_call(): pl.pallas_call(body, out_shape=tuple((jax.ShapeDtypeStruct(*shape) for sh...  17.8 us
    ppermute x15, waiting for transfers between devices, to_mode(): lax.ppermute(value, 'mode', [(m, (m + steps) % MODES) for m in range(MODE...  17.2 us
  transfers between devices with their start and end apart: 26, of which 13 were waited for; matrix products, arithmetic and copies ran while one was open for 6% of the time, Pallas kernels for 3%

profile of v3, /device:TPU:1, one launch (start us, length us, event | category | flops | bytes accessed | tf_op | source)
XLA Modules:
  0.0 139.3 jit_solution(5813834270377883427)
XLA Ops:
  1.8 2.2 %collective-permute-start.8 = (bf16[256,256]{1,0:T(8,128)(2,1)S(1)}, bf16[256,256]{1,0:T(8,128)(2,1)S(1)}, u32[]{:S(2)}, u32[]{:S(2)}) collective-permute-start(bf16[256,256]{1,0:T(8,128)(2,1)S(1)} %fusion.13), channel_id=1, source_target_pairs={{0,1},{1,2},{2,3},{3,0},{4,5},{5,6},{6,7},{7,4},{8,9},{9,10},{10,1... | collective-permute-start | bytes 393224 | tf_op jit(solution)/shard_map/ppermute | solution.py:294
  3.9 2.6 %collective-permute-start.7 = (bf16[256,256]{1,0:T(8,128)(2,1)S(1)}, bf16[256,256]{1,0:T(8,128)(2,1)S(1)}, u32[]{:S(2)}, u32[]{:S(2)}) collective-permute-start(bf16[256,256]{1,0:T(8,128)(2,1)S(1)} %fusion.13), channel_id=1, source_target_pairs={{0,2},{1,3},{2,0},{3,1},{4,6},{5,7},{6,4},{7,5},{8,10},{9,11},{10,... | collective-permute-start | bytes 393224 | tf_op jit(solution)/shard_map/ppermute | solution.py:294
  17.4 3.4 %collective-permute-start = (bf16[2,256,256]{2,1,0:T(8,128)(2,1)S(1)}, bf16[2,256,256]{2,1,0:T(8,128)(2,1)S(1)}, u32[]{:S(2)}, u32[]{:S(2)}) collective-permute-start(bf16[2,256,256]{2,1,0:T(8,128)(2,1)S(1)} %get-tuple-element.46), channel_id=1, source_target_pairs={{4,0},{8,4},{12,8},{16,12},{20,16},{24,20},{28,24},{32,28},{36,32}... | collective-permute-start | bytes 786440 | tf_op jit(solution)/shard_map/ppermute | solution.py:290
  24.2 2.0 %collective-permute-start.3 = (bf16[2,2,64,384]{3,2,1,0:T(8,128)(2,1)S(1)}, bf16[2,2,64,384]{3,2,1,0:T(8,128)(2,1)S(1)}, u32[]{:S(2)}, u32[]{:S(2)}) collective-permute-start(bf16[2,2,64,384]{3,2,1,0:T(8,128)(2,1)S(1)} %constant_dynamic-update-slice_fusion.l0), channel_id=1, source_target_pairs={{0,3},{1,0},{2,1},{3,2},{4,7},{5,4},{6,5},{7,6},{8,11},{9,8},{10,9... | collective-permute-start | bytes 589832 | tf_op jit(solution)/shard_map/ppermute | solution.py:294
  26.4 2.8 %collective-permute-start.10 = (bf16[2,256,256]{2,1,0:T(8,128)(2,1)S(1)}, bf16[2,256,256]{2,1,0:T(8,128)(2,1)S(1)}, u32[]{:S(2)}, u32[]{:S(2)}) collective-permute-start(bf16[2,256,256]{2,1,0:T(8,128)(2,1)S(1)} %get-tuple-element.45), channel_id=1, source_target_pairs={{4,0},{8,4},{12,8},{16,12},{20,16},{24,20},{28,24},{32,28},{36,32}... | collective-permute-start | bytes 786440 | tf_op jit(solution)/shard_map/ppermute | solution.py:290
  29.2 5.3 %collective-permute-done.5.l3 = bf16[2,2,64,384]{3,2,1,0:T(8,128)(2,1)S(1)} collective-permute-done((bf16[2,2,64,384]{3,2,1,0:T(8,128)(2,1)S(1)}, bf16[2,2,64,384]{3,2,1,0:T(8,128)(2,1)S(1)}, u32[]{:S(2)}, u32[]{:S(2)}) %collective-permute-start.5) | collective-permute-done | bytes 196640 | tf_op jit(solution)/shard_map/ppermute | solution.py:294
  34.9 3.9 %shard_map.122 = (f32[2,4,256,512]{3,2,1,0:T(8,128)S(1)}, f32[2,2,256,256]{3,2,1,0:T(8,128)S(1)}) custom-call(s32[19]{0:T(128)S(1)} %pad_add_fusion.meta, bf16[2,2,256,256]{3,2,1,0:T(8,128)(2,1)S(1)} %bitcast.66, bf16[2,256,256]{2,1,0:T(8,128)(2,1)S(1)} %collective-permute-done.east, bf16[2,2,64,384]{3,2,1,0:T(8,128)(2,1)S(1)} %constant_dynamic-update-slice_fusion.l0, ...), custom_call_target="tpu_custom_call" | custom-call | flops 2147483648 | bytes 12582912 | tf_op jit(solution)/shard_map/pallas_call | solution.py:238
  38.8 8.8 %shard_map.123 = (bf16[2,4,512,256]{3,2,1,0:T(8,128)(2,1)S(1)}, bf16[2,2,3,64,128]{4,3,2,1,0:T(8,128)(2,1)S(1)}, bf16[2,2,3,64,128]{4,3,2,1,0:T(8,128)(2,1)S(1)}...) custom-call(s32[19]{0:T(128)S(1)} %pad_add_fusion.meta, bf16[2,2,256,256]{3,2,1,0:T(8,128)(2,1)S(1)} %bitcast.67, ...), custom_call_target="tpu_custom_call" | custom-call | flops 4294967296 | bytes 12582912 | tf_op jit(solution)/shard_map/pallas_call | solution.py:238
  47.7 5.0 %shard_map.124 = (bf16[2,2,3,64,128]{4,3,2,1,0:T(8,128)(2,1)S(1)}, bf16[2,2,3,64,128]{4,3,2,1,0:T(8,128)(2,1)S(1)}, bf16[2,2,3,64,128]{4,3,2,1,0:T(8,128)(2,1)S(...) custom-call(s32[19]{0:T(128)S(1)} %pad_add_fusion.meta, ...), custom_call_target="tpu_custom_call" | custom-call | flops 2147483648 | bytes 12582912 | tf_op jit(solution)/shard_map/pallas_call | solution.py:238
  52.7 1.6 %collective-permute-start.11 = (bf16[2,2,3,64,128]{4,3,2,1,0:T(8,128)(2,1)S(1)}, bf16[2,2,3,64,128]{4,3,2,1,0:T(8,128)(2,1)S(1)}, u32[]{:S(2)}, u32[]{:S(2)}) collective-permute-start(bf16[2,2,3,64,128]{4,3,2,1,0:T(8,128)(2,1)S(1)} %get-tuple-element.31), channel_id=1, source_target_pairs={{0,1},{1,2},{2,3},{3,0},{4,5},{5,6},{6,7},{7,4},{8,9},{9,10},{10,1... | collective-permute-start | bytes 589832 | tf_op jit(solution)/shard_map/ppermute | solution.py:294
  54.3 2.9 %collective-permute-start.12 = (bf16[2,2,3,64,128]{4,3,2,1,0:T(8,128)(2,1)S(1)}, bf16[2,2,3,64,128]{4,3,2,1,0:T(8,128)(2,1)S(1)}, u32[]{:S(2)}, u32[]{:S(2)}) collective-permute-start(bf16[2,2,3,64,128]{4,3,2,1,0:T(8,128)(2,1)S(1)} %get-tuple-element.32), channel_id=1, source_target_pairs={{0,2},{1,3},{2,0},{3,1},{4,6},{5,7},{6,4},{7,5},{8,10},{9,11},{10,... | collective-permute-start | bytes 589832 | tf_op jit(solution)/shard_map/ppermute | solution.py:294
  57.1 1.5 %collective-permute-start.14 = (bf16[2,2,3,64,128]{4,3,2,1,0:T(8,128)(2,1)S(1)}, bf16[2,2,3,64,128]{4,3,2,1,0:T(8,128)(2,1)S(1)}, u32[]{:S(2)}, u32[]{:S(2)}) collective-permute-start(bf16[2,2,3,64,128]{4,3,2,1,0:T(8,128)(2,1)S(1)} %get-tuple-element.35), channel_id=1, source_target_pairs={{0,1},{1,2},{2,3},{3,0},{4,5},{5,6},{6,7},{7,4},{8,9},{9,10},{10,1... | collective-permute-start | bytes 589832 | tf_op jit(solution)/shard_map/ppermute | solution.py:294
  58.7 1.5 %collective-permute-done.11 = bf16[2,2,3,64,128]{4,3,2,1,0:T(8,128)(2,1)S(1)} collective-permute-done((bf16[2,2,3,64,128]{4,3,2,1,0:T(8,128)(2,1)S(1)}, bf16[2,2,3,64,128]{4,3,2,1,0:T(8,128)(2,1)S(1)}, u32[]{:S(2)}, u32[]{:S(2)}) %collective-permute-start.11) | collective-permute-done | bytes 196640 | tf_op jit(solution)/shard_map/ppermute | solution.py:294
  60.2 1.7 %collective-permute-start.16 = (bf16[2,2,3,64,128]{4,3,2,1,0:T(8,128)(2,1)S(1)}, bf16[2,2,3,64,128]{4,3,2,1,0:T(8,128)(2,1)S(1)}, u32[]{:S(2)}, u32[]{:S(2)}) collective-permute-start(bf16[2,2,3,64,128]{4,3,2,1,0:T(8,128)(2,1)S(1)} %get-tuple-element.37), channel_id=1, source_target_pairs={{0,3},{1,0},{2,1},{3,2},{4,7},{5,4},{6,5},{7,6},{8,11},{9,8},{10,9... | collective-permute-start | bytes 589832 | tf_op jit(solution)/shard_map/ppermute | solution.py:294
  61.9 4.0 %collective-permute-done.12 = bf16[2,2,3,64,128]{4,3,2,1,0:T(8,128)(2,1)S(1)} collective-permute-done((bf16[2,2,3,64,128]{4,3,2,1,0:T(8,128)(2,1)S(1)}, bf16[2,2,3,64,128]{4,3,2,1,0:T(8,128)(2,1)S(1)}, u32[]{:S(2)}, u32[]{:S(2)}) %collective-permute-start.12) | collective-permute-done | bytes 196640 | tf_op jit(solution)/shard_map/ppermute | solution.py:294
  65.9 2.3 %collective-permute-start.19 = (bf16[4,256,256]{2,1,0:T(8,128)(2,1)S(1)}, bf16[4,256,256]{2,1,0:T(8,128)(2,1)S(1)}, u32[]{:S(2)}, u32[]{:S(2)}) collective-permute-start(bf16[4,256,256]{2,1,0:T(8,128)(2,1)S(1)} %get-tuple-element.39), channel_id=1, source_target_pairs={{0,4},{4,0},{8,12},{12,8},{16,20},{20,16},{24,28},{28,24},{32,36},... | collective-permute-start | bytes 1572872 | tf_op jit(solution)/shard_map/ppermute | solution.py:302
  69.1 5.2 %collective-permute-done.15 = bf16[2,2,3,64,128]{4,3,2,1,0:T(8,128)(2,1)S(1)} collective-permute-done((bf16[2,2,3,64,128]{4,3,2,1,0:T(8,128)(2,1)S(1)}, bf16[2,2,3,64,128]{4,3,2,1,0:T(8,128)(2,1)S(1)}, u32[]{:S(2)}, u32[]{:S(2)}) %collective-permute-start.15) | collective-permute-done | bytes 196640 | tf_op jit(solution)/shard_map/ppermute | solution.py:294
  74.4 13.3 %collective-permute-start.17 = (bf16[2,2,3,64,128]{4,3,2,1,0:T(8,128)(2,1)S(1)}, bf16[2,2,3,64,128]{4,3,2,1,0:T(8,128)(2,1)S(1)}, u32[]{:S(2)}, u32[]{:S(2)}) collective-permute-start(bf16[2,2,3,64,128]{4,3,2,1,0:T(8,128)(2,1)S(1)} %fusion.12), channel_id=1, source_target_pairs={{0,32},{4,36},{8,40},{12,44},{16,48},{20,52},{24,56},{28,60},{32,6... | collective-permute-start | bytes 589832 | tf_op jit(solution)/shard_map/ppermute | solution.py:290
  88.8 2.1 %collective-permute-start.22 = (bf16[256,256]{1,0:T(8,128)(2,1)S(1)}, bf16[256,256]{1,0:T(8,128)(2,1)S(1)}, u32[]{:S(2)}, u32[]{:S(2)}) collective-permute-start(bf16[256,256]{1,0:T(8,128)(2,1)S(1)} %get-tuple-element.43), channel_id=1, source_target_pairs={{0,3},{1,0},{2,1},{3,2},{4,7},{5,4},{6,5},{7,6},{8,11},{9,8},{10,9... | collective-permute-start | bytes 393224 | tf_op jit(solution)/shard_map/ppermute | solution.py:294
  92.1 4.9 %collective-permute-start.18 = (bf16[2,2,2,64,128]{4,3,1,0,2:T(8,128)(2,1)S(1)}, bf16[2,2,2,64,128]{4,3,1,0,2:T(8,128)(2,1)S(1)}, u32[]{:S(2)}, u32[]{:S(2)}) collective-permute-start(bf16[2,2,2,64,128]{4,3,1,0,2:T(8,128)(2,1)S(1)} %copy.27), channel_id=1, source_target_pairs={{0,4},{4,8},{8,12},{12,16},{16,20},{20,24},{24,28},{28,32},{32,36}... | collective-permute-start | bytes 393224 | tf_op jit(solution)/shard_map/ppermute | solution.py:290
  97.8 15.6 %all-to-all-start = ((bf16[32,8,256]{2,1,0:T(8,128)(2,1)}), bf16[32,8,256]{2,1,0:T(8,128)(2,1)S(1)}, u32[]{:S(2)}, u32[]{:S(2)}) async-start(bf16[32,8,256]{2,1,0:T(8,128)(2,1)} %fusion.14), calls=%async_computation | async-start | bytes 262144 | tf_op jit(solution)/shard_map/all_to_all | solution.py:328
  113.5 9.2 %all-to-all-done = bf16[32,8,256]{2,1,0:T(8,128)(2,1)S(1)} async-done(((bf16[32,8,256]{2,1,0:T(8,128)(2,1)}), bf16[32,8,256]{2,1,0:T(8,128)(2,1)S(1)}, u32[]{:S(2)}, u32[]{:S(2)}) %all-to-all-start) | async-done | bytes 131104 | tf_op jit(solution)/shard_map/all_to_all | solution.py:328
  123.4 3.9 %all-to-all-start.1 = ((bf16[32,8,256]{2,1,0:T(8,128)(2,1)}), bf16[32,8,256]{2,1,0:T(8,128)(2,1)S(1)}, u32[]{:S(2)}, u32[]{:S(2)}) async-start(bf16[32,8,256]{2,1,0:T(8,128)(2,1)} %broadcast_in_dim.38), calls=%async_computation.1 | async-start | bytes 262144 | tf_op jit(solution)/shard_map/all_to_all | solution.py:328
  128.0 9.0 %all-to-all-done.1 = bf16[32,8,256]{2,1,0:T(8,128)(2,1)S(1)} async-done(((bf16[32,8,256]{2,1,0:T(8,128)(2,1)}), bf16[32,8,256]{2,1,0:T(8,128)(2,1)S(1)}, u32[]{:S(2)}, u32[]{:S(2)}) %all-to-all-start.1) | async-done | bytes 131104 | tf_op jit(solution)/shard_map/all_to_all | solution.py:328
  (68 shorter events, 23.0 us)
Async XLA Ops:
  1.8 15.6 %collective-permute-start.8 = (bf16[256,256]{1,0:T(8,128)(2,1)S(1)}, bf16[256,256]{1,0:T(8,128)(2,1)S(1)}, u32[]{:S(2)}, u32[]{:S(2)}) collective-permute-start(bf16[256,256]{1,0:T(8,128)(2,1)S(1)} %fusion.13), channel_id=1, source_target_pairs={{0,1},{1,2},{2,3},{3,0},{4,5},{5,6},{6,7},{7,4},{8,9},{9,10},{10,1... | collective-permute-start | bytes 393224 | tf_op jit(solution)/shard_map/ppermute | solution.py:294
  3.9 16.9 %collective-permute-start.7 = (bf16[256,256]{1,0:T(8,128)(2,1)S(1)}, bf16[256,256]{1,0:T(8,128)(2,1)S(1)}, u32[]{:S(2)}, u32[]{:S(2)}) collective-permute-start(bf16[256,256]{1,0:T(8,128)(2,1)S(1)} %fusion.13), channel_id=1, source_target_pairs={{0,2},{1,3},{2,0},{3,1},{4,6},{5,7},{6,4},{7,5},{8,10},{9,11},{10,... | collective-permute-start | bytes 393224 | tf_op jit(solution)/shard_map/ppermute | solution.py:294
  6.6 14.3 %collective-permute-start.6 = (bf16[256,256]{1,0:T(8,128)(2,1)S(1)}, bf16[256,256]{1,0:T(8,128)(2,1)S(1)}, u32[]{:S(2)}, u32[]{:S(2)}) collective-permute-start(bf16[256,256]{1,0:T(8,128)(2,1)S(1)} %fusion.13), channel_id=1, source_target_pairs={{0,3},{1,0},{2,1},{3,2},{4,7},{5,4},{6,5},{7,6},{8,11},{9,8},{10,9... | collective-permute-start | bytes 393224 | tf_op jit(solution)/shard_map/ppermute | solution.py:294
  8.6 14.2 %collective-permute-start.2 = (bf16[2,2,64,256]{3,2,1,0:T(8,128)(2,1)S(1)}, bf16[2,2,64,256]{3,2,1,0:T(8,128)(2,1)S(1)}, u32[]{:S(2)}, u32[]{:S(2)}) collective-permute-start(bf16[2,2,64,256]{3,2,1,0:T(8,128)(2,1)S(1)} %dynamic-slice_bitcast_fusion.1), channel_id=1, source_target_pairs={{36,0},{40,4},{44,8},{48,12},{52,16},{56,20},{60,24},{64,28},{68,3... | collective-permute-start | bytes 393224 | tf_op jit(solution)/shard_map/ppermute | solution.py:290
  9.9 11.4 %collective-permute-start.1 = (bf16[2,2,64,128]{3,2,1,0:T(8,128)(2,1)S(1)}, bf16[2,2,64,128]{3,2,1,0:T(8,128)(2,1)S(1)}, u32[]{:S(2)}, u32[]{:S(2)}) collective-permute-start(bf16[2,2,64,128]{3,2,1,0:T(8,128)(2,1)S(1)} %slice.59), channel_id=1, source_target_pairs={{32,0},{36,4},{40,8},{44,12},{48,16},{52,20},{56,24},{60,28},{64,3... | collective-permute-start | bytes 196616 | tf_op jit(solution)/shard_map/ppermute | solution.py:290
  17.4 9.0 %collective-permute-start = (bf16[2,256,256]{2,1,0:T(8,128)(2,1)S(1)}, bf16[2,256,256]{2,1,0:T(8,128)(2,1)S(1)}, u32[]{:S(2)}, u32[]{:S(2)}) collective-permute-start(bf16[2,256,256]{2,1,0:T(8,128)(2,1)S(1)} %get-tuple-element.46), channel_id=1, source_target_pairs={{4,0},{8,4},{12,8},{16,12},{20,16},{24,20},{28,24},{32,28},{36,32}... | collective-permute-start | bytes 786440 | tf_op jit(solution)/shard_map/ppermute | solution.py:290
  20.9 14.0 %collective-permute-start.9 = (bf16[3,256,256]{2,1,0:T(8,128)(2,1)S(1)}, bf16[3,256,256]{2,1,0:T(8,128)(2,1)S(1)}, u32[]{:S(2)}, u32[]{:S(2)}) collective-permute-start(bf16[3,256,256]{2,1,0:T(8,128)(2,1)S(1)} %pad_maximum_fusion.9.near), channel_id=1, source_target_pairs={{0,4},{4,0},{8,12},{12,8},{16,20},{20,16},{24,28},{28,24},{32,36},... | collective-permute-start | bytes 1179656 | tf_op jit(solution)/shard_map/ppermute | solution.py:302
  22.7 11.8 %collective-permute-start.5 = (bf16[2,2,64,384]{3,2,1,0:T(8,128)(2,1)S(1)}, bf16[2,2,64,384]{3,2,1,0:T(8,128)(2,1)S(1)}, u32[]{:S(2)}, u32[]{:S(2)}) collective-permute-start(bf16[2,2,64,384]{3,2,1,0:T(8,128)(2,1)S(1)} %constant_dynamic-update-slice_fusion.l0), channel_id=1, source_target_pairs={{0,1},{1,2},{2,3},{3,0},{4,5},{5,6},{6,7},{7,4},{8,9},{9,10},{10,1... | collective-permute-start | bytes 589832 | tf_op jit(solution)/shard_map/ppermute | solution.py:294
  23.2 11.3 %collective-permute-start.4 = (bf16[2,2,64,384]{3,2,1,0:T(8,128)(2,1)S(1)}, bf16[2,2,64,384]{3,2,1,0:T(8,128)(2,1)S(1)}, u32[]{:S(2)}, u32[]{:S(2)}) collective-permute-start(bf16[2,2,64,384]{3,2,1,0:T(8,128)(2,1)S(1)} %constant_dynamic-update-slice_fusion.l0), channel_id=1, source_target_pairs={{0,2},{1,3},{2,0},{3,1},{4,6},{5,7},{6,4},{7,5},{8,10},{9,11},{10,... | collective-permute-start | bytes 589832 | tf_op jit(solution)/shard_map/ppermute | solution.py:294
  24.2 10.6 %collective-permute-start.3 = (bf16[2,2,64,384]{3,2,1,0:T(8,128)(2,1)S(1)}, bf16[2,2,64,384]{3,2,1,0:T(8,128)(2,1)S(1)}, u32[]{:S(2)}, u32[]{:S(2)}) collective-permute-start(bf16[2,2,64,384]{3,2,1,0:T(8,128)(2,1)S(1)} %constant_dynamic-update-slice_fusion.l0), channel_id=1, source_target_pairs={{0,3},{1,0},{2,1},{3,2},{4,7},{5,4},{6,5},{7,6},{8,11},{9,8},{10,9... | collective-permute-start | bytes 589832 | tf_op jit(solution)/shard_map/ppermute | solution.py:294
  26.4 12.5 %collective-permute-start.10 = (bf16[2,256,256]{2,1,0:T(8,128)(2,1)S(1)}, bf16[2,256,256]{2,1,0:T(8,128)(2,1)S(1)}, u32[]{:S(2)}, u32[]{:S(2)}) collective-permute-start(bf16[2,256,256]{2,1,0:T(8,128)(2,1)S(1)} %get-tuple-element.45), channel_id=1, source_target_pairs={{4,0},{8,4},{12,8},{16,12},{20,16},{24,20},{28,24},{32,28},{36,32}... | collective-permute-start | bytes 786440 | tf_op jit(solution)/shard_map/ppermute | solution.py:290
  52.7 7.5 %collective-permute-start.11 = (bf16[2,2,3,64,128]{4,3,2,1,0:T(8,128)(2,1)S(1)}, bf16[2,2,3,64,128]{4,3,2,1,0:T(8,128)(2,1)S(1)}, u32[]{:S(2)}, u32[]{:S(2)}) collective-permute-start(bf16[2,2,3,64,128]{4,3,2,1,0:T(8,128)(2,1)S(1)} %get-tuple-element.31), channel_id=1, source_target_pairs={{0,1},{1,2},{2,3},{3,0},{4,5},{5,6},{6,7},{7,4},{8,9},{9,10},{10,1... | collective-permute-start | bytes 589832 | tf_op jit(solution)/shard_map/ppermute | solution.py:294
  54.3 11.6 %collective-permute-start.12 = (bf16[2,2,3,64,128]{4,3,2,1,0:T(8,128)(2,1)S(1)}, bf16[2,2,3,64,128]{4,3,2,1,0:T(8,128)(2,1)S(1)}, u32[]{:S(2)}, u32[]{:S(2)}) collective-permute-start(bf16[2,2,3,64,128]{4,3,2,1,0:T(8,128)(2,1)S(1)} %get-tuple-element.32), channel_id=1, source_target_pairs={{0,2},{1,3},{2,0},{3,1},{4,6},{5,7},{6,4},{7,5},{8,10},{9,11},{10,... | collective-permute-start | bytes 589832 | tf_op jit(solution)/shard_map/ppermute | solution.py:294
  57.1 11.1 %collective-permute-start.13 = (bf16[2,2,3,64,128]{4,3,2,1,0:T(8,128)(2,1)S(1)}, bf16[2,2,3,64,128]{4,3,2,1,0:T(8,128)(2,1)S(1)}, u32[]{:S(2)}, u32[]{:S(2)}) collective-permute-start(bf16[2,2,3,64,128]{4,3,2,1,0:T(8,128)(2,1)S(1)} %get-tuple-element.33), channel_id=1, source_target_pairs={{0,3},{1,0},{2,1},{3,2},{4,7},{5,4},{6,5},{7,6},{8,11},{9,8},{10,9... | collective-permute-start | bytes 589832 | tf_op jit(solution)/shard_map/ppermute | solution.py:294
  57.1 11.9 %collective-permute-start.14 = (bf16[2,2,3,64,128]{4,3,2,1,0:T(8,128)(2,1)S(1)}, bf16[2,2,3,64,128]{4,3,2,1,0:T(8,128)(2,1)S(1)}, u32[]{:S(2)}, u32[]{:S(2)}) collective-permute-start(bf16[2,2,3,64,128]{4,3,2,1,0:T(8,128)(2,1)S(1)} %get-tuple-element.35), channel_id=1, source_target_pairs={{0,1},{1,2},{2,3},{3,0},{4,5},{5,6},{6,7},{7,4},{8,9},{9,10},{10,1... | collective-permute-start | bytes 589832 | tf_op jit(solution)/shard_map/ppermute | solution.py:294
  58.6 15.7 %collective-permute-start.15 = (bf16[2,2,3,64,128]{4,3,2,1,0:T(8,128)(2,1)S(1)}, bf16[2,2,3,64,128]{4,3,2,1,0:T(8,128)(2,1)S(1)}, u32[]{:S(2)}, u32[]{:S(2)}) collective-permute-start(bf16[2,2,3,64,128]{4,3,2,1,0:T(8,128)(2,1)S(1)} %get-tuple-element.36), channel_id=1, source_target_pairs={{0,2},{1,3},{2,0},{3,1},{4,6},{5,7},{6,4},{7,5},{8,10},{9,11},{10,... | collective-permute-start | bytes 589832 | tf_op jit(solution)/shard_map/ppermute | solution.py:294
  60.2 14.1 %collective-permute-start.16 = (bf16[2,2,3,64,128]{4,3,2,1,0:T(8,128)(2,1)S(1)}, bf16[2,2,3,64,128]{4,3,2,1,0:T(8,128)(2,1)S(1)}, u32[]{:S(2)}, u32[]{:S(2)}) collective-permute-start(bf16[2,2,3,64,128]{4,3,2,1,0:T(8,128)(2,1)S(1)} %get-tuple-element.37), channel_id=1, source_target_pairs={{0,3},{1,0},{2,1},{3,2},{4,7},{5,4},{6,5},{7,6},{8,11},{9,8},{10,9... | collective-permute-start | bytes 589832 | tf_op jit(solution)/shard_map/ppermute | solution.py:294
  65.9 21.9 %collective-permute-start.19 = (bf16[4,256,256]{2,1,0:T(8,128)(2,1)S(1)}, bf16[4,256,256]{2,1,0:T(8,128)(2,1)S(1)}, u32[]{:S(2)}, u32[]{:S(2)}) collective-permute-start(bf16[4,256,256]{2,1,0:T(8,128)(2,1)S(1)} %get-tuple-element.39), channel_id=1, source_target_pairs={{0,4},{4,0},{8,12},{12,8},{16,20},{20,16},{24,28},{28,24},{32,36},... | collective-permute-start | bytes 1572872 | tf_op jit(solution)/shard_map/ppermute | solution.py:302
  74.4 17.5 %collective-permute-start.17 = (bf16[2,2,3,64,128]{4,3,2,1,0:T(8,128)(2,1)S(1)}, bf16[2,2,3,64,128]{4,3,2,1,0:T(8,128)(2,1)S(1)}, u32[]{:S(2)}, u32[]{:S(2)}) collective-permute-start(bf16[2,2,3,64,128]{4,3,2,1,0:T(8,128)(2,1)S(1)} %fusion.12), channel_id=1, source_target_pairs={{0,32},{4,36},{8,40},{12,44},{16,48},{20,52},{24,56},{28,60},{32,6... | collective-permute-start | bytes 589832 | tf_op jit(solution)/shard_map/ppermute | solution.py:290
  88.0 9.0 %collective-permute-start.20 = (bf16[256,256]{1,0:T(8,128)(2,1)S(1)}, bf16[256,256]{1,0:T(8,128)(2,1)S(1)}, u32[]{:S(2)}, u32[]{:S(2)}) collective-permute-start(bf16[256,256]{1,0:T(8,128)(2,1)S(1)} %get-tuple-element.42), channel_id=1, source_target_pairs={{0,1},{1,2},{2,3},{3,0},{4,5},{5,6},{6,7},{7,4},{8,9},{9,10},{10,1... | collective-permute-start | bytes 393224 | tf_op jit(solution)/shard_map/ppermute | solution.py:294
  88.8 8.2 %collective-permute-start.22 = (bf16[256,256]{1,0:T(8,128)(2,1)S(1)}, bf16[256,256]{1,0:T(8,128)(2,1)S(1)}, u32[]{:S(2)}, u32[]{:S(2)}) collective-permute-start(bf16[256,256]{1,0:T(8,128)(2,1)S(1)} %get-tuple-element.43), channel_id=1, source_target_pairs={{0,3},{1,0},{2,1},{3,2},{4,7},{5,4},{6,5},{7,6},{8,11},{9,8},{10,9... | collective-permute-start | bytes 393224 | tf_op jit(solution)/shard_map/ppermute | solution.py:294
  92.1 21.4 %collective-permute-start.18 = (bf16[2,2,2,64,128]{4,3,1,0,2:T(8,128)(2,1)S(1)}, bf16[2,2,2,64,128]{4,3,1,0,2:T(8,128)(2,1)S(1)}, u32[]{:S(2)}, u32[]{:S(2)}) collective-permute-start(bf16[2,2,2,64,128]{4,3,1,0,2:T(8,128)(2,1)S(1)} %copy.27), channel_id=1, source_target_pairs={{0,4},{4,8},{8,12},{12,16},{16,20},{20,24},{24,28},{28,32},{32,36}... | collective-permute-start | bytes 393224 | tf_op jit(solution)/shard_map/ppermute | solution.py:290
  97.8 24.9 %all-to-all-start = ((bf16[32,8,256]{2,1,0:T(8,128)(2,1)}), bf16[32,8,256]{2,1,0:T(8,128)(2,1)S(1)}, u32[]{:S(2)}, u32[]{:S(2)}) async-start(bf16[32,8,256]{2,1,0:T(8,128)(2,1)} %fusion.14), calls=%async_computation | async-start | bytes 262144 | tf_op jit(solution)/shard_map/all_to_all | solution.py:328
  123.4 13.6 %all-to-all-start.1 = ((bf16[32,8,256]{2,1,0:T(8,128)(2,1)}), bf16[32,8,256]{2,1,0:T(8,128)(2,1)S(1)}, u32[]{:S(2)}, u32[]{:S(2)}) async-start(bf16[32,8,256]{2,1,0:T(8,128)(2,1)} %broadcast_in_dim.38), calls=%async_computation.1 | async-start | bytes 262144 | tf_op jit(solution)/shard_map/all_to_all | solution.py:328
  (4 other events, 67.4 us)

commit v4 on v2

--- a/solution.py
+++ b/solution.py
@@ -63,7 +63,7 @@
 
 def load_probes(probes, meta, own, near, far):
     core = meta[2 * SLOTS + 2]
-    probes[0] = own[...]
+    probes[0] = own[...].astype(bf16)
     for step in range(1, MODES):
         probes[step, core] = near[step - 1]
         probes[step, 1 - core] = far[step - 1]
@@ -71,7 +71,7 @@
 
 def corner_of(meta, turn):
     slot = meta[2 * SLOTS + 1] + MODES * turn
-    return meta[2 * slot], meta[2 * slot + 1] - HALF, slot < meta[2 * SLOTS]
+    return meta[slot], meta[SLOTS + slot] - HALF, slot < meta[2 * SLOTS]
 
 
 def cut(window, patch, row, col):
@@ -147,7 +147,7 @@
 
         return each_mode(one_mode)
 
-    lax.fori_loop(0, 2, one_slot, 0)
+    lax.fori_loop(0, 2, one_slot, 0, unroll=True)
 
 
 def detector_kernel(meta, own, east, l0, l1, l2, l3, arrived, measured, plus, minus, arrived_grad, g0, g1, g2, g3, window, patch, rows, lanes, far, weight, second, total):
@@ -196,7 +196,7 @@
         place(total, second, row, col)
         return 0
 
-    lax.fori_loop(0, 2, one_slot, 0)
+    lax.fori_loop(0, 2, one_slot, 0, unroll=True)
     share_rows(total, (g0, g1, g2, g3), meta[2 * SLOTS + 1])
 
 
@@ -225,7 +225,7 @@
         place(total, first, row, col)
         return 0
 
-    lax.fori_loop(0, 2, one_slot, 0)
+    lax.fori_loop(0, 2, one_slot, 0, unroll=True)
     share_rows(total, (g0, g1, g2, g3), meta[2 * SLOTS + 1])
     core = meta[2 * SLOTS + 2]
     kept[...] = probe_total[core]
@@ -342,11 +342,10 @@
     lower = jnp.concatenate([south, corner], axis=-1)
     quarters = [lower] + fetch(lower)
     pieces = (own, east, *quarters)
-    probe = probes[0].astype(bf16)
     matrices = block_forms(*lax.optimization_barrier(tuple(jnp.asarray(table) for table in constants())))
-    meta = jnp.concatenate([offsets.reshape(-1), counts, jnp.stack([mode, core])]).astype(jnp.int32)
+    meta = jnp.concatenate([offsets[0].T.reshape(-1), counts, jnp.stack([mode, core])]).astype(jnp.int32)
     turns = lax.dynamic_index_in_dim(measured[0].reshape(2, MODES, PW, PW), mode, 1, keepdims=False)
-    all_probes = (probe, near, far)
+    all_probes = (probes[0], near, far)
     second_shares, first_shares, kept, sent = kernels(meta, pieces, all_probes, turns, matrices)
     second = add_up(send_rows(second_shares))
     halves = kept + to_core(sent).astype(f32)

time: 140 us -> 138 us (0.986)
  Pallas kernels: 19.3 us -> 17.7 us
    ppermute x3, starting transfers between devices: 2.41 us -> 4.5 us  [to_core(): return lax.ppermute(value, 'tile', [(t, t ^ 1) for t in range(TILES)])]
    pallas_call x3, Pallas kernels: 19.3 us -> 17.7 us  [kernel_call(): pl.pallas_call(body, out_shape=tuple((jax.ShapeDtypeStruct(*shape) for sh...]
    ppermute x5, waiting for transfers between devices: 3.75 us -> 5.2 us  [toward(): return lax.ppermute(value, 'tile', pairs)]
where the time goes in v4:
time: 138 us
  starting transfers between devices  65.3 us (47%)
  waiting for transfers between devices  43.9 us (32%)
  Pallas kernels  17.7 us (13%)
  other arithmetic  5.59 us (4%)
  local copies, waits for them, and re-layouts  3.59 us (3%)
  between operations  1.63 us (1%)
    ppermute x5, starting transfers between devices, toward(): return lax.ppermute(value, 'tile', pairs)  23.7 us
    ppermute x15, starting transfers between devices, to_mode(): lax.ppermute(value, 'mode', [(m, (m + steps) % MODES) for m in range(MODE...  21 us
    ppermute x15, waiting for transfers between devices, to_mode(): lax.ppermute(value, 'mode', [(m, (m + steps) % MODES) for m in range(MODE...  19.5 us
    all_to_all x2, waiting for transfers between devices, exchange(): return lax.all_to_all(value, 'tile', 0, 0, axis_index_groups=groups)  18.2 us
    pallas_call x3, Pallas kernels, kernel_call(): pl.pallas_call(body, out_shape=tuple((jax.ShapeDtypeStruct(*shape) for sh...  17.7 us
    all_to_all x2, starting transfers between devices, exchange(): return lax.all_to_all(value, 'tile', 0, 0, axis_index_groups=groups)  16.1 us
    ppermute x5, waiting for transfers between devices, toward(): return lax.ppermute(value, 'tile', pairs)  5.2 us
    ppermute x3, starting transfers between devices, to_core(): return lax.ppermute(value, 'tile', [(t, t ^ 1) for t in range(TILES)])  4.5 us
  transfers between devices with their start and end apart: 25, of which 12 were waited for; matrix products, arithmetic and copies ran while one was open for 5% of the time, Pallas kernels for 0%

profile of v4, /device:TPU:1, one launch (start us, length us, event | category | flops | bytes accessed | tf_op | source)
XLA Modules:
  0.0 137.7 jit_solution(3925212169197633589)
XLA Ops:
  1.8 2.2 %collective-permute-start.8 = (bf16[256,256]{1,0:T(8,128)(2,1)S(1)}, bf16[256,256]{1,0:T(8,128)(2,1)S(1)}, u32[]{:S(2)}, u32[]{:S(2)}) collective-permute-start(bf16[256,256]{1,0:T(8,128)(2,1)S(1)} %fusion.13), channel_id=1, source_target_pairs={{0,1},{1,2},{2,3},{3,0},{4,5},{5,6},{6,7},{7,4},{8,9},{9,10},{10,1... | collective-permute-start | bytes 393224 | tf_op jit(solution)/shard_map/ppermute | solution.py:293
  4.0 2.6 %collective-permute-start.7 = (bf16[256,256]{1,0:T(8,128)(2,1)S(1)}, bf16[256,256]{1,0:T(8,128)(2,1)S(1)}, u32[]{:S(2)}, u32[]{:S(2)}) collective-permute-start(bf16[256,256]{1,0:T(8,128)(2,1)S(1)} %fusion.13), channel_id=1, source_target_pairs={{0,2},{1,3},{2,0},{3,1},{4,6},{5,7},{6,4},{7,5},{8,10},{9,11},{10,... | collective-permute-start | bytes 393224 | tf_op jit(solution)/shard_map/ppermute | solution.py:293
  13.9 3.4 %collective-permute-start = (bf16[2,2,256,256]{3,2,1,0:T(8,128)(2,1)}, bf16[2,2,256,256]{3,2,1,0:T(8,128)(2,1)S(1)}, u32[]{:S(2)}, u32[]{:S(2)}) collective-permute-start(bf16[2,2,256,256]{3,2,1,0:T(8,128)(2,1)} %bitcast.64), channel_id=1, source_target_pairs={{4,0},{8,4},{12,8},{16,12},{20,16},{24,20},{28,24},{32,28},{36,32}... | collective-permute-start | bytes 1572872 | tf_op jit(solution)/shard_map/ppermute | solution.py:289
  17.6 3.7 %collective-permute-done.1 = bf16[2,2,64,128]{3,2,1,0:T(8,128)(2,1)S(1)} collective-permute-done((bf16[2,2,64,128]{3,2,1,0:T(8,128)(2,1)S(1)}, bf16[2,2,64,128]{3,2,1,0:T(8,128)(2,1)S(1)}, u32[]{:S(2)}, u32[]{:S(2)}) %collective-permute-start.1) | collective-permute-done | bytes 65568 | tf_op jit(solution)/shard_map/ppermute | solution.py:289
  24.3 2.0 %collective-permute-start.3 = (bf16[2,2,64,384]{3,2,1,0:T(8,128)(2,1)S(1)}, bf16[2,2,64,384]{3,2,1,0:T(8,128)(2,1)S(1)}, u32[]{:S(2)}, u32[]{:S(2)}) collective-permute-start(bf16[2,2,64,384]{3,2,1,0:T(8,128)(2,1)S(1)} %constant_dynamic-update-slice_fusion.l0), channel_id=1, source_target_pairs={{0,3},{1,0},{2,1},{3,2},{4,7},{5,4},{6,5},{7,6},{8,11},{9,8},{10,9... | collective-permute-start | bytes 589832 | tf_op jit(solution)/shard_map/ppermute | solution.py:293
  27.6 7.0 %collective-permute-done.5.l3 = bf16[2,2,64,384]{3,2,1,0:T(8,128)(2,1)S(1)} collective-permute-done((bf16[2,2,64,384]{3,2,1,0:T(8,128)(2,1)S(1)}, bf16[2,2,64,384]{3,2,1,0:T(8,128)(2,1)S(1)}, u32[]{:S(2)}, u32[]{:S(2)}) %collective-permute-start.5) | collective-permute-done | bytes 196640 | tf_op jit(solution)/shard_map/ppermute | solution.py:293
  34.9 4.0 %shard_map.122 = (f32[2,4,256,512]{3,2,1,0:T(8,128)S(1)}, f32[2,2,256,256]{3,2,1,0:T(8,128)S(1)}) custom-call(s32[19]{0:T(128)S(1)} %pad_add_fusion.meta, bf16[2,2,256,256]{3,2,1,0:T(8,128)(2,1)S(1)} %bitcast.65, bf16[2,2,256,256]{3,2,1,0:T(8,128)(2,1)S(1)} %collective-permute-done.east, bf16[2,2,64,384]{3,2,1,0:T(8,128)(2,1)S(1)} %constant_dynamic-update-slice_fusion.l0, ...), custom_call_target="tpu_custom_call" | custom-call | flops 2147483648 | bytes 12582912 | tf_op jit(solution)/shard_map/pallas_call | solution.py:238
  39.0 8.4 %shard_map.123 = (bf16[2,4,512,256]{3,2,1,0:T(8,128)(2,1)S(1)}, bf16[2,2,3,64,128]{4,3,2,1,0:T(8,128)(2,1)S(1)}, bf16[2,2,3,64,128]{4,3,2,1,0:T(8,128)(2,1)S(1)}...) custom-call(s32[19]{0:T(128)S(1)} %pad_add_fusion.meta, bf16[2,2,256,256]{3,2,1,0:T(8,128)(2,1)S(1)} %bitcast.66, ...), custom_call_target="tpu_custom_call" | custom-call | flops 4294967296 | bytes 12582912 | tf_op jit(solution)/shard_map/pallas_call | solution.py:238
  47.4 5.3 %shard_map.124 = (bf16[2,2,3,64,128]{4,3,2,1,0:T(8,128)(2,1)S(1)}, bf16[2,2,3,64,128]{4,3,2,1,0:T(8,128)(2,1)S(1)}, bf16[2,2,3,64,128]{4,3,2,1,0:T(8,128)(2,1)S(...) custom-call(s32[19]{0:T(128)S(1)} %pad_add_fusion.meta, ...), custom_call_target="tpu_custom_call" | custom-call | flops 2147483648 | bytes 12582912 | tf_op jit(solution)/shard_map/pallas_call | solution.py:238
  52.7 1.6 %collective-permute-start.10 = (bf16[2,2,3,64,128]{4,3,2,1,0:T(8,128)(2,1)S(1)}, bf16[2,2,3,64,128]{4,3,2,1,0:T(8,128)(2,1)S(1)}, u32[]{:S(2)}, u32[]{:S(2)}) collective-permute-start(bf16[2,2,3,64,128]{4,3,2,1,0:T(8,128)(2,1)S(1)} %get-tuple-element.31), channel_id=1, source_target_pairs={{0,1},{1,2},{2,3},{3,0},{4,5},{5,6},{6,7},{7,4},{8,9},{9,10},{10,1... | collective-permute-start | bytes 589832 | tf_op jit(solution)/shard_map/ppermute | solution.py:293
  54.3 2.8 %collective-permute-start.11 = (bf16[2,2,3,64,128]{4,3,2,1,0:T(8,128)(2,1)S(1)}, bf16[2,2,3,64,128]{4,3,2,1,0:T(8,128)(2,1)S(1)}, u32[]{:S(2)}, u32[]{:S(2)}) collective-permute-start(bf16[2,2,3,64,128]{4,3,2,1,0:T(8,128)(2,1)S(1)} %get-tuple-element.32), channel_id=1, source_target_pairs={{0,2},{1,3},{2,0},{3,1},{4,6},{5,7},{6,4},{7,5},{8,10},{9,11},{10,... | collective-permute-start | bytes 589832 | tf_op jit(solution)/shard_map/ppermute | solution.py:293
  58.7 1.5 %collective-permute-done.10 = bf16[2,2,3,64,128]{4,3,2,1,0:T(8,128)(2,1)S(1)} collective-permute-done((bf16[2,2,3,64,128]{4,3,2,1,0:T(8,128)(2,1)S(1)}, bf16[2,2,3,64,128]{4,3,2,1,0:T(8,128)(2,1)S(1)}, u32[]{:S(2)}, u32[]{:S(2)}) %collective-permute-start.10) | collective-permute-done | bytes 196640 | tf_op jit(solution)/shard_map/ppermute | solution.py:293
  60.2 1.7 %collective-permute-start.15 = (bf16[2,2,3,64,128]{4,3,2,1,0:T(8,128)(2,1)S(1)}, bf16[2,2,3,64,128]{4,3,2,1,0:T(8,128)(2,1)S(1)}, u32[]{:S(2)}, u32[]{:S(2)}) collective-permute-start(bf16[2,2,3,64,128]{4,3,2,1,0:T(8,128)(2,1)S(1)} %get-tuple-element.37), channel_id=1, source_target_pairs={{0,3},{1,0},{2,1},{3,2},{4,7},{5,4},{6,5},{7,6},{8,11},{9,8},{10,9... | collective-permute-start | bytes 589832 | tf_op jit(solution)/shard_map/ppermute | solution.py:293
  61.9 4.0 %collective-permute-done.11 = bf16[2,2,3,64,128]{4,3,2,1,0:T(8,128)(2,1)S(1)} collective-permute-done((bf16[2,2,3,64,128]{4,3,2,1,0:T(8,128)(2,1)S(1)}, bf16[2,2,3,64,128]{4,3,2,1,0:T(8,128)(2,1)S(1)}, u32[]{:S(2)}, u32[]{:S(2)}) %collective-permute-start.11) | collective-permute-done | bytes 196640 | tf_op jit(solution)/shard_map/ppermute | solution.py:293
  65.9 2.4 %collective-permute-start.18 = (bf16[4,256,256]{2,1,0:T(8,128)(2,1)S(1)}, bf16[4,256,256]{2,1,0:T(8,128)(2,1)S(1)}, u32[]{:S(2)}, u32[]{:S(2)}) collective-permute-start(bf16[4,256,256]{2,1,0:T(8,128)(2,1)S(1)} %get-tuple-element.39), channel_id=1, source_target_pairs={{0,4},{4,0},{8,12},{12,8},{16,20},{20,16},{24,28},{28,24},{32,36},... | collective-permute-start | bytes 1572872 | tf_op jit(solution)/shard_map/ppermute | solution.py:301
  69.1 5.2 %collective-permute-done.14 = bf16[2,2,3,64,128]{4,3,2,1,0:T(8,128)(2,1)S(1)} collective-permute-done((bf16[2,2,3,64,128]{4,3,2,1,0:T(8,128)(2,1)S(1)}, bf16[2,2,3,64,128]{4,3,2,1,0:T(8,128)(2,1)S(1)}, u32[]{:S(2)}, u32[]{:S(2)}) %collective-permute-start.14) | collective-permute-done | bytes 196640 | tf_op jit(solution)/shard_map/ppermute | solution.py:293
  74.4 13.4 %collective-permute-start.16 = (bf16[2,2,3,64,128]{4,3,2,1,0:T(8,128)(2,1)S(1)}, bf16[2,2,3,64,128]{4,3,2,1,0:T(8,128)(2,1)S(1)}, u32[]{:S(2)}, u32[]{:S(2)}) collective-permute-start(bf16[2,2,3,64,128]{4,3,2,1,0:T(8,128)(2,1)S(1)} %fusion.12), channel_id=1, source_target_pairs={{0,32},{4,36},{8,40},{12,44},{16,48},{20,52},{24,56},{28,60},{32,6... | collective-permute-start | bytes 589832 | tf_op jit(solution)/shard_map/ppermute | solution.py:289
  88.8 2.1 %collective-permute-start.21 = (bf16[256,256]{1,0:T(8,128)(2,1)S(1)}, bf16[256,256]{1,0:T(8,128)(2,1)S(1)}, u32[]{:S(2)}, u32[]{:S(2)}) collective-permute-start(bf16[256,256]{1,0:T(8,128)(2,1)S(1)} %get-tuple-element.43), channel_id=1, source_target_pairs={{0,3},{1,0},{2,1},{3,2},{4,7},{5,4},{6,5},{7,6},{8,11},{9,8},{10,9... | collective-permute-start | bytes 393224 | tf_op jit(solution)/shard_map/ppermute | solution.py:293
  92.1 4.3 %collective-permute-start.17 = (bf16[2,2,2,64,128]{4,3,1,0,2:T(8,128)(2,1)S(1)}, bf16[2,2,2,64,128]{4,3,1,0,2:T(8,128)(2,1)S(1)}, u32[]{:S(2)}, u32[]{:S(2)}) collective-permute-start(bf16[2,2,2,64,128]{4,3,1,0,2:T(8,128)(2,1)S(1)} %copy.21), channel_id=1, source_target_pairs={{0,4},{4,8},{8,12},{12,16},{16,20},{20,24},{24,28},{28,32},{32,36}... | collective-permute-start | bytes 393224 | tf_op jit(solution)/shard_map/ppermute | solution.py:289
  97.9 12.2 %all-to-all-start = ((bf16[32,8,256]{2,1,0:T(8,128)(2,1)}), bf16[32,8,256]{2,1,0:T(8,128)(2,1)S(1)}, u32[]{:S(2)}, u32[]{:S(2)}) async-start(bf16[32,8,256]{2,1,0:T(8,128)(2,1)} %fusion.14), calls=%async_computation | async-start | bytes 262144 | tf_op jit(solution)/shard_map/all_to_all | solution.py:327
  110.1 9.8 %all-to-all-done = bf16[32,8,256]{2,1,0:T(8,128)(2,1)S(1)} async-done(((bf16[32,8,256]{2,1,0:T(8,128)(2,1)}), bf16[32,8,256]{2,1,0:T(8,128)(2,1)S(1)}, u32[]{:S(2)}, u32[]{:S(2)}) %all-to-all-start) | async-done | bytes 131104 | tf_op jit(solution)/shard_map/all_to_all | solution.py:327
  120.6 3.9 %all-to-all-start.1 = ((bf16[32,8,256]{2,1,0:T(8,128)(2,1)}), bf16[32,8,256]{2,1,0:T(8,128)(2,1)S(1)}, u32[]{:S(2)}, u32[]{:S(2)}) async-start(bf16[32,8,256]{2,1,0:T(8,128)(2,1)} %broadcast_in_dim.38), calls=%async_computation.1 | async-start | bytes 262144 | tf_op jit(solution)/shard_map/all_to_all | solution.py:327
  125.3 8.4 %all-to-all-done.1 = bf16[32,8,256]{2,1,0:T(8,128)(2,1)S(1)} async-done(((bf16[32,8,256]{2,1,0:T(8,128)(2,1)}), bf16[32,8,256]{2,1,0:T(8,128)(2,1)S(1)}, u32[]{:S(2)}, u32[]{:S(2)}) %all-to-all-start.1) | async-done | bytes 131104 | tf_op jit(solution)/shard_map/all_to_all | solution.py:327
  133.7 2.0 %collective-permute-start.22 = (bf16[256,256]{1,0:T(8,128)(2,1)S(1)}, bf16[256,256]{1,0:T(8,128)(2,1)S(1)}, u32[]{:S(2)}, u32[]{:S(2)}) collective-permute-start(bf16[256,256]{1,0:T(8,128)(2,1)S(1)} %bitcast.69), channel_id=1, source_target_pairs={{0,4},{4,0},{8,12},{12,8},{16,20},{20,16},{24,28},{28,24},{32,36},... | collective-permute-start | bytes 393224 | tf_op jit(solution)/shard_map/ppermute | solution.py:301
  (65 shorter events, 22.1 us)
Async XLA Ops:
  1.8 12.1 %collective-permute-start.8 = (bf16[256,256]{1,0:T(8,128)(2,1)S(1)}, bf16[256,256]{1,0:T(8,128)(2,1)S(1)}, u32[]{:S(2)}, u32[]{:S(2)}) collective-permute-start(bf16[256,256]{1,0:T(8,128)(2,1)S(1)} %fusion.13), channel_id=1, source_target_pairs={{0,1},{1,2},{2,3},{3,0},{4,5},{5,6},{6,7},{7,4},{8,9},{9,10},{10,1... | collective-permute-start | bytes 393224 | tf_op jit(solution)/shard_map/ppermute | solution.py:293
  4.0 13.4 %collective-permute-start.7 = (bf16[256,256]{1,0:T(8,128)(2,1)S(1)}, bf16[256,256]{1,0:T(8,128)(2,1)S(1)}, u32[]{:S(2)}, u32[]{:S(2)}) collective-permute-start(bf16[256,256]{1,0:T(8,128)(2,1)S(1)} %fusion.13), channel_id=1, source_target_pairs={{0,2},{1,3},{2,0},{3,1},{4,6},{5,7},{6,4},{7,5},{8,10},{9,11},{10,... | collective-permute-start | bytes 393224 | tf_op jit(solution)/shard_map/ppermute | solution.py:293
  6.6 10.8 %collective-permute-start.6 = (bf16[256,256]{1,0:T(8,128)(2,1)S(1)}, bf16[256,256]{1,0:T(8,128)(2,1)S(1)}, u32[]{:S(2)}, u32[]{:S(2)}) collective-permute-start(bf16[256,256]{1,0:T(8,128)(2,1)S(1)} %fusion.13), channel_id=1, source_target_pairs={{0,3},{1,0},{2,1},{3,2},{4,7},{5,4},{6,5},{7,6},{8,11},{9,8},{10,9... | collective-permute-start | bytes 393224 | tf_op jit(solution)/shard_map/ppermute | solution.py:293
  8.6 14.2 %collective-permute-start.2 = (bf16[2,2,64,256]{3,2,1,0:T(8,128)(2,1)S(1)}, bf16[2,2,64,256]{3,2,1,0:T(8,128)(2,1)S(1)}, u32[]{:S(2)}, u32[]{:S(2)}) collective-permute-start(bf16[2,2,64,256]{3,2,1,0:T(8,128)(2,1)S(1)} %dynamic-slice_bitcast_fusion.1), channel_id=1, source_target_pairs={{36,0},{40,4},{44,8},{48,12},{52,16},{56,20},{60,24},{64,28},{68,3... | collective-permute-start | bytes 393224 | tf_op jit(solution)/shard_map/ppermute | solution.py:289
  9.9 11.4 %collective-permute-start.1 = (bf16[2,2,64,128]{3,2,1,0:T(8,128)(2,1)S(1)}, bf16[2,2,64,128]{3,2,1,0:T(8,128)(2,1)S(1)}, u32[]{:S(2)}, u32[]{:S(2)}) collective-permute-start(bf16[2,2,64,128]{3,2,1,0:T(8,128)(2,1)S(1)} %slice.49), channel_id=1, source_target_pairs={{32,0},{36,4},{40,8},{44,12},{48,16},{52,20},{56,24},{60,28},{64,3... | collective-permute-start | bytes 196616 | tf_op jit(solution)/shard_map/ppermute | solution.py:289
  13.9 21.0 %collective-permute-start = (bf16[2,2,256,256]{3,2,1,0:T(8,128)(2,1)}, bf16[2,2,256,256]{3,2,1,0:T(8,128)(2,1)S(1)}, u32[]{:S(2)}, u32[]{:S(2)}) collective-permute-start(bf16[2,2,256,256]{3,2,1,0:T(8,128)(2,1)} %bitcast.64), channel_id=1, source_target_pairs={{4,0},{8,4},{12,8},{16,12},{20,16},{24,20},{28,24},{32,28},{36,32}... | collective-permute-start | bytes 1572872 | tf_op jit(solution)/shard_map/ppermute | solution.py:289
  17.5 17.5 %collective-permute-start.9 = (bf16[3,256,256]{2,1,0:T(8,128)(2,1)S(1)}, bf16[3,256,256]{2,1,0:T(8,128)(2,1)S(1)}, u32[]{:S(2)}, u32[]{:S(2)}) collective-permute-start(bf16[3,256,256]{2,1,0:T(8,128)(2,1)S(1)} %pad_maximum_fusion.9.near), channel_id=1, source_target_pairs={{0,4},{4,0},{8,12},{12,8},{16,20},{20,16},{24,28},{28,24},{32,36},... | collective-permute-start | bytes 1179656 | tf_op jit(solution)/shard_map/ppermute | solution.py:301
  22.8 11.8 %collective-permute-start.5 = (bf16[2,2,64,384]{3,2,1,0:T(8,128)(2,1)S(1)}, bf16[2,2,64,384]{3,2,1,0:T(8,128)(2,1)S(1)}, u32[]{:S(2)}, u32[]{:S(2)}) collective-permute-start(bf16[2,2,64,384]{3,2,1,0:T(8,128)(2,1)S(1)} %constant_dynamic-update-slice_fusion.l0), channel_id=1, source_target_pairs={{0,1},{1,2},{2,3},{3,0},{4,5},{5,6},{6,7},{7,4},{8,9},{9,10},{10,1... | collective-permute-start | bytes 589832 | tf_op jit(solution)/shard_map/ppermute | solution.py:293
  23.3 11.3 %collective-permute-start.4 = (bf16[2,2,64,384]{3,2,1,0:T(8,128)(2,1)S(1)}, bf16[2,2,64,384]{3,2,1,0:T(8,128)(2,1)S(1)}, u32[]{:S(2)}, u32[]{:S(2)}) collective-permute-start(bf16[2,2,64,384]{3,2,1,0:T(8,128)(2,1)S(1)} %constant_dynamic-update-slice_fusion.l0), channel_id=1, source_target_pairs={{0,2},{1,3},{2,0},{3,1},{4,6},{5,7},{6,4},{7,5},{8,10},{9,11},{10,... | collective-permute-start | bytes 589832 | tf_op jit(solution)/shard_map/ppermute | solution.py:293
  24.3 10.6 %collective-permute-start.3 = (bf16[2,2,64,384]{3,2,1,0:T(8,128)(2,1)S(1)}, bf16[2,2,64,384]{3,2,1,0:T(8,128)(2,1)S(1)}, u32[]{:S(2)}, u32[]{:S(2)}) collective-permute-start(bf16[2,2,64,384]{3,2,1,0:T(8,128)(2,1)S(1)} %constant_dynamic-update-slice_fusion.l0), channel_id=1, source_target_pairs={{0,3},{1,0},{2,1},{3,2},{4,7},{5,4},{6,5},{7,6},{8,11},{9,8},{10,9... | collective-permute-start | bytes 589832 | tf_op jit(solution)/shard_map/ppermute | solution.py:293
  52.7 7.5 %collective-permute-start.10 = (bf16[2,2,3,64,128]{4,3,2,1,0:T(8,128)(2,1)S(1)}, bf16[2,2,3,64,128]{4,3,2,1,0:T(8,128)(2,1)S(1)}, u32[]{:S(2)}, u32[]{:S(2)}) collective-permute-start(bf16[2,2,3,64,128]{4,3,2,1,0:T(8,128)(2,1)S(1)} %get-tuple-element.31), channel_id=1, source_target_pairs={{0,1},{1,2},{2,3},{3,0},{4,5},{5,6},{6,7},{7,4},{8,9},{9,10},{10,1... | collective-permute-start | bytes 589832 | tf_op jit(solution)/shard_map/ppermute | solution.py:293
  54.3 11.6 %collective-permute-start.11 = (bf16[2,2,3,64,128]{4,3,2,1,0:T(8,128)(2,1)S(1)}, bf16[2,2,3,64,128]{4,3,2,1,0:T(8,128)(2,1)S(1)}, u32[]{:S(2)}, u32[]{:S(2)}) collective-permute-start(bf16[2,2,3,64,128]{4,3,2,1,0:T(8,128)(2,1)S(1)} %get-tuple-element.32), channel_id=1, source_target_pairs={{0,2},{1,3},{2,0},{3,1},{4,6},{5,7},{6,4},{7,5},{8,10},{9,11},{10,... | collective-permute-start | bytes 589832 | tf_op jit(solution)/shard_map/ppermute | solution.py:293
  57.1 11.1 %collective-permute-start.12 = (bf16[2,2,3,64,128]{4,3,2,1,0:T(8,128)(2,1)S(1)}, bf16[2,2,3,64,128]{4,3,2,1,0:T(8,128)(2,1)S(1)}, u32[]{:S(2)}, u32[]{:S(2)}) collective-permute-start(bf16[2,2,3,64,128]{4,3,2,1,0:T(8,128)(2,1)S(1)} %get-tuple-element.33), channel_id=1, source_target_pairs={{0,3},{1,0},{2,1},{3,2},{4,7},{5,4},{6,5},{7,6},{8,11},{9,8},{10,9... | collective-permute-start | bytes 589832 | tf_op jit(solution)/shard_map/ppermute | solution.py:293
  57.1 12.0 %collective-permute-start.13 = (bf16[2,2,3,64,128]{4,3,2,1,0:T(8,128)(2,1)S(1)}, bf16[2,2,3,64,128]{4,3,2,1,0:T(8,128)(2,1)S(1)}, u32[]{:S(2)}, u32[]{:S(2)}) collective-permute-start(bf16[2,2,3,64,128]{4,3,2,1,0:T(8,128)(2,1)S(1)} %get-tuple-element.35), channel_id=1, source_target_pairs={{0,1},{1,2},{2,3},{3,0},{4,5},{5,6},{6,7},{7,4},{8,9},{9,10},{10,1... | collective-permute-start | bytes 589832 | tf_op jit(solution)/shard_map/ppermute | solution.py:293
  58.6 15.7 %collective-permute-start.14 = (bf16[2,2,3,64,128]{4,3,2,1,0:T(8,128)(2,1)S(1)}, bf16[2,2,3,64,128]{4,3,2,1,0:T(8,128)(2,1)S(1)}, u32[]{:S(2)}, u32[]{:S(2)}) collective-permute-start(bf16[2,2,3,64,128]{4,3,2,1,0:T(8,128)(2,1)S(1)} %get-tuple-element.36), channel_id=1, source_target_pairs={{0,2},{1,3},{2,0},{3,1},{4,6},{5,7},{6,4},{7,5},{8,10},{9,11},{10,... | collective-permute-start | bytes 589832 | tf_op jit(solution)/shard_map/ppermute | solution.py:293
  60.2 14.1 %collective-permute-start.15 = (bf16[2,2,3,64,128]{4,3,2,1,0:T(8,128)(2,1)S(1)}, bf16[2,2,3,64,128]{4,3,2,1,0:T(8,128)(2,1)S(1)}, u32[]{:S(2)}, u32[]{:S(2)}) collective-permute-start(bf16[2,2,3,64,128]{4,3,2,1,0:T(8,128)(2,1)S(1)} %get-tuple-element.37), channel_id=1, source_target_pairs={{0,3},{1,0},{2,1},{3,2},{4,7},{5,4},{6,5},{7,6},{8,11},{9,8},{10,9... | collective-permute-start | bytes 589832 | tf_op jit(solution)/shard_map/ppermute | solution.py:293
  65.9 22.0 %collective-permute-start.18 = (bf16[4,256,256]{2,1,0:T(8,128)(2,1)S(1)}, bf16[4,256,256]{2,1,0:T(8,128)(2,1)S(1)}, u32[]{:S(2)}, u32[]{:S(2)}) collective-permute-start(bf16[4,256,256]{2,1,0:T(8,128)(2,1)S(1)} %get-tuple-element.39), channel_id=1, source_target_pairs={{0,4},{4,0},{8,12},{12,8},{16,20},{20,16},{24,28},{28,24},{32,36},... | collective-permute-start | bytes 1572872 | tf_op jit(solution)/shard_map/ppermute | solution.py:301
  74.4 17.6 %collective-permute-start.16 = (bf16[2,2,3,64,128]{4,3,2,1,0:T(8,128)(2,1)S(1)}, bf16[2,2,3,64,128]{4,3,2,1,0:T(8,128)(2,1)S(1)}, u32[]{:S(2)}, u32[]{:S(2)}) collective-permute-start(bf16[2,2,3,64,128]{4,3,2,1,0:T(8,128)(2,1)S(1)} %fusion.12), channel_id=1, source_target_pairs={{0,32},{4,36},{8,40},{12,44},{16,48},{20,52},{24,56},{28,60},{32,6... | collective-permute-start | bytes 589832 | tf_op jit(solution)/shard_map/ppermute | solution.py:289
  88.0 8.3 %collective-permute-start.19 = (bf16[256,256]{1,0:T(8,128)(2,1)S(1)}, bf16[256,256]{1,0:T(8,128)(2,1)S(1)}, u32[]{:S(2)}, u32[]{:S(2)}) collective-permute-start(bf16[256,256]{1,0:T(8,128)(2,1)S(1)} %get-tuple-element.42), channel_id=1, source_target_pairs={{0,1},{1,2},{2,3},{3,0},{4,5},{5,6},{6,7},{7,4},{8,9},{9,10},{10,1... | collective-permute-start | bytes 393224 | tf_op jit(solution)/shard_map/ppermute | solution.py:293
  88.8 7.6 %collective-permute-start.21 = (bf16[256,256]{1,0:T(8,128)(2,1)S(1)}, bf16[256,256]{1,0:T(8,128)(2,1)S(1)}, u32[]{:S(2)}, u32[]{:S(2)}) collective-permute-start(bf16[256,256]{1,0:T(8,128)(2,1)S(1)} %get-tuple-element.43), channel_id=1, source_target_pairs={{0,3},{1,0},{2,1},{3,2},{4,7},{5,4},{6,5},{7,6},{8,11},{9,8},{10,9... | collective-permute-start | bytes 393224 | tf_op jit(solution)/shard_map/ppermute | solution.py:293
  90.9 6.3 %collective-permute-start.20 = (bf16[256,256]{1,0:T(8,128)(2,1)S(1)}, bf16[256,256]{1,0:T(8,128)(2,1)S(1)}, u32[]{:S(2)}, u32[]{:S(2)}) collective-permute-start(bf16[256,256]{1,0:T(8,128)(2,1)S(1)} %get-tuple-element.44), channel_id=1, source_target_pairs={{0,2},{1,3},{2,0},{3,1},{4,6},{5,7},{6,4},{7,5},{8,10},{9,11},{10,... | collective-permute-start | bytes 393224 | tf_op jit(solution)/shard_map/ppermute | solution.py:293
  92.1 18.0 %collective-permute-start.17 = (bf16[2,2,2,64,128]{4,3,1,0,2:T(8,128)(2,1)S(1)}, bf16[2,2,2,64,128]{4,3,1,0,2:T(8,128)(2,1)S(1)}, u32[]{:S(2)}, u32[]{:S(2)}) collective-permute-start(bf16[2,2,2,64,128]{4,3,1,0,2:T(8,128)(2,1)S(1)} %copy.21), channel_id=1, source_target_pairs={{0,4},{4,8},{8,12},{12,16},{16,20},{20,24},{24,28},{28,32},{32,36}... | collective-permute-start | bytes 393224 | tf_op jit(solution)/shard_map/ppermute | solution.py:289
  97.9 22.0 %all-to-all-start = ((bf16[32,8,256]{2,1,0:T(8,128)(2,1)}), bf16[32,8,256]{2,1,0:T(8,128)(2,1)S(1)}, u32[]{:S(2)}, u32[]{:S(2)}) async-start(bf16[32,8,256]{2,1,0:T(8,128)(2,1)} %fusion.14), calls=%async_computation | async-start | bytes 262144 | tf_op jit(solution)/shard_map/all_to_all | solution.py:327
  120.6 13.1 %all-to-all-start.1 = ((bf16[32,8,256]{2,1,0:T(8,128)(2,1)}), bf16[32,8,256]{2,1,0:T(8,128)(2,1)S(1)}, u32[]{:S(2)}, u32[]{:S(2)}) async-start(bf16[32,8,256]{2,1,0:T(8,128)(2,1)} %broadcast_in_dim.38), calls=%async_computation.1 | async-start | bytes 262144 | tf_op jit(solution)/shard_map/all_to_all | solution.py:327
  (4 other events, 83.6 us)
